TPU v7x, 32 devices: a whole 2x2x4 slice. The times are simulated.
32 devices in a mesh: runs: 2 (over x), fibre: 16 (over z, y, core).
Axes of the slice: x: 2, y: 2, z: 4, core: 2. Of those that a mesh axis runs over, the one named last changes fastest.
Arguments:
- records: bfloat16 [2048, 1600], P(('runs', 'fibre')), parts along dimension 0, may hold values from -6 to 6
- filter_taps: bfloat16 [9, 63], replicated, may hold values from -0.25 to 0.25
- segment_ids: int32 [2048], P('runs'), parts along dimension 0, may hold values from 0 to 7, never falling along the last dimension, each value on 1 to 256 neighbouring positions
Outputs:
- correlations: bfloat16 [2048, 5, 2048], P(('runs', 'fibre')), parts along dimension 0
- source_gathers: bfloat16 [2048, 512], P(('runs', 'fibre')), parts along dimension 0
There are 2 independent parts, one for each index of `runs`. A program takes and returns all parts, laid end to end along the dimension named above; an argument that names none is the same for every part. Nothing has to cross between parts.
Inputs may be any that keep to these rules, and one draw needn't show every extreme that they name: `segment_ids`: segment numbers never fall along the fibre; each segment has 1 to 256 channels and one has exactly 256.
All inputs are finite; a program needn't handle non-finite values.
Results may differ from a plain program's by a relative error of at most 0.0073.
Values may be sent and summed in bfloat16 or wider, within the bound.
No kernel may reach another device: no remote copies, remote signals or barrier semaphores. Data moves between devices by JAX's collectives and lax.ppermute only.
A program may use at most 128 MiB of HBM per device.

v0:
```python
import functools

import jax
import jax.numpy as jnp
import numpy as np
from jax import lax
from jax.experimental import pallas as pl
from jax.experimental.pallas import tpu as pltpu
from jax.sharding import PartitionSpec as P


CB = 64
W = 4
F = 200
L = 400
TAPS = 63
SPAN = 9
LAGS = 32
BAND = 4
HALF = (SPAN - 1) // 2
SLOT = 16
HALO = 8
CHUNK = 128
NCHUNK = -(-W * L // CHUNK)
FP = 256
KP = W * 2 * FP
ROWS = (BAND + 1) * CB
SHIFT = L % CHUNK
COVER = 4 * CHUNK

f32 = jnp.float32
bf16 = jnp.bfloat16


def dft_table():
    t = np.arange(L)
    taper = 0.5 - 0.5 * np.cos((t + 0.5) * (2.0 * np.pi / L))
    phase = (t[:, None] * np.arange(F)[None, :] % L) * (2.0 * np.pi / L)
    lead = (W - 1) * SHIFT
    table = np.zeros((lead + COVER, 2 * FP))
    table[lead : lead + L, :F] = taper[:, None] * np.cos(phase)
    table[lead : lead + L, FP : FP + F] = -taper[:, None] * np.sin(phase)
    return jnp.asarray(table.astype(np.float32), bf16)


def lag_tables():
    m = np.arange(LAGS) - LAGS // 2
    phase = (m[:, None] * np.arange(F)[None, :] % L) * (2.0 * np.pi / L)
    scale = 1.0 / np.sqrt(2.0 * L)
    tables = np.zeros((2, LAGS, FP))
    tables[0, :, :F] = np.cos(phase) * scale
    tables[1, :, :F] = -np.sin(phase) * scale
    return jnp.asarray(tables.astype(np.float32), bf16).astype(f32)


def prep_kernel(index_ref, taps_ref, ids_ref, band_ref, seg_ref, pseg_ref, pick_ref):
    device = index_ref[0]
    total = ids_ref.shape[1]
    count = total // CB
    wide = jnp.concatenate([taps_ref[...].astype(f32), jnp.zeros((SPAN, 2 * CHUNK - TAPS), f32)], axis=1)
    for e in range(SPAN):
        row = jnp.broadcast_to(wide[e : e + 1, :], (CHUNK, 2 * CHUNK))
        band_ref[e * CHUNK : (e + 1) * CHUNK, :] = pltpu.roll(row, 0, 1, stride=1, stride_axis=0).astype(bf16)

    ids = jnp.broadcast_to(ids_ref[...].astype(bf16), (CHUNK, total))

    def segments_at(channels):
        rows = channels.shape[0]
        channels = jnp.where(channels < 0, channels + total, channels)
        channels = jnp.where(channels >= total, channels - total, channels)
        hit = lax.broadcasted_iota(jnp.int32, (rows, total), 1) == channels
        return lax.dot_general(
            jnp.where(hit, 1.0, 0.0).astype(bf16), ids, (((1,), (1,)), ((), ())), preferred_element_type=f32
        )

    def rows_of(rows):
        return lax.broadcasted_iota(jnp.int32, (rows, 1), 0)

    start = device * CB
    near = segments_at(start - HALO + rows_of(ROWS + 2 * HALO))
    seg_ref[...] = near
    for k in range(BAND + 1):
        block = near[HALO + k * CB : HALO + (k + 1) * CB]
        turned = jnp.transpose(jnp.concatenate([block, block], axis=0))
        pseg_ref[k : k + 1, :] = jnp.where(device + k < count, turned[:1], -1.0)
    pseg_ref[BAND + 1 :, :] = jnp.full((8 - BAND - 1, CHUNK), -1.0, f32)

    row = rows_of(SPAN * count)
    e, r = row // count, row % count
    agree = segments_at(start + r * CB + e - HALF) == segments_at(start + r * CB)
    want_block = jnp.where(e < HALF, r - 1, r)
    want_block = jnp.where(want_block < 0, count - 1, want_block)
    side = rows_of(HALO)

    def column_of(block, edge_row):
        other = block // 2 + device % 2
        other = jnp.where(other >= count // 2, other - count // 2, other)
        place = jnp.where(block % 2 == 0, block // 2, count // 2 + other)
        return place * SLOT + edge_row

    columns = SLOT * count

    def one_hot(column, valid):
        hit = lax.broadcasted_iota(jnp.int32, (column.shape[0], columns), 1) == column
        return jnp.where(hit & valid, 1.0, 0.0).astype(bf16)

    agree = jnp.broadcast_to(agree[:, :1], (SPAN * count, columns))
    pick_ref[: SPAN * count, :] = one_hot(column_of(want_block, e), agree)
    low = column_of(jnp.full((HALO, 1), count - 1, jnp.int32), side - HALF)
    pick_ref[SPAN * count : SPAN * count + HALO, :] = one_hot(low, side >= HALF)
    high = column_of(jnp.full((HALO, 1), BAND + 1, jnp.int32), side + HALF)
    pick_ref[SPAN * count + HALO :, :] = one_hot(high, side < HALF)


def main_kernel(pieces, *refs):
    index_ref, own_ref, two_ref, four_ref, sown_ref, stwo_ref, sfour_ref = refs[:7]
    edge_refs, swapped_refs, refs = refs[7 : 7 + pieces], refs[7 + pieces : 7 + 2 * pieces], refs[7 + 2 * pieces :]
    pick_ref, seg_ref, pseg_ref, band_ref, dft_ref, lag_ref, out_ref, src_ref = refs[:8]
    rec, masked, smasked, edges, filt, spec, turned = refs[8:]
    even = index_ref[0] % 2 == 0
    count = edges.shape[0] // SLOT

    def chunk(rows, j):
        piece = rows[:, j * CHUNK : min((j + 1) * CHUNK, W * L)]
        if piece.shape[1] < CHUNK:
            piece = jnp.concatenate(
                [piece, jnp.zeros((piece.shape[0], CHUNK - piece.shape[1]), piece.dtype)], axis=1
            )
        return piece

    def put(start, rows):
        for j in range(NCHUNK):
            rec[j, start : start + rows.shape[0], :] = chunk(rows, j)

    stwo = stwo_ref[...].astype(f32)
    put(HALO, own_ref[...].astype(f32))
    put(HALO + CB, jnp.where(even, sown_ref[...].astype(f32), stwo))
    put(HALO + 2 * CB, two_ref[...].astype(f32))
    put(HALO + 3 * CB, jnp.where(even, stwo, sfour_ref[...].astype(f32)))
    put(HALO + 4 * CB, four_ref[...].astype(f32))

    empty = jnp.zeros((SLOT - SPAN, W * L), f32)
    for half, blocks, rest in ((0, (own_ref, two_ref, four_ref), edge_refs), (1, (sown_ref, stwo_ref, sfour_ref), swapped_refs)):
        slot = half * count // 2
        for ref in blocks:
            rows = [ref[CB - HALO :].astype(f32)[HALO - HALF :], ref[:HALO].astype(f32)[: HALF + 1]]
            edges[slot * SLOT : (slot + 1) * SLOT, :] = jnp.concatenate(rows + [empty], axis=0).astype(bf16)
            slot += 1
        for ref in rest:
            rows = ref[...].astype(f32)
            for first in range(0, rows.shape[0], SPAN):
                edges[slot * SLOT : (slot + 1) * SLOT, :] = jnp.concatenate(
                    [rows[first : first + SPAN], empty], axis=0
                ).astype(bf16)
                slot += 1
    picked = jnp.dot(pick_ref[...], edges[...], preferred_element_type=f32)
    put(0, picked[SPAN * count : SPAN * count + HALO])
    put(HALO + ROWS, picked[SPAN * count + HALO :])
    for e in range(SPAN):
        for j in range(NCHUNK):
            smasked[j * count : (j + 1) * count, e * CHUNK : (e + 1) * CHUNK] = chunk(
                picked[e * count : (e + 1) * count], j
            ).astype(bf16)

    def filtered(inputs, rows, start):
        share = jnp.dot(inputs[...], band_ref[...], preferred_element_type=f32)
        for j in range(NCHUNK):
            result = share[j * rows : (j + 1) * rows, :CHUNK]
            if j:
                result = result + share[(j - 1) * rows : j * rows, CHUNK:]
            filt[j, pl.ds(start, rows), :] = result.astype(bf16)

    filtered(smasked, count, ROWS)

    @pl.loop(0, BAND + 1)
    def _(k):
        base = pl.multiple_of(k * CB, CB)
        centre = seg_ref[pl.ds(base + HALO, CB), :]
        for e in range(SPAN):
            first = base + (HALO - HALF + e)
            keep = seg_ref[pl.ds(first, CB), :] == centre
            for j in range(NCHUNK):
                rows = rec[j, pl.ds(first, CB), :]
                masked[j * CB : (j + 1) * CB, e * CHUNK : (e + 1) * CHUNK] = jnp.where(keep, rows, 0.0).astype(bf16)
        filtered(masked, CB, base)

    for w in range(W):
        first = w * (L // CHUNK)
        lhs = jnp.concatenate([filt[first + q] for q in range(COVER // CHUNK)], axis=1)
        lead = (W - 1 - w) * SHIFT
        raw = jnp.dot(lhs, dft_ref[lead : lead + COVER, :], preferred_element_type=f32)
        power = jnp.sum(raw * raw, axis=-1, keepdims=True) * (1.0 / L)
        spec[:, w * 2 * FP : (w + 1) * 2 * FP] = (raw * lax.rsqrt(power + 1e-06)).astype(bf16)

    row = lax.broadcasted_iota(jnp.int32, (count, count), 0)
    column = lax.broadcasted_iota(jnp.int32, (count, count), 1)
    ahead = row - index_ref[0]
    ahead = jnp.where(ahead < 0, ahead + count, ahead)
    order = jnp.where(ahead == column, 1.0, 0.0).astype(bf16)
    spec[ROWS:, :] = jnp.dot(order, spec[ROWS:, :], preferred_element_type=f32).astype(bf16)

    group = turned.shape[0] // CB
    own_seg = seg_ref[HALO : HALO + CB, :]

    @pl.loop(0, LAGS // group)
    def _(step):
        start = pl.multiple_of(step * group, group)
        cosines = lag_ref[0, pl.ds(start, group), :]
        sines = lag_ref[1, pl.ds(start, group), :]
        for w in range(W):
            re_at, im_at = w * 2 * FP, w * 2 * FP + FP
            re = spec[:CB, re_at : re_at + FP].astype(f32)
            im = spec[:CB, im_at : im_at + FP].astype(f32)
            for g in range(group):
                c, s = cosines[g : g + 1, :], sines[g : g + 1, :]
                turned[g * CB : (g + 1) * CB, re_at : re_at + FP] = (re * c + im * s).astype(bf16)
                turned[g * CB : (g + 1) * CB, im_at : im_at + FP] = (im * c - re * s).astype(bf16)
        total = lax.dot_general(
            turned[...], spec[...], (((1,), (1,)), ((), ())), preferred_element_type=f32
        )
        for pair in range(group // 2):
            low = total[2 * pair * CB : (2 * pair + 1) * CB]
            high = total[(2 * pair + 1) * CB : (2 * pair + 2) * CB]
            lanes = pl.ds(pl.multiple_of(start * CB + pair * 2 * CB, 2 * CB), 2 * CB)
            for k in range(BAND + 1):
                both = jnp.concatenate(
                    [low[:, k * CB : (k + 1) * CB], high[:, k * CB : (k + 1) * CB]], axis=1
                )
                keep = own_seg == pseg_ref[k : k + 1, :]
                out_ref[k, :, lanes] = jnp.where(keep, both, 0.0).astype(bf16)
        sources = jnp.concatenate(
            [total[g * CB : (g + 1) * CB, ROWS : ROWS + count] for g in range(group)], axis=1
        )
        src_ref[:, pl.ds(pl.multiple_of(start * count, group * count), group * count)] = sources.astype(bf16)


VMEM = pl.BlockSpec(memory_space=pltpu.VMEM)
SMEM = pl.BlockSpec(memory_space=pltpu.SMEM)


def call(kernel, shapes, scratch, specs, **kwargs):
    return pl.pallas_call(
        kernel, out_shape=shapes, in_specs=specs, out_specs=jax.tree.map(lambda _: VMEM, shapes), scratch_shapes=scratch, **kwargs
    )


def per_device(records, filter_taps, segment_ids):
    count = lax.axis_size("fibre")
    device = lax.axis_index("fibre")

    def ahead(value, distance):
        return lax.ppermute(value, "fibre", [(i, (i - distance) % count) for i in range(count)])

    def swap(value):
        return lax.ppermute(value, "fibre", [(i, i ^ 1) for i in range(count)])

    four = ahead(records, 4)
    two = ahead(records, 2)
    sown = swap(records)

    def edges_of(rows):
        return jnp.concatenate([rows[CB - HALF :], rows[: HALF + 1]], axis=0)

    edge = edges_of(records)
    pieces = []
    for s in range(3, min(8, count // 2)):
        pieces.append(ahead(edge, 2 * s))
    have = 8
    if have < count // 2:
        known = jnp.concatenate([edge, edges_of(two), edges_of(four)] + pieces, axis=0)
    while have < count // 2:
        parts = []
        for s in range(1, 8):
            left = count // 2 - s * have
            if left > 0:
                parts.append(ahead(known[: SPAN * left], 2 * s * have))
        pieces += parts
        known = jnp.concatenate([known] + parts, axis=0)
        have = known.shape[0] // SPAN
    swapped = [swap(piece) for piece in pieces]
    sfour, stwo = swap(four), swap(two)

    index = device.reshape(1)
    band, segs, pseg, pick = call(
        prep_kernel,
        (
            jax.ShapeDtypeStruct((SPAN * CHUNK, 2 * CHUNK), bf16),
            jax.ShapeDtypeStruct((ROWS + 2 * HALO, CHUNK), f32),
            jax.ShapeDtypeStruct((8, CHUNK), f32),
            jax.ShapeDtypeStruct((SPAN * count + 2 * HALO, SLOT * count), bf16),
        ),
        (),
        [SMEM, VMEM, VMEM],
    )(index, filter_taps, segment_ids.reshape(1, -1))

    group = 8
    stacked, source_out = call(
        functools.partial(main_kernel, len(pieces)),
        (
            jax.ShapeDtypeStruct((BAND + 1, CB, LAGS * CB), bf16),
            jax.ShapeDtypeStruct((CB, LAGS * count), bf16),
        ),
        [
            pltpu.VMEM((NCHUNK, ROWS + 2 * HALO, CHUNK), f32),
            pltpu.VMEM((NCHUNK * CB, SPAN * CHUNK), bf16),
            pltpu.VMEM((NCHUNK * count, SPAN * CHUNK), bf16),
            pltpu.VMEM((SLOT * count, W * L), bf16),
            pltpu.VMEM((NCHUNK, ROWS + count, CHUNK), bf16),
            pltpu.VMEM((ROWS + count, KP), bf16),
            pltpu.VMEM((group * CB, KP), bf16),
        ],
        [SMEM] + [VMEM] * (12 + 2 * len(pieces)),
    )(
        index, records, two, four, sown, stwo, sfour, *pieces, *swapped, pick, segs, pseg, band,
        dft_table(), lag_tables(),
    )
    return (jnp.swapaxes(stacked, 0, 1), source_out)


def solution(mesh):
    return jax.shard_map(
        per_device,
        mesh=mesh,
        in_specs=(P(("runs", "fibre"), None), P(), P("runs")),
        out_specs=(P(("runs", "fibre"), None, None), P(("runs", "fibre"), None)),
        check_vma=False,
    )
```

profile of v0, /device:TPU:0, one launch (start us, length us, event | category | flops | bytes accessed | tf_op | source)
XLA Modules:
  0.0 53.9 jit_solution(3735829066994087274)
XLA Ops:
  0.6 5.1 %collective-permute-start.1 = (bf16[64,1600]{1,0:T(8,128)(2,1)}, bf16[64,1600]{1,0:T(8,128)(2,1)S(1)}, u32[]{:S(2)}, u32[]{:S(2)}) collective-permute-start(bf16[64,1600]{1,0:T(8,128)(2,1)} %refs_1_.1), channel_id=1, source_target_pairs={{0,12},{1,13},{2,14},{3,15},{4,0},{5,1},{6,2},{7,3},{8,4},{9,5},{1... | collective-permute-start | bytes 614408 | tf_op jit(solution)/shard_map/ppermute | solution.py:252
  5.8 1.4 %collective-permute-start = (bf16[64,1600]{1,0:T(8,128)(2,1)}, bf16[64,1600]{1,0:T(8,128)(2,1)S(1)}, u32[]{:S(2)}, u32[]{:S(2)}) collective-permute-start(bf16[64,1600]{1,0:T(8,128)(2,1)} %refs_1_.1), channel_id=1, source_target_pairs={{0,14},{1,15},{2,0},{3,1},{4,2},{5,3},{6,4},{7,5},{8,6},{9,7},{10,... | collective-permute-start | bytes 614408 | tf_op jit(solution)/shard_map/ppermute | solution.py:252
  7.2 0.8 %slice.6 = bf16[4,1600]{1,0:T(4,128)(2,1)S(1)} slice(bf16[64,1600]{1,0:T(8,128)(2,1)} %refs_1_.1), slice={[60:64], [0:1600]} | slice | bytes 25600 | tf_op jit(solution)/shard_map/slice | solution.py:262
  8.0 0.7 %slice.7 = bf16[5,1600]{1,0:T(8,128)(2,1)S(1)} slice(bf16[64,1600]{1,0:T(8,128)(2,1)} %refs_1_.1), slice={[0:5], [0:1600]} | slice | bytes 32000 | tf_op jit(solution)/shard_map/slice | solution.py:262
  8.7 3.0 %collective-permute-done.1.refs_3_ = bf16[64,1600]{1,0:T(8,128)(2,1)S(1)} collective-permute-done((bf16[64,1600]{1,0:T(8,128)(2,1)}, bf16[64,1600]{1,0:T(8,128)(2,1)S(1)}, u32[]{:S(2)}, u32[]{:S(2)}) %collective-permute-start.1) | collective-permute-done | bytes 204832 | tf_op jit(solution)/shard_map/ppermute | solution.py:252
  11.7 3.4 %collective-permute-done.refs_2_ = bf16[64,1600]{1,0:T(8,128)(2,1)S(1)} collective-permute-done((bf16[64,1600]{1,0:T(8,128)(2,1)}, bf16[64,1600]{1,0:T(8,128)(2,1)S(1)}, u32[]{:S(2)}, u32[]{:S(2)}) %collective-permute-start) | collective-permute-done | bytes 204832 | tf_op jit(solution)/shard_map/ppermute | solution.py:252
  15.2 0.1 collective-permute-start.9
  15.3 1.7 %collective-permute-start.8 = (bf16[9,1600]{1,0:T(8,128)(2,1)S(1)}, bf16[9,1600]{1,0:T(8,128)(2,1)S(1)}, u32[]{:S(2)}, u32[]{:S(2)}) collective-permute-start(bf16[9,1600]{1,0:T(8,128)(2,1)S(1)} %pad_maximum_fusion), channel_id=1, source_target_pairs={{0,4},{1,5},{2,6},{3,7},{4,8},{5,9},{6,10},{7,11},{8,12},{9,13},{1... | collective-permute-start | bytes 86408 | tf_op jit(solution)/shard_map/ppermute | solution.py:252
  17.0 5.9 %collective-permute-done.9.refs_11_ = bf16[9,1600]{1,0:T(8,128)(2,1)S(1)} collective-permute-done((bf16[9,1600]{1,0:T(8,128)(2,1)S(1)}, bf16[9,1600]{1,0:T(8,128)(2,1)S(1)}, u32[]{:S(2)}, u32[]{:S(2)}) %collective-permute-start.9) | collective-permute-done | bytes 28832 | tf_op jit(solution)/shard_map/ppermute | solution.py:252
  23.0 0.1 collective-permute-done.8.refs_10_
  23.1 2.0 %collective-permute-start.6 = (bf16[9,1600]{1,0:T(8,128)(2,1)S(1)}, bf16[9,1600]{1,0:T(8,128)(2,1)S(1)}, u32[]{:S(2)}, u32[]{:S(2)}) collective-permute-start(bf16[9,1600]{1,0:T(8,128)(2,1)S(1)} %pad_maximum_fusion), channel_id=1, source_target_pairs={{0,8},{1,9},{2,10},{3,11},{4,12},{5,13},{6,14},{7,15},{8,0},{9,1},... | collective-permute-start | bytes 86408 | tf_op jit(solution)/shard_map/ppermute | solution.py:252
  25.1 4.7 %collective-permute-done.7.refs_9_ = bf16[9,1600]{1,0:T(8,128)(2,1)S(1)} collective-permute-done((bf16[9,1600]{1,0:T(8,128)(2,1)S(1)}, bf16[9,1600]{1,0:T(8,128)(2,1)S(1)}, u32[]{:S(2)}, u32[]{:S(2)}) %collective-permute-start.7) | collective-permute-done | bytes 28832 | tf_op jit(solution)/shard_map/ppermute | solution.py:252
  29.9 0.1 collective-permute-start.14
  29.9 4.9 %collective-permute-done.5.refs_7_ = bf16[9,1600]{1,0:T(8,128)(2,1)S(1)} collective-permute-done((bf16[9,1600]{1,0:T(8,128)(2,1)S(1)}, bf16[9,1600]{1,0:T(8,128)(2,1)S(1)}, u32[]{:S(2)}, u32[]{:S(2)}) %collective-permute-start.5) | collective-permute-done | bytes 28832 | tf_op jit(solution)/shard_map/ppermute | solution.py:252
  34.9 0.5 collective-permute-start.12
  35.4 0.7 %collective-permute-done.13.refs_15_ = bf16[9,1600]{1,0:T(8,128)(2,1)S(1)} collective-permute-done((bf16[9,1600]{1,0:T(8,128)(2,1)S(1)}, bf16[9,1600]{1,0:T(8,128)(2,1)S(1)}, u32[]{:S(2)}, u32[]{:S(2)}) %collective-permute-start.13) | collective-permute-done | bytes 28832 | tf_op jit(solution)/shard_map/ppermute | solution.py:255
  36.1 0.2 collective-permute-start.11
  36.3 0.3 collective-permute-start.10
  36.6 2.1 %shard_map.68 = (bf16[1152,256]{1,0:T(8,128)(2,1)}, f32[336,128]{1,0:T(8,128)}, f32[8,128]{1,0:T(8,128)}, bf16[160,256]{1,0:T(8,128)(2,1)}) custom-call(s32[1]{0:T(128)} %bitcast.index_ref.refs_0_, bf16[9,63]{1,0:T(8,128)(2,1)} %taps_ref.1, s32[1,1024]{1,0:T(1,128)} %bitcast.3), custom_call_target="tpu_custom_call" | custom-call | tf_op jit(solution)/shard_map/pallas_call | solution.py:284
  38.9 0.4 copy-done.13
  39.3 0.1 copy-done.2
  39.4 0.1 copy-done.3
  39.5 0.1 copy-done.4
  39.5 14.3 %shard_map.69 = (bf16[5,64,2048]{2,1,0:T(8,128)(2,1)}, bf16[64,512]{1,0:T(8,128)(2,1)}) custom-call(s32[1]{0:T(128)} %bitcast.index_ref.refs_0_, bf16[64,1600]{1,0:T(8,128)(2,1)} %refs_1_.1, bf16[64,1600]{1,0:T(8,128)(2,1)} %copy-done.1, bf16[64,1600]{1,0:T(8,128)(2,1)} %copy-done, bf16[64,1600]{1,0:T(8,128)(2,1)} %copy-done.2, bf16[64,1600]{1,0:T(8,128)(2,1)} %copy-done.4, ...), custom_call_target="tpu_custom_call" | custom-call | tf_op jit(solution)/shard_map/pallas_call | solution.py:297
  (41 shorter events, 0.1 us)
Async XLA Ops:
  0.6 11.1 %collective-permute-start.1 = (bf16[64,1600]{1,0:T(8,128)(2,1)}, bf16[64,1600]{1,0:T(8,128)(2,1)S(1)}, u32[]{:S(2)}, u32[]{:S(2)}) collective-permute-start(bf16[64,1600]{1,0:T(8,128)(2,1)} %refs_1_.1), channel_id=1, source_target_pairs={{0,12},{1,13},{2,14},{3,15},{4,0},{5,1},{6,2},{7,3},{8,4},{9,5},{1... | collective-permute-start | bytes 614408 | tf_op jit(solution)/shard_map/ppermute | solution.py:252
  5.8 9.4 %collective-permute-start = (bf16[64,1600]{1,0:T(8,128)(2,1)}, bf16[64,1600]{1,0:T(8,128)(2,1)S(1)}, u32[]{:S(2)}, u32[]{:S(2)}) collective-permute-start(bf16[64,1600]{1,0:T(8,128)(2,1)} %refs_1_.1), channel_id=1, source_target_pairs={{0,14},{1,15},{2,0},{3,1},{4,2},{5,3},{6,4},{7,5},{8,6},{9,7},{10,... | collective-permute-start | bytes 614408 | tf_op jit(solution)/shard_map/ppermute | solution.py:252
  7.2 31.5 %collective-permute-start.2 = (bf16[64,1600]{1,0:T(8,128)(2,1)}, bf16[64,1600]{1,0:T(8,128)(2,1)S(1)}, u32[]{:S(2)}, u32[]{:S(2)}) collective-permute-start(bf16[64,1600]{1,0:T(8,128)(2,1)} %refs_1_.1), channel_id=1, source_target_pairs={{0,1},{1,0},{2,3},{3,2},{4,5},{5,4},{6,7},{7,6},{8,9},{9,8},{10,11... | collective-permute-start | bytes 614408 | tf_op jit(solution)/shard_map/ppermute | solution.py:255
  11.7 27.1 %copy-start = (bf16[64,1600]{1,0:T(8,128)(2,1)}, bf16[64,1600]{1,0:T(8,128)(2,1)S(1)}, u32[]{:S(2)}) copy-start(bf16[64,1600]{1,0:T(8,128)(2,1)S(1)} %collective-permute-done.1.refs_3_) | copy-start | bytes 614404
  11.7 27.0 %collective-permute-start.4 = (bf16[64,1600]{1,0:T(8,128)(2,1)S(1)}, bf16[64,1600]{1,0:T(8,128)(2,1)S(1)}, u32[]{:S(2)}, u32[]{:S(2)}) collective-permute-start(bf16[64,1600]{1,0:T(8,128)(2,1)S(1)} %collective-permute-done.1.refs_3_), channel_id=1, source_target_pairs={{0,1},{1,0},{2,3},{3,2},{4,5},{5,4},{6,7},{7,6},{8,9},{9,8},{10,11... | collective-permute-start | bytes 614408 | tf_op jit(solution)/shard_map/ppermute | solution.py:255
  15.2 23.6 %copy-start.1 = (bf16[64,1600]{1,0:T(8,128)(2,1)}, bf16[64,1600]{1,0:T(8,128)(2,1)S(1)}, u32[]{:S(2)}) copy-start(bf16[64,1600]{1,0:T(8,128)(2,1)S(1)} %collective-permute-done.refs_2_) | copy-start | bytes 614404
  15.2 23.6 %collective-permute-start.3 = (bf16[64,1600]{1,0:T(8,128)(2,1)S(1)}, bf16[64,1600]{1,0:T(8,128)(2,1)S(1)}, u32[]{:S(2)}, u32[]{:S(2)}) collective-permute-start(bf16[64,1600]{1,0:T(8,128)(2,1)S(1)} %collective-permute-done.refs_2_), channel_id=1, source_target_pairs={{0,1},{1,0},{2,3},{3,2},{4,5},{5,4},{6,7},{7,6},{8,9},{9,8},{10,11... | collective-permute-start | bytes 614408 | tf_op jit(solution)/shard_map/ppermute | solution.py:255
  15.2 7.8 %collective-permute-start.9 = (bf16[9,1600]{1,0:T(8,128)(2,1)S(1)}, bf16[9,1600]{1,0:T(8,128)(2,1)S(1)}, u32[]{:S(2)}, u32[]{:S(2)}) collective-permute-start(bf16[9,1600]{1,0:T(8,128)(2,1)S(1)} %pad_maximum_fusion), channel_id=1, source_target_pairs={{0,2},{1,3},{2,4},{3,5},{4,6},{5,7},{6,8},{7,9},{8,10},{9,11},{10,... | collective-permute-start | bytes 86408 | tf_op jit(solution)/shard_map/ppermute | solution.py:252
  15.3 7.8 %collective-permute-start.8 = (bf16[9,1600]{1,0:T(8,128)(2,1)S(1)}, bf16[9,1600]{1,0:T(8,128)(2,1)S(1)}, u32[]{:S(2)}, u32[]{:S(2)}) collective-permute-start(bf16[9,1600]{1,0:T(8,128)(2,1)S(1)} %pad_maximum_fusion), channel_id=1, source_target_pairs={{0,4},{1,5},{2,6},{3,7},{4,8},{5,9},{6,10},{7,11},{8,12},{9,13},{1... | collective-permute-start | bytes 86408 | tf_op jit(solution)/shard_map/ppermute | solution.py:252
  23.0 15.8 %copy-start.5 = (bf16[9,1600]{1,0:T(8,128)(2,1)}, bf16[9,1600]{1,0:T(8,128)(2,1)S(1)}, u32[]{:S(2)}) copy-start(bf16[9,1600]{1,0:T(8,128)(2,1)S(1)} %collective-permute-done.9.refs_11_) | copy-start | bytes 86404
  23.0 6.8 %collective-permute-start.7 = (bf16[9,1600]{1,0:T(8,128)(2,1)S(1)}, bf16[9,1600]{1,0:T(8,128)(2,1)S(1)}, u32[]{:S(2)}, u32[]{:S(2)}) collective-permute-start(bf16[9,1600]{1,0:T(8,128)(2,1)S(1)} %pad_maximum_fusion), channel_id=1, source_target_pairs={{0,6},{1,7},{2,8},{3,9},{4,10},{5,11},{6,12},{7,13},{8,14},{9,15},... | collective-permute-start | bytes 86408 | tf_op jit(solution)/shard_map/ppermute | solution.py:252
  23.1 15.7 %copy-start.6 = (bf16[9,1600]{1,0:T(8,128)(2,1)}, bf16[9,1600]{1,0:T(8,128)(2,1)S(1)}, u32[]{:S(2)}) copy-start(bf16[9,1600]{1,0:T(8,128)(2,1)S(1)} %collective-permute-done.8.refs_10_) | copy-start | bytes 86404
  23.1 6.8 %collective-permute-start.6 = (bf16[9,1600]{1,0:T(8,128)(2,1)S(1)}, bf16[9,1600]{1,0:T(8,128)(2,1)S(1)}, u32[]{:S(2)}, u32[]{:S(2)}) collective-permute-start(bf16[9,1600]{1,0:T(8,128)(2,1)S(1)} %pad_maximum_fusion), channel_id=1, source_target_pairs={{0,8},{1,9},{2,10},{3,11},{4,12},{5,13},{6,14},{7,15},{8,0},{9,1},... | collective-permute-start | bytes 86408 | tf_op jit(solution)/shard_map/ppermute | solution.py:252
  29.8 9.0 %copy-start.7 = (bf16[9,1600]{1,0:T(8,128)(2,1)}, bf16[9,1600]{1,0:T(8,128)(2,1)S(1)}, u32[]{:S(2)}) copy-start(bf16[9,1600]{1,0:T(8,128)(2,1)S(1)} %collective-permute-done.7.refs_9_) | copy-start | bytes 86404
  29.8 5.0 %collective-permute-start.5 = (bf16[9,1600]{1,0:T(8,128)(2,1)S(1)}, bf16[9,1600]{1,0:T(8,128)(2,1)S(1)}, u32[]{:S(2)}, u32[]{:S(2)}) collective-permute-start(bf16[9,1600]{1,0:T(8,128)(2,1)S(1)} %pad_maximum_fusion), channel_id=1, source_target_pairs={{0,10},{1,11},{2,12},{3,13},{4,14},{5,15},{6,0},{7,1},{8,2},{9,3},... | collective-permute-start | bytes 86408 | tf_op jit(solution)/shard_map/ppermute | solution.py:252
  29.9 9.0 %copy-start.8 = (bf16[9,1600]{1,0:T(8,128)(2,1)}, bf16[9,1600]{1,0:T(8,128)(2,1)S(1)}, u32[]{:S(2)}) copy-start(bf16[9,1600]{1,0:T(8,128)(2,1)S(1)} %collective-permute-done.6.refs_8_) | copy-start | bytes 86404
  29.9 5.0 %collective-permute-start.14 = (bf16[9,1600]{1,0:T(8,128)(2,1)S(1)}, bf16[9,1600]{1,0:T(8,128)(2,1)S(1)}, u32[]{:S(2)}, u32[]{:S(2)}) collective-permute-start(bf16[9,1600]{1,0:T(8,128)(2,1)S(1)} %collective-permute-done.9.refs_11_), channel_id=1, source_target_pairs={{0,1},{1,0},{2,3},{3,2},{4,5},{5,4},{6,7},{7,6},{8,9},{9,8},{10,11... | collective-permute-start | bytes 86408 | tf_op jit(solution)/shard_map/ppermute | solution.py:255
  34.9 4.0 %copy-start.9 = (bf16[9,1600]{1,0:T(8,128)(2,1)}, bf16[9,1600]{1,0:T(8,128)(2,1)S(1)}, u32[]{:S(2)}) copy-start(bf16[9,1600]{1,0:T(8,128)(2,1)S(1)} %collective-permute-done.5.refs_7_) | copy-start | bytes 86404
  34.9 1.2 %collective-permute-start.13 = (bf16[9,1600]{1,0:T(8,128)(2,1)S(1)}, bf16[9,1600]{1,0:T(8,128)(2,1)S(1)}, u32[]{:S(2)}, u32[]{:S(2)}) collective-permute-start(bf16[9,1600]{1,0:T(8,128)(2,1)S(1)} %collective-permute-done.8.refs_10_), channel_id=1, source_target_pairs={{0,1},{1,0},{2,3},{3,2},{4,5},{5,4},{6,7},{7,6},{8,9},{9,8},{10,11... | collective-permute-start | bytes 86408 | tf_op jit(solution)/shard_map/ppermute | solution.py:255
  34.9 4.0 %copy-start.10 = (bf16[9,1600]{1,0:T(8,128)(2,1)}, bf16[9,1600]{1,0:T(8,128)(2,1)S(1)}, u32[]{:S(2)}) copy-start(bf16[9,1600]{1,0:T(8,128)(2,1)S(1)} %collective-permute-done.14.refs_16_) | copy-start | bytes 86404
  34.9 1.4 %collective-permute-start.12 = (bf16[9,1600]{1,0:T(8,128)(2,1)S(1)}, bf16[9,1600]{1,0:T(8,128)(2,1)S(1)}, u32[]{:S(2)}, u32[]{:S(2)}) collective-permute-start(bf16[9,1600]{1,0:T(8,128)(2,1)S(1)} %collective-permute-done.7.refs_9_), channel_id=1, source_target_pairs={{0,1},{1,0},{2,3},{3,2},{4,5},{5,4},{6,7},{7,6},{8,9},{9,8},{10,11... | collective-permute-start | bytes 86408 | tf_op jit(solution)/shard_map/ppermute | solution.py:255
  36.1 2.7 %copy-start.11 = (bf16[9,1600]{1,0:T(8,128)(2,1)}, bf16[9,1600]{1,0:T(8,128)(2,1)S(1)}, u32[]{:S(2)}) copy-start(bf16[9,1600]{1,0:T(8,128)(2,1)S(1)} %collective-permute-done.13.refs_15_) | copy-start | bytes 86404
  36.1 2.6 %collective-permute-start.11 = (bf16[9,1600]{1,0:T(8,128)(2,1)S(1)}, bf16[9,1600]{1,0:T(8,128)(2,1)S(1)}, u32[]{:S(2)}, u32[]{:S(2)}) collective-permute-start(bf16[9,1600]{1,0:T(8,128)(2,1)S(1)} %collective-permute-done.6.refs_8_), channel_id=1, source_target_pairs={{0,1},{1,0},{2,3},{3,2},{4,5},{5,4},{6,7},{7,6},{8,9},{9,8},{10,11... | collective-permute-start | bytes 86408 | tf_op jit(solution)/shard_map/ppermute | solution.py:255
  36.3 2.4 %collective-permute-start.10 = (bf16[9,1600]{1,0:T(8,128)(2,1)S(1)}, bf16[9,1600]{1,0:T(8,128)(2,1)S(1)}, u32[]{:S(2)}, u32[]{:S(2)}) collective-permute-start(bf16[9,1600]{1,0:T(8,128)(2,1)S(1)} %collective-permute-done.5.refs_7_), channel_id=1, source_target_pairs={{0,1},{1,0},{2,3},{3,2},{4,5},{5,4},{6,7},{7,6},{8,9},{9,8},{10,11... | collective-permute-start | bytes 86408 | tf_op jit(solution)/shard_map/ppermute | solution.py:255
  (6 other events, 6.0 us)
where the time goes:
time: 54.2 us; the launch traced here: 53.9 us
  waiting for transfers between devices  22.9 us (42%)
  Pallas kernels  16.4 us (30%)
  starting transfers between devices  11.5 us (21%)
  local copies, waits for them, and re-layouts  2.25 us (4%)
  between operations  0.82 us (2%)
    ppermute x7, waiting for transfers between devices, ahead(): lax.ppermute(value, 'fibre', [(i, (i - distance) % count) for i in range(...  22.1 us
    pallas_call x1, Pallas kernels, per_device(): call(functools.partial(main_kernel, len(pieces)), (jax.ShapeDtypeStruct((...  14.3 us
    ppermute x7, starting transfers between devices, ahead(): lax.ppermute(value, 'fibre', [(i, (i - distance) % count) for i in range(...  10.4 us
    pallas_call x1, Pallas kernels, per_device(): call(prep_kernel, (jax.ShapeDtypeStruct((SPAN * CHUNK, 2 * CHUNK), bf16),...  2.05 us
    slice x2, local copies, waits for them, and re-layouts, edges_of(): return jnp.concatenate([rows[CB - HALF:], rows[:HALF + 1]], axis=0)  1.53 us
    ppermute x8, starting transfers between devices, swap(): return lax.ppermute(value, 'fibre', [(i, i ^ 1) for i in range(count)])  1.09 us
  transfers between devices with their start and end apart: 15, of which 7 were waited for; matrix products, arithmetic and copies ran while one was open for 3% of the time, Pallas kernels for 4%

commit v1 on v0

--- a/solution.py
+++ b/solution.py
@@ -28,6 +28,10 @@
 SHIFT = L % CHUNK
 COVER = 4 * CHUNK
 
+VMEM_LIMIT = 28 << 20
+PREP_LIMIT = 12 << 20
+TABLE_LIMIT = 4 << 20
+
 f32 = jnp.float32
 bf16 = jnp.bfloat16
 
@@ -53,9 +57,16 @@
     return jnp.asarray(tables.astype(np.float32), bf16).astype(f32)
 
 
-def prep_kernel(index_ref, taps_ref, ids_ref, band_ref, seg_ref, pseg_ref, pick_ref):
+def edge_rows(ref):
+    return jnp.concatenate(
+        [ref[CB - HALO :].astype(f32)[HALO - HALF :], ref[:HALO].astype(f32)[: HALF + 1]], axis=0
+    )
+
+
+def prep_kernel(index_ref, taps_ref, ids_ref, own_ref, edge_ref, band_ref, seg_ref, pseg_ref, pick_ref):
     device = index_ref[0]
     total = ids_ref.shape[1]
+    edge_ref[...] = edge_rows(own_ref).astype(bf16)
     count = total // CB
     wide = jnp.concatenate([taps_ref[...].astype(f32), jnp.zeros((SPAN, 2 * CHUNK - TAPS), f32)], axis=1)
     for e in range(SPAN):
@@ -112,11 +123,17 @@
     pick_ref[SPAN * count + HALO :, :] = one_hot(high, side < HALF)
 
 
+def copy_kernel(*refs):
+    half = len(refs) // 2
+    for source, target in zip(refs[:half], refs[half:]):
+        target[...] = source[...]
+
+
 def main_kernel(pieces, *refs):
     index_ref, own_ref, two_ref, four_ref, sown_ref, stwo_ref, sfour_ref = refs[:7]
     edge_refs, swapped_refs, refs = refs[7 : 7 + pieces], refs[7 + pieces : 7 + 2 * pieces], refs[7 + 2 * pieces :]
     pick_ref, seg_ref, pseg_ref, band_ref, dft_ref, lag_ref, out_ref, src_ref = refs[:8]
-    rec, masked, smasked, edges, filt, spec, turned = refs[8:]
+    rec, masked, smasked, edges, filt, spec, turned, totals = refs[8:]
     even = index_ref[0] % 2 == 0
     count = edges.shape[0] // SLOT
 
@@ -133,18 +150,18 @@
             rec[j, start : start + rows.shape[0], :] = chunk(rows, j)
 
     stwo = stwo_ref[...].astype(f32)
-    put(HALO, own_ref[...].astype(f32))
     put(HALO + CB, jnp.where(even, sown_ref[...].astype(f32), stwo))
     put(HALO + 2 * CB, two_ref[...].astype(f32))
     put(HALO + 3 * CB, jnp.where(even, stwo, sfour_ref[...].astype(f32)))
     put(HALO + 4 * CB, four_ref[...].astype(f32))
+    put(HALO, own_ref[...].astype(f32))
 
     empty = jnp.zeros((SLOT - SPAN, W * L), f32)
     for half, blocks, rest in ((0, (own_ref, two_ref, four_ref), edge_refs), (1, (sown_ref, stwo_ref, sfour_ref), swapped_refs)):
         slot = half * count // 2
         for ref in blocks:
-            rows = [ref[CB - HALO :].astype(f32)[HALO - HALF :], ref[:HALO].astype(f32)[: HALF + 1]]
-            edges[slot * SLOT : (slot + 1) * SLOT, :] = jnp.concatenate(rows + [empty], axis=0).astype(bf16)
+            rows = edge_rows(ref)
+            edges[slot * SLOT : (slot + 1) * SLOT, :] = jnp.concatenate([rows, empty], axis=0).astype(bf16)
             slot += 1
         for ref in rest:
             rows = ref[...].astype(f32)
@@ -172,17 +189,17 @@
 
     filtered(smasked, count, ROWS)
 
-    @pl.loop(0, BAND + 1)
-    def _(k):
-        base = pl.multiple_of(k * CB, CB)
+    for k in range(BAND + 1):
+        base = k * CB
+        held = masked.at[k % 2]
         centre = seg_ref[pl.ds(base + HALO, CB), :]
         for e in range(SPAN):
             first = base + (HALO - HALF + e)
             keep = seg_ref[pl.ds(first, CB), :] == centre
             for j in range(NCHUNK):
                 rows = rec[j, pl.ds(first, CB), :]
-                masked[j * CB : (j + 1) * CB, e * CHUNK : (e + 1) * CHUNK] = jnp.where(keep, rows, 0.0).astype(bf16)
-        filtered(masked, CB, base)
+                held[j * CB : (j + 1) * CB, e * CHUNK : (e + 1) * CHUNK] = jnp.where(keep, rows, 0.0).astype(bf16)
+        filtered(held, CB, base)
 
     for w in range(W):
         first = w * (L // CHUNK)
@@ -200,10 +217,10 @@
     spec[ROWS:, :] = jnp.dot(order, spec[ROWS:, :], preferred_element_type=f32).astype(bf16)
 
     group = turned.shape[0] // CB
+    steps = LAGS // group
     own_seg = seg_ref[HALO : HALO + CB, :]
 
-    @pl.loop(0, LAGS // group)
-    def _(step):
+    def multiply(step, slot):
         start = pl.multiple_of(step * group, group)
         cosines = lag_ref[0, pl.ds(start, group), :]
         sines = lag_ref[1, pl.ds(start, group), :]
@@ -215,23 +232,34 @@
                 c, s = cosines[g : g + 1, :], sines[g : g + 1, :]
                 turned[g * CB : (g + 1) * CB, re_at : re_at + FP] = (re * c + im * s).astype(bf16)
                 turned[g * CB : (g + 1) * CB, im_at : im_at + FP] = (im * c - re * s).astype(bf16)
-        total = lax.dot_general(
+        totals[slot] = lax.dot_general(
             turned[...], spec[...], (((1,), (1,)), ((), ())), preferred_element_type=f32
         )
+
+    def write(step, slot):
+        start = pl.multiple_of(step * group, group)
         for pair in range(group // 2):
-            low = total[2 * pair * CB : (2 * pair + 1) * CB]
-            high = total[(2 * pair + 1) * CB : (2 * pair + 2) * CB]
+            low, high = 2 * pair * CB, (2 * pair + 1) * CB
             lanes = pl.ds(pl.multiple_of(start * CB + pair * 2 * CB, 2 * CB), 2 * CB)
             for k in range(BAND + 1):
                 both = jnp.concatenate(
-                    [low[:, k * CB : (k + 1) * CB], high[:, k * CB : (k + 1) * CB]], axis=1
+                    [totals[slot, at : at + CB, k * CB : (k + 1) * CB] for at in (low, high)], axis=1
                 )
                 keep = own_seg == pseg_ref[k : k + 1, :]
                 out_ref[k, :, lanes] = jnp.where(keep, both, 0.0).astype(bf16)
         sources = jnp.concatenate(
-            [total[g * CB : (g + 1) * CB, ROWS : ROWS + count] for g in range(group)], axis=1
+            [totals[slot, g * CB : (g + 1) * CB, ROWS : ROWS + count] for g in range(group)], axis=1
         )
         src_ref[:, pl.ds(pl.multiple_of(start * count, group * count), group * count)] = sources.astype(bf16)
+
+    multiply(0, 0)
+
+    @pl.loop(1, steps)
+    def _(step):
+        write(step - 1, (step - 1) % 2)
+        multiply(step, step % 2)
+
+    write(steps - 1, (steps - 1) % 2)
 
 
 VMEM = pl.BlockSpec(memory_space=pltpu.VMEM)
@@ -258,10 +286,25 @@
     two = ahead(records, 2)
     sown = swap(records)
 
+    index = device.reshape(1)
+    few = count <= 16
+    edge, band, segs, pseg, pick = call(
+        prep_kernel,
+        (
+            jax.ShapeDtypeStruct((SPAN, W * L), bf16),
+            jax.ShapeDtypeStruct((SPAN * CHUNK, 2 * CHUNK), bf16),
+            jax.ShapeDtypeStruct((ROWS + 2 * HALO, CHUNK), f32),
+            jax.ShapeDtypeStruct((8, CHUNK), f32),
+            jax.ShapeDtypeStruct((SPAN * count + 2 * HALO, SLOT * count), bf16),
+        ),
+        (),
+        [SMEM, VMEM, VMEM, VMEM],
+        compiler_params=pltpu.CompilerParams(vmem_limit_bytes=PREP_LIMIT if few else None),
+    )(index, filter_taps, segment_ids.reshape(1, -1), records)
+
     def edges_of(rows):
         return jnp.concatenate([rows[CB - HALF :], rows[: HALF + 1]], axis=0)
 
-    edge = edges_of(records)
     pieces = []
     for s in range(3, min(8, count // 2)):
         pieces.append(ahead(edge, 2 * s))
@@ -280,20 +323,15 @@
     swapped = [swap(piece) for piece in pieces]
     sfour, stwo = swap(four), swap(two)
 
-    index = device.reshape(1)
-    band, segs, pseg, pick = call(
-        prep_kernel,
-        (
-            jax.ShapeDtypeStruct((SPAN * CHUNK, 2 * CHUNK), bf16),
-            jax.ShapeDtypeStruct((ROWS + 2 * HALO, CHUNK), f32),
-            jax.ShapeDtypeStruct((8, CHUNK), f32),
-            jax.ShapeDtypeStruct((SPAN * count + 2 * HALO, SLOT * count), bf16),
-        ),
+    group = 8
+    tables = (records, dft_table(), lag_tables())
+    own, dft, lags = call(
+        copy_kernel,
+        tuple(jax.ShapeDtypeStruct(table.shape, table.dtype) for table in tables),
         (),
-        [SMEM, VMEM, VMEM],
-    )(index, filter_taps, segment_ids.reshape(1, -1))
-
-    group = 8
+        [VMEM] * 3,
+        compiler_params=pltpu.CompilerParams(vmem_limit_bytes=TABLE_LIMIT),
+    )(*tables)
     stacked, source_out = call(
         functools.partial(main_kernel, len(pieces)),
         (
@@ -302,17 +340,19 @@
         ),
         [
             pltpu.VMEM((NCHUNK, ROWS + 2 * HALO, CHUNK), f32),
-            pltpu.VMEM((NCHUNK * CB, SPAN * CHUNK), bf16),
+            pltpu.VMEM((2, NCHUNK * CB, SPAN * CHUNK), bf16),
             pltpu.VMEM((NCHUNK * count, SPAN * CHUNK), bf16),
             pltpu.VMEM((SLOT * count, W * L), bf16),
             pltpu.VMEM((NCHUNK, ROWS + count, CHUNK), bf16),
             pltpu.VMEM((ROWS + count, KP), bf16),
             pltpu.VMEM((group * CB, KP), bf16),
+            pltpu.VMEM((2, group * CB, ROWS + count), f32),
         ],
         [SMEM] + [VMEM] * (12 + 2 * len(pieces)),
+        compiler_params=pltpu.CompilerParams(vmem_limit_bytes=VMEM_LIMIT if few else None),
     )(
-        index, records, two, four, sown, stwo, sfour, *pieces, *swapped, pick, segs, pseg, band,
-        dft_table(), lag_tables(),
+        index, own, two, four, sown, stwo, sfour, *pieces, *swapped, pick, segs, pseg, band,
+        dft, lags,
     )
     return (jnp.swapaxes(stacked, 0, 1), source_out)
 

time: 54.2 us -> 54.6 us (level)
  Pallas kernels: 16.4 us -> 13.5 us
  local copies, waits for them, and re-layouts: 2.25 us -> 4.2 us
  waiting for transfers between devices: 22.9 us -> 24.5 us
    unnamed x30 -> x10, local copies, waits for them, and re-layouts: 0.72 us -> 4.2 us
    pallas_call x1, Pallas kernels: 14.3 us -> 12.7 us  [per_device(): call(functools.partial(main_kernel, len(pieces)), (jax.ShapeDtypeStruct((...]
    ppermute x7, waiting for transfers between devices: 22.1 us -> 23.8 us  [ahead(): lax.ppermute(value, 'fibre', [(i, (i - distance) % count) for i in range(...]
    slice x2 -> x0, local copies, waits for them, and re-layouts: 1.53 us -> none  [edges_of(): return jnp.concatenate([rows[CB - HALF:], rows[:HALF + 1]], axis=0)]
    pallas_call x1 -> x2, Pallas kernels: 2.05 us -> 0.77 us  [the longest x1 0.71 us: per_device(): call(prep_kernel, (jax.ShapeDtypeStruct((SPAN, W * L), bf16), jax.ShapeDt...]
  transfers between devices with their start and end apart: 15 -> 15, of which waited for: 7 -> 7; matrix products, arithmetic and copies ran while one was open for 3% -> 0% of each run, Pallas kernels for 4% -> 1%
where the time goes in v1:
time: 54.6 us; the launch traced here: 54.3 us
  waiting for transfers between devices  24.5 us (45%)
  Pallas kernels  13.5 us (25%)
  starting transfers between devices  11.4 us (21%)
  local copies, waits for them, and re-layouts  4.2 us (8%)
  between operations  0.7 us (1%)
    ppermute x7, waiting for transfers between devices, ahead(): lax.ppermute(value, 'fibre', [(i, (i - distance) % count) for i in range(...  23.8 us
    pallas_call x1, Pallas kernels, per_device(): call(functools.partial(main_kernel, len(pieces)), (jax.ShapeDtypeStruct((...  12.7 us
    ppermute x7, starting transfers between devices, ahead(): lax.ppermute(value, 'fibre', [(i, (i - distance) % count) for i in range(...  10.4 us
    unnamed x10, local copies, waits for them, and re-layouts  4.2 us
  transfers between devices with their start and end apart: 15, of which 7 were waited for; matrix products, arithmetic and copies ran while one was open for 0% of the time, Pallas kernels for 1%

profile of v1, /device:TPU:0, one launch (start us, length us, event | category | flops | bytes accessed | tf_op | source)
XLA Modules:
  0.0 54.3 jit_solution(4892673803851673166)
XLA Ops:
  0.6 5.1 %collective-permute-start.1 = (bf16[64,1600]{1,0:T(8,128)(2,1)}, bf16[64,1600]{1,0:T(8,128)(2,1)S(1)}, u32[]{:S(2)}, u32[]{:S(2)}) collective-permute-start(bf16[64,1600]{1,0:T(8,128)(2,1)} %own_ref.1), channel_id=1, source_target_pairs={{0,12},{1,13},{2,14},{3,15},{4,0},{5,1},{6,2},{7,3},{8,4},{9,5},{1... | collective-permute-start | bytes 614408 | tf_op jit(solution)/shard_map/ppermute | solution.py:280
  5.8 1.4 %collective-permute-start = (bf16[64,1600]{1,0:T(8,128)(2,1)}, bf16[64,1600]{1,0:T(8,128)(2,1)S(1)}, u32[]{:S(2)}, u32[]{:S(2)}) collective-permute-start(bf16[64,1600]{1,0:T(8,128)(2,1)} %own_ref.1), channel_id=1, source_target_pairs={{0,14},{1,15},{2,0},{3,1},{4,2},{5,3},{6,4},{7,5},{8,6},{9,7},{10,... | collective-permute-start | bytes 614408 | tf_op jit(solution)/shard_map/ppermute | solution.py:280
  7.2 4.5 %collective-permute-done.1.refs_3_ = bf16[64,1600]{1,0:T(8,128)(2,1)S(1)} collective-permute-done((bf16[64,1600]{1,0:T(8,128)(2,1)}, bf16[64,1600]{1,0:T(8,128)(2,1)S(1)}, u32[]{:S(2)}, u32[]{:S(2)}) %collective-permute-start.1) | collective-permute-done | bytes 204832 | tf_op jit(solution)/shard_map/ppermute | solution.py:280
  11.7 3.4 %collective-permute-done.refs_2_ = bf16[64,1600]{1,0:T(8,128)(2,1)S(1)} collective-permute-done((bf16[64,1600]{1,0:T(8,128)(2,1)}, bf16[64,1600]{1,0:T(8,128)(2,1)S(1)}, u32[]{:S(2)}, u32[]{:S(2)}) %collective-permute-start) | collective-permute-done | bytes 204832 | tf_op jit(solution)/shard_map/ppermute | solution.py:280
  15.2 0.9 %copy-done = bf16[64,1600]{1,0:T(8,128)(2,1)S(1)} copy-done((bf16[64,1600]{1,0:T(8,128)(2,1)S(1)}, bf16[64,1600]{1,0:T(8,128)(2,1)}, u32[]{:S(2)}) %copy-start) | copy-done | bytes 204824
  16.1 0.7 %copy-done.3 = bf16[9,63]{1,0:T(8,128)(2,1)S(1)} copy-done((bf16[9,63]{1,0:T(8,128)(2,1)S(1)}, bf16[9,63]{1,0:T(8,128)(2,1)}, u32[]{:S(2)}) %copy-start.3) | copy-done | bytes 1158
  16.8 0.7 %copy-done.4 = s32[1024]{0:T(1024)S(1)} copy-done((s32[1024]{0:T(1024)S(1)}, s32[1024]{0:T(1024)}, u32[]{:S(2)}) %copy-start.4) | copy-done | bytes 4120
  17.5 0.7 %shard_map.69 = (bf16[9,1600]{1,0:T(8,128)(2,1)S(1)}, bf16[1152,256]{1,0:T(8,128)(2,1)S(1)}, f32[336,128]{1,0:T(8,128)S(1)}, f32[8,128]{1,0:T(8,128)S(1)}, bf16[160,256]{1,0:T(8,128)(2,1)S(1)}) custom-call(s32[1]{0:T(128)} %bitcast.index_ref.refs_0_, bf16[9,63]{1,0:T(8,128)(2,1)S(1)} %copy-done.3, s32[1,1024]{1,0:T(1,128)S(1)} %bitcast.3, ...), custom_call_target="tpu_custom_call" | custom-call | tf_op jit(solution)/shard_map/pallas_call | solution.py:291
  18.2 0.1 collective-permute-start.9
  18.3 1.7 %collective-permute-start.8 = (bf16[9,1600]{1,0:T(8,128)(2,1)S(1)}, bf16[9,1600]{1,0:T(8,128)(2,1)S(1)}, u32[]{:S(2)}, u32[]{:S(2)}) collective-permute-start(bf16[9,1600]{1,0:T(8,128)(2,1)S(1)} %get-tuple-element.13), channel_id=1, source_target_pairs={{0,4},{1,5},{2,6},{3,7},{4,8},{5,9},{6,10},{7,11},{8,12},{9,13},{1... | collective-permute-start | bytes 86408 | tf_op jit(solution)/shard_map/ppermute | solution.py:280
  20.0 5.9 %collective-permute-done.9.refs_11_ = bf16[9,1600]{1,0:T(8,128)(2,1)S(1)} collective-permute-done((bf16[9,1600]{1,0:T(8,128)(2,1)S(1)}, bf16[9,1600]{1,0:T(8,128)(2,1)S(1)}, u32[]{:S(2)}, u32[]{:S(2)}) %collective-permute-start.9) | collective-permute-done | bytes 28832 | tf_op jit(solution)/shard_map/ppermute | solution.py:280
  25.9 0.1 collective-permute-done.8.refs_10_
  26.0 2.0 %collective-permute-start.6 = (bf16[9,1600]{1,0:T(8,128)(2,1)S(1)}, bf16[9,1600]{1,0:T(8,128)(2,1)S(1)}, u32[]{:S(2)}, u32[]{:S(2)}) collective-permute-start(bf16[9,1600]{1,0:T(8,128)(2,1)S(1)} %get-tuple-element.13), channel_id=1, source_target_pairs={{0,8},{1,9},{2,10},{3,11},{4,12},{5,13},{6,14},{7,15},{8,0},{9,1},... | collective-permute-start | bytes 86408 | tf_op jit(solution)/shard_map/ppermute | solution.py:280
  28.1 4.7 %collective-permute-done.7.refs_9_ = bf16[9,1600]{1,0:T(8,128)(2,1)S(1)} collective-permute-done((bf16[9,1600]{1,0:T(8,128)(2,1)S(1)}, bf16[9,1600]{1,0:T(8,128)(2,1)S(1)}, u32[]{:S(2)}, u32[]{:S(2)}) %collective-permute-start.7) | collective-permute-done | bytes 28832 | tf_op jit(solution)/shard_map/ppermute | solution.py:280
  32.8 5.0 %collective-permute-done.5.refs_7_ = bf16[9,1600]{1,0:T(8,128)(2,1)S(1)} collective-permute-done((bf16[9,1600]{1,0:T(8,128)(2,1)S(1)}, bf16[9,1600]{1,0:T(8,128)(2,1)S(1)}, u32[]{:S(2)}, u32[]{:S(2)}) %collective-permute-start.5) | collective-permute-done | bytes 28832 | tf_op jit(solution)/shard_map/ppermute | solution.py:280
  37.8 0.5 collective-permute-start.12
  38.3 0.7 %collective-permute-done.13.refs_15_ = bf16[9,1600]{1,0:T(8,128)(2,1)S(1)} collective-permute-done((bf16[9,1600]{1,0:T(8,128)(2,1)S(1)}, bf16[9,1600]{1,0:T(8,128)(2,1)S(1)}, u32[]{:S(2)}, u32[]{:S(2)}) %collective-permute-start.13) | collective-permute-done | bytes 28832 | tf_op jit(solution)/shard_map/ppermute | solution.py:283
  39.1 0.2 collective-permute-start.11
  39.2 0.0 collective-permute-done.12.refs_14_
  39.2 0.3 collective-permute-start.10
  39.6 1.1 %copy-done.1 = bf16[560,512]{1,0:T(8,128)(2,1)S(1)} copy-done((bf16[560,512]{1,0:T(8,128)(2,1)S(1)}, bf16[560,512]{1,0:T(8,128)(2,1)}, u32[]{:S(2)}) %copy-start.1) | copy-done | bytes 573464
  40.6 0.8 %copy-done.2 = f32[2,32,256]{2,1,0:T(8,128)S(1)} copy-done((f32[2,32,256]{2,1,0:T(8,128)S(1)}, f32[2,32,256]{2,1,0:T(8,128)}, u32[]{:S(2)}) %copy-start.2) | copy-done | bytes 65560
  41.5 0.1 shard_map.68
  41.6 12.7 %shard_map.70 = (bf16[5,64,2048]{2,1,0:T(8,128)(2,1)}, bf16[64,512]{1,0:T(8,128)(2,1)}) custom-call(s32[1]{0:T(128)} %bitcast.index_ref.refs_0_, bf16[64,1600]{1,0:T(8,128)(2,1)S(1)} %get-tuple-element.12.refs_1_, bf16[64,1600]{1,0:T(8,128)(2,1)S(1)} %collective-permute-done.refs_2_, bf16[64,1600]{1,0:T(8,128)(2,1)S(1)} %collective-permute-done.1.refs_3_, ...), custom_call_target="tpu_custom_call" | custom-call | tf_op jit(solution)/shard_map/pallas_call | solution.py:335
  (19 shorter events, 0.0 us)
Async XLA Ops:
  0.6 11.1 %collective-permute-start.1 = (bf16[64,1600]{1,0:T(8,128)(2,1)}, bf16[64,1600]{1,0:T(8,128)(2,1)S(1)}, u32[]{:S(2)}, u32[]{:S(2)}) collective-permute-start(bf16[64,1600]{1,0:T(8,128)(2,1)} %own_ref.1), channel_id=1, source_target_pairs={{0,12},{1,13},{2,14},{3,15},{4,0},{5,1},{6,2},{7,3},{8,4},{9,5},{1... | collective-permute-start | bytes 614408 | tf_op jit(solution)/shard_map/ppermute | solution.py:280
  5.8 9.4 %collective-permute-start = (bf16[64,1600]{1,0:T(8,128)(2,1)}, bf16[64,1600]{1,0:T(8,128)(2,1)S(1)}, u32[]{:S(2)}, u32[]{:S(2)}) collective-permute-start(bf16[64,1600]{1,0:T(8,128)(2,1)} %own_ref.1), channel_id=1, source_target_pairs={{0,14},{1,15},{2,0},{3,1},{4,2},{5,3},{6,4},{7,5},{8,6},{9,7},{10,... | collective-permute-start | bytes 614408 | tf_op jit(solution)/shard_map/ppermute | solution.py:280
  7.2 34.4 %collective-permute-start.2 = (bf16[64,1600]{1,0:T(8,128)(2,1)}, bf16[64,1600]{1,0:T(8,128)(2,1)S(1)}, u32[]{:S(2)}, u32[]{:S(2)}) collective-permute-start(bf16[64,1600]{1,0:T(8,128)(2,1)} %own_ref.1), channel_id=1, source_target_pairs={{0,1},{1,0},{2,3},{3,2},{4,5},{5,4},{6,7},{7,6},{8,9},{9,8},{10,11... | collective-permute-start | bytes 614408 | tf_op jit(solution)/shard_map/ppermute | solution.py:283
  11.7 29.9 %collective-permute-start.4 = (bf16[64,1600]{1,0:T(8,128)(2,1)S(1)}, bf16[64,1600]{1,0:T(8,128)(2,1)S(1)}, u32[]{:S(2)}, u32[]{:S(2)}) collective-permute-start(bf16[64,1600]{1,0:T(8,128)(2,1)S(1)} %collective-permute-done.1.refs_3_), channel_id=1, source_target_pairs={{0,1},{1,0},{2,3},{3,2},{4,5},{5,4},{6,7},{7,6},{8,9},{9,8},{10,11... | collective-permute-start | bytes 614408 | tf_op jit(solution)/shard_map/ppermute | solution.py:283
  15.2 26.4 %collective-permute-start.3 = (bf16[64,1600]{1,0:T(8,128)(2,1)S(1)}, bf16[64,1600]{1,0:T(8,128)(2,1)S(1)}, u32[]{:S(2)}, u32[]{:S(2)}) collective-permute-start(bf16[64,1600]{1,0:T(8,128)(2,1)S(1)} %collective-permute-done.refs_2_), channel_id=1, source_target_pairs={{0,1},{1,0},{2,3},{3,2},{4,5},{5,4},{6,7},{7,6},{8,9},{9,8},{10,11... | collective-permute-start | bytes 614408 | tf_op jit(solution)/shard_map/ppermute | solution.py:283
  15.2 0.9 %copy-start = (bf16[64,1600]{1,0:T(8,128)(2,1)S(1)}, bf16[64,1600]{1,0:T(8,128)(2,1)}, u32[]{:S(2)}) copy-start(bf16[64,1600]{1,0:T(8,128)(2,1)} %own_ref.1) | copy-start | bytes 614404
  16.1 0.7 %copy-start.3 = (bf16[9,63]{1,0:T(8,128)(2,1)S(1)}, bf16[9,63]{1,0:T(8,128)(2,1)}, u32[]{:S(2)}) copy-start(bf16[9,63]{1,0:T(8,128)(2,1)} %taps_ref.1) | copy-start | bytes 3406
  16.8 0.7 %copy-start.4 = (s32[1024]{0:T(1024)S(1)}, s32[1024]{0:T(1024)}, u32[]{:S(2)}) copy-start(s32[1024]{0:T(1024)} %param.7) | copy-start | bytes 12292
  18.2 7.8 %collective-permute-start.9 = (bf16[9,1600]{1,0:T(8,128)(2,1)S(1)}, bf16[9,1600]{1,0:T(8,128)(2,1)S(1)}, u32[]{:S(2)}, u32[]{:S(2)}) collective-permute-start(bf16[9,1600]{1,0:T(8,128)(2,1)S(1)} %get-tuple-element.13), channel_id=1, source_target_pairs={{0,2},{1,3},{2,4},{3,5},{4,6},{5,7},{6,8},{7,9},{8,10},{9,11},{10,... | collective-permute-start | bytes 86408 | tf_op jit(solution)/shard_map/ppermute | solution.py:280
  18.3 7.8 %collective-permute-start.8 = (bf16[9,1600]{1,0:T(8,128)(2,1)S(1)}, bf16[9,1600]{1,0:T(8,128)(2,1)S(1)}, u32[]{:S(2)}, u32[]{:S(2)}) collective-permute-start(bf16[9,1600]{1,0:T(8,128)(2,1)S(1)} %get-tuple-element.13), channel_id=1, source_target_pairs={{0,4},{1,5},{2,6},{3,7},{4,8},{5,9},{6,10},{7,11},{8,12},{9,13},{1... | collective-permute-start | bytes 86408 | tf_op jit(solution)/shard_map/ppermute | solution.py:280
  25.9 6.8 %collective-permute-start.7 = (bf16[9,1600]{1,0:T(8,128)(2,1)S(1)}, bf16[9,1600]{1,0:T(8,128)(2,1)S(1)}, u32[]{:S(2)}, u32[]{:S(2)}) collective-permute-start(bf16[9,1600]{1,0:T(8,128)(2,1)S(1)} %get-tuple-element.13), channel_id=1, source_target_pairs={{0,6},{1,7},{2,8},{3,9},{4,10},{5,11},{6,12},{7,13},{8,14},{9,15},... | collective-permute-start | bytes 86408 | tf_op jit(solution)/shard_map/ppermute | solution.py:280
  26.0 6.8 %collective-permute-start.6 = (bf16[9,1600]{1,0:T(8,128)(2,1)S(1)}, bf16[9,1600]{1,0:T(8,128)(2,1)S(1)}, u32[]{:S(2)}, u32[]{:S(2)}) collective-permute-start(bf16[9,1600]{1,0:T(8,128)(2,1)S(1)} %get-tuple-element.13), channel_id=1, source_target_pairs={{0,8},{1,9},{2,10},{3,11},{4,12},{5,13},{6,14},{7,15},{8,0},{9,1},... | collective-permute-start | bytes 86408 | tf_op jit(solution)/shard_map/ppermute | solution.py:280
  32.8 5.0 %collective-permute-start.5 = (bf16[9,1600]{1,0:T(8,128)(2,1)S(1)}, bf16[9,1600]{1,0:T(8,128)(2,1)S(1)}, u32[]{:S(2)}, u32[]{:S(2)}) collective-permute-start(bf16[9,1600]{1,0:T(8,128)(2,1)S(1)} %get-tuple-element.13), channel_id=1, source_target_pairs={{0,10},{1,11},{2,12},{3,13},{4,14},{5,15},{6,0},{7,1},{8,2},{9,3},... | collective-permute-start | bytes 86408 | tf_op jit(solution)/shard_map/ppermute | solution.py:280
  32.8 5.0 %collective-permute-start.14 = (bf16[9,1600]{1,0:T(8,128)(2,1)S(1)}, bf16[9,1600]{1,0:T(8,128)(2,1)S(1)}, u32[]{:S(2)}, u32[]{:S(2)}) collective-permute-start(bf16[9,1600]{1,0:T(8,128)(2,1)S(1)} %collective-permute-done.9.refs_11_), channel_id=1, source_target_pairs={{0,1},{1,0},{2,3},{3,2},{4,5},{5,4},{6,7},{7,6},{8,9},{9,8},{10,11... | collective-permute-start | bytes 86408 | tf_op jit(solution)/shard_map/ppermute | solution.py:283
  37.8 1.2 %collective-permute-start.13 = (bf16[9,1600]{1,0:T(8,128)(2,1)S(1)}, bf16[9,1600]{1,0:T(8,128)(2,1)S(1)}, u32[]{:S(2)}, u32[]{:S(2)}) collective-permute-start(bf16[9,1600]{1,0:T(8,128)(2,1)S(1)} %collective-permute-done.8.refs_10_), channel_id=1, source_target_pairs={{0,1},{1,0},{2,3},{3,2},{4,5},{5,4},{6,7},{7,6},{8,9},{9,8},{10,11... | collective-permute-start | bytes 86408 | tf_op jit(solution)/shard_map/ppermute | solution.py:283
  37.8 1.4 %collective-permute-start.12 = (bf16[9,1600]{1,0:T(8,128)(2,1)S(1)}, bf16[9,1600]{1,0:T(8,128)(2,1)S(1)}, u32[]{:S(2)}, u32[]{:S(2)}) collective-permute-start(bf16[9,1600]{1,0:T(8,128)(2,1)S(1)} %collective-permute-done.7.refs_9_), channel_id=1, source_target_pairs={{0,1},{1,0},{2,3},{3,2},{4,5},{5,4},{6,7},{7,6},{8,9},{9,8},{10,11... | collective-permute-start | bytes 86408 | tf_op jit(solution)/shard_map/ppermute | solution.py:283
  39.1 2.5 %collective-permute-start.11 = (bf16[9,1600]{1,0:T(8,128)(2,1)S(1)}, bf16[9,1600]{1,0:T(8,128)(2,1)S(1)}, u32[]{:S(2)}, u32[]{:S(2)}) collective-permute-start(bf16[9,1600]{1,0:T(8,128)(2,1)S(1)} %collective-permute-done.6.refs_8_), channel_id=1, source_target_pairs={{0,1},{1,0},{2,3},{3,2},{4,5},{5,4},{6,7},{7,6},{8,9},{9,8},{10,11... | collective-permute-start | bytes 86408 | tf_op jit(solution)/shard_map/ppermute | solution.py:283
  39.2 2.3 %collective-permute-start.10 = (bf16[9,1600]{1,0:T(8,128)(2,1)S(1)}, bf16[9,1600]{1,0:T(8,128)(2,1)S(1)}, u32[]{:S(2)}, u32[]{:S(2)}) collective-permute-start(bf16[9,1600]{1,0:T(8,128)(2,1)S(1)} %collective-permute-done.5.refs_7_), channel_id=1, source_target_pairs={{0,1},{1,0},{2,3},{3,2},{4,5},{5,4},{6,7},{7,6},{8,9},{9,8},{10,11... | collective-permute-start | bytes 86408 | tf_op jit(solution)/shard_map/ppermute | solution.py:283
  39.6 1.1 %copy-start.1 = (bf16[560,512]{1,0:T(8,128)(2,1)S(1)}, bf16[560,512]{1,0:T(8,128)(2,1)}, u32[]{:S(2)}) copy-start(bf16[560,512]{1,0:T(8,128)(2,1)} %constant.8.clone.refs_1_) | copy-start | bytes 1720324
  40.6 0.8 %copy-start.2 = (f32[2,32,256]{2,1,0:T(8,128)S(1)}, f32[2,32,256]{2,1,0:T(8,128)}, u32[]{:S(2)}) copy-start(f32[2,32,256]{2,1,0:T(8,128)} %constant.10.refs_2_) | copy-start | bytes 196612

commit v2 on v1

--- a/solution.py
+++ b/solution.py
@@ -30,7 +30,6 @@
 
 VMEM_LIMIT = 28 << 20
 PREP_LIMIT = 12 << 20
-TABLE_LIMIT = 4 << 20
 
 f32 = jnp.float32
 bf16 = jnp.bfloat16
@@ -57,15 +56,27 @@
     return jnp.asarray(tables.astype(np.float32), bf16).astype(f32)
 
 
+def start_loads(pairs, sems):
+    loads = [pltpu.make_async_copy(source, target, sems.at[i]) for i, (source, target) in enumerate(pairs)]
+    for load in loads:
+        load.start()
+    return loads
+
+
 def edge_rows(ref):
     return jnp.concatenate(
         [ref[CB - HALO :].astype(f32)[HALO - HALF :], ref[:HALO].astype(f32)[: HALF + 1]], axis=0
     )
 
 
-def prep_kernel(index_ref, taps_ref, ids_ref, own_ref, edge_ref, band_ref, seg_ref, pseg_ref, pick_ref):
+def prep_kernel(
+    index_ref, taps_hbm, ids_hbm, own_hbm, edge_ref, band_ref, seg_ref, pseg_ref, pick_ref, taps_ref, ids_ref, own_ref, sems
+):
     device = index_ref[0]
     total = ids_ref.shape[1]
+    loads = start_loads(((own_hbm, own_ref), (taps_hbm, taps_ref), (ids_hbm, ids_ref)), sems)
+    for load in loads:
+        load.wait()
     edge_ref[...] = edge_rows(own_ref).astype(bf16)
     count = total // CB
     wide = jnp.concatenate([taps_ref[...].astype(f32), jnp.zeros((SPAN, 2 * CHUNK - TAPS), f32)], axis=1)
@@ -123,17 +134,12 @@
     pick_ref[SPAN * count + HALO :, :] = one_hot(high, side < HALF)
 
 
-def copy_kernel(*refs):
-    half = len(refs) // 2
-    for source, target in zip(refs[:half], refs[half:]):
-        target[...] = source[...]
-
-
 def main_kernel(pieces, *refs):
-    index_ref, own_ref, two_ref, four_ref, sown_ref, stwo_ref, sfour_ref = refs[:7]
+    index_ref, own_hbm, two_ref, four_ref, sown_ref, stwo_ref, sfour_ref = refs[:7]
     edge_refs, swapped_refs, refs = refs[7 : 7 + pieces], refs[7 + pieces : 7 + 2 * pieces], refs[7 + 2 * pieces :]
-    pick_ref, seg_ref, pseg_ref, band_ref, dft_ref, lag_ref, out_ref, src_ref = refs[:8]
-    rec, masked, smasked, edges, filt, spec, turned, totals = refs[8:]
+    pick_ref, seg_ref, pseg_ref, band_ref, dft_hbm, lag_hbm, out_ref, src_ref = refs[:8]
+    rec, masked, smasked, edges, filt, spec, turned, totals, own_ref, dft_ref, lag_ref, sems = refs[8:]
+    loads = start_loads(((own_hbm, own_ref), (dft_hbm, dft_ref), (lag_hbm, lag_ref)), sems)
     even = index_ref[0] % 2 == 0
     count = edges.shape[0] // SLOT
 
@@ -154,6 +160,7 @@
     put(HALO + 2 * CB, two_ref[...].astype(f32))
     put(HALO + 3 * CB, jnp.where(even, stwo, sfour_ref[...].astype(f32)))
     put(HALO + 4 * CB, four_ref[...].astype(f32))
+    loads[0].wait()
     put(HALO, own_ref[...].astype(f32))
 
     empty = jnp.zeros((SLOT - SPAN, W * L), f32)
@@ -201,6 +208,8 @@
                 held[j * CB : (j + 1) * CB, e * CHUNK : (e + 1) * CHUNK] = jnp.where(keep, rows, 0.0).astype(bf16)
         filtered(held, CB, base)
 
+    loads[1].wait()
+    loads[2].wait()
     for w in range(W):
         first = w * (L // CHUNK)
         lhs = jnp.concatenate([filt[first + q] for q in range(COVER // CHUNK)], axis=1)
@@ -264,6 +273,7 @@
 
 VMEM = pl.BlockSpec(memory_space=pltpu.VMEM)
 SMEM = pl.BlockSpec(memory_space=pltpu.SMEM)
+HBM = pl.BlockSpec(memory_space=pltpu.HBM)
 
 
 def call(kernel, shapes, scratch, specs, **kwargs):
@@ -287,6 +297,7 @@
     sown = swap(records)
 
     index = device.reshape(1)
+    stay = functools.partial(pltpu.with_memory_space_constraint, memory_space=pltpu.HBM)
     few = count <= 16
     edge, band, segs, pseg, pick = call(
         prep_kernel,
@@ -297,10 +308,15 @@
             jax.ShapeDtypeStruct((8, CHUNK), f32),
             jax.ShapeDtypeStruct((SPAN * count + 2 * HALO, SLOT * count), bf16),
         ),
-        (),
-        [SMEM, VMEM, VMEM, VMEM],
+        [
+            pltpu.VMEM(filter_taps.shape, bf16),
+            pltpu.VMEM((1,) + segment_ids.shape, jnp.int32),
+            pltpu.VMEM(records.shape, bf16),
+            pltpu.SemaphoreType.DMA((3,)),
+        ],
+        [SMEM, HBM, HBM, HBM],
         compiler_params=pltpu.CompilerParams(vmem_limit_bytes=PREP_LIMIT if few else None),
-    )(index, filter_taps, segment_ids.reshape(1, -1), records)
+    )(index, stay(filter_taps), stay(segment_ids.reshape(1, -1)), stay(records))
 
     def edges_of(rows):
         return jnp.concatenate([rows[CB - HALF :], rows[: HALF + 1]], axis=0)
@@ -324,14 +340,7 @@
     sfour, stwo = swap(four), swap(two)
 
     group = 8
-    tables = (records, dft_table(), lag_tables())
-    own, dft, lags = call(
-        copy_kernel,
-        tuple(jax.ShapeDtypeStruct(table.shape, table.dtype) for table in tables),
-        (),
-        [VMEM] * 3,
-        compiler_params=pltpu.CompilerParams(vmem_limit_bytes=TABLE_LIMIT),
-    )(*tables)
+    dft, lags = dft_table(), lag_tables()
     stacked, source_out = call(
         functools.partial(main_kernel, len(pieces)),
         (
@@ -347,12 +356,16 @@
             pltpu.VMEM((ROWS + count, KP), bf16),
             pltpu.VMEM((group * CB, KP), bf16),
             pltpu.VMEM((2, group * CB, ROWS + count), f32),
+            pltpu.VMEM((CB, W * L), bf16),
+            pltpu.VMEM(dft.shape, bf16),
+            pltpu.VMEM(lags.shape, f32),
+            pltpu.SemaphoreType.DMA((3,)),
         ],
-        [SMEM] + [VMEM] * (12 + 2 * len(pieces)),
+        [SMEM, HBM] + [VMEM] * (9 + 2 * len(pieces)) + [HBM] * 2,
         compiler_params=pltpu.CompilerParams(vmem_limit_bytes=VMEM_LIMIT if few else None),
     )(
-        index, own, two, four, sown, stwo, sfour, *pieces, *swapped, pick, segs, pseg, band,
-        dft, lags,
+        index, stay(records), two, four, sown, stwo, sfour, *pieces, *swapped, pick, segs, pseg, band,
+        stay(dft), stay(lags),
     )
     return (jnp.swapaxes(stacked, 0, 1), source_out)
 

time: 54.6 us -> 53.3 us (0.976)
  local copies, waits for them, and re-layouts: 4.2 us -> 0 us
  Pallas kernels: 13.5 us -> 15.6 us
  waiting for transfers between devices: 24.5 us -> 25.4 us
    unnamed x10 -> x0, local copies, waits for them, and re-layouts: 4.2 us -> none
    pallas_call x1, Pallas kernels: 12.7 us -> 13.9 us  [per_device(): call(functools.partial(main_kernel, len(pieces)), (jax.ShapeDtypeStruct((...]
    pallas_call x1, Pallas kernels: 0.71 us -> 1.69 us  [per_device(): call(prep_kernel, (jax.ShapeDtypeStruct((SPAN, W * L), bf16), jax.ShapeDt...]
    ppermute x8, waiting for transfers between devices: 0.74 us -> 1.62 us  [swap(): return lax.ppermute(value, 'fibre', [(i, i ^ 1) for i in range(count)])]
  transfers between devices with their start and end apart: 15 -> 15, of which waited for: 7 -> 9; matrix products, arithmetic and copies ran while one was open for 0% -> 0% of each run, Pallas kernels for 1% -> 3%
where the time goes in v2:
time: 53.3 us; the launch traced here: 53.1 us
  waiting for transfers between devices  25.4 us (48%)
  Pallas kernels  15.6 us (29%)
  starting transfers between devices  11.5 us (22%)
  between operations  0.66 us (1%)
    ppermute x7, waiting for transfers between devices, ahead(): lax.ppermute(value, 'fibre', [(i, (i - distance) % count) for i in range(...  23.8 us
    pallas_call x1, Pallas kernels, per_device(): call(functools.partial(main_kernel, len(pieces)), (jax.ShapeDtypeStruct((...  13.9 us
    ppermute x7, starting transfers between devices, ahead(): lax.ppermute(value, 'fibre', [(i, (i - distance) % count) for i in range(...  10.4 us
    pallas_call x1, Pallas kernels, per_device(): call(prep_kernel, (jax.ShapeDtypeStruct((SPAN, W * L), bf16), jax.ShapeDt...  1.69 us
    ppermute x8, waiting for transfers between devices, swap(): return lax.ppermute(value, 'fibre', [(i, i ^ 1) for i in range(count)])  1.62 us
  transfers between devices with their start and end apart: 15, of which 9 were waited for; matrix products, arithmetic and copies ran while one was open for 0% of the time, Pallas kernels for 3%

profile of v2, /device:TPU:0, one launch (start us, length us, event | category | flops | bytes accessed | tf_op | source)
XLA Modules:
  0.0 53.1 jit_solution(12029465864843047959)
XLA Ops:
  0.6 5.1 %collective-permute-start.1 = (bf16[64,1600]{1,0:T(8,128)(2,1)}, bf16[64,1600]{1,0:T(8,128)(2,1)S(1)}, u32[]{:S(2)}, u32[]{:S(2)}) collective-permute-start(bf16[64,1600]{1,0:T(8,128)(2,1)} %refs_1_.1), channel_id=1, source_target_pairs={{0,12},{1,13},{2,14},{3,15},{4,0},{5,1},{6,2},{7,3},{8,4},{9,5},{1... | collective-permute-start | bytes 614408 | tf_op jit(solution)/shard_map/ppermute | solution.py:290
  5.8 1.4 %collective-permute-start = (bf16[64,1600]{1,0:T(8,128)(2,1)}, bf16[64,1600]{1,0:T(8,128)(2,1)S(1)}, u32[]{:S(2)}, u32[]{:S(2)}) collective-permute-start(bf16[64,1600]{1,0:T(8,128)(2,1)} %refs_1_.1), channel_id=1, source_target_pairs={{0,14},{1,15},{2,0},{3,1},{4,2},{5,3},{6,4},{7,5},{8,6},{9,7},{10,... | collective-permute-start | bytes 614408 | tf_op jit(solution)/shard_map/ppermute | solution.py:290
  7.2 4.5 %collective-permute-done.1.refs_3_ = bf16[64,1600]{1,0:T(8,128)(2,1)S(1)} collective-permute-done((bf16[64,1600]{1,0:T(8,128)(2,1)}, bf16[64,1600]{1,0:T(8,128)(2,1)S(1)}, u32[]{:S(2)}, u32[]{:S(2)}) %collective-permute-start.1) | collective-permute-done | bytes 204832 | tf_op jit(solution)/shard_map/ppermute | solution.py:290
  11.7 3.4 %collective-permute-done.refs_2_ = bf16[64,1600]{1,0:T(8,128)(2,1)S(1)} collective-permute-done((bf16[64,1600]{1,0:T(8,128)(2,1)}, bf16[64,1600]{1,0:T(8,128)(2,1)S(1)}, u32[]{:S(2)}, u32[]{:S(2)}) %collective-permute-start) | collective-permute-done | bytes 204832 | tf_op jit(solution)/shard_map/ppermute | solution.py:290
  15.2 0.0 collective-permute-start.3
  15.2 1.7 %shard_map.68 = (bf16[9,1600]{1,0:T(8,128)(2,1)S(1)}, bf16[1152,256]{1,0:T(8,128)(2,1)S(1)}, f32[336,128]{1,0:T(8,128)S(1)}, f32[8,128]{1,0:T(8,128)S(1)}, bf16[160,256]{1,0:T(8,128)(2,1)S(1)}) custom-call(s32[1]{0:T(128)} %bitcast.index_ref.refs_0_, bf16[9,63]{1,0:T(8,128)(2,1)} %taps_hbm.1, s32[1,1024]{1,0:T(1,128)} %bitcast.3, bf16[64,1600]{1,0:T(8,128)(2,1)} %refs_1_.1), custom_call_target="tpu_custom_call" | custom-call | tf_op jit(solution)/shard_map/pallas_call | solution.py:302
  16.9 0.1 collective-permute-start.9
  17.0 1.7 %collective-permute-start.8 = (bf16[9,1600]{1,0:T(8,128)(2,1)S(1)}, bf16[9,1600]{1,0:T(8,128)(2,1)S(1)}, u32[]{:S(2)}, u32[]{:S(2)}) collective-permute-start(bf16[9,1600]{1,0:T(8,128)(2,1)S(1)} %get-tuple-element.9), channel_id=1, source_target_pairs={{0,4},{1,5},{2,6},{3,7},{4,8},{5,9},{6,10},{7,11},{8,12},{9,13},{1... | collective-permute-start | bytes 86408 | tf_op jit(solution)/shard_map/ppermute | solution.py:290
  18.7 5.9 %collective-permute-done.9.refs_11_ = bf16[9,1600]{1,0:T(8,128)(2,1)S(1)} collective-permute-done((bf16[9,1600]{1,0:T(8,128)(2,1)S(1)}, bf16[9,1600]{1,0:T(8,128)(2,1)S(1)}, u32[]{:S(2)}, u32[]{:S(2)}) %collective-permute-start.9) | collective-permute-done | bytes 28832 | tf_op jit(solution)/shard_map/ppermute | solution.py:290
  24.7 0.1 collective-permute-done.8.refs_10_
  24.8 2.0 %collective-permute-start.6 = (bf16[9,1600]{1,0:T(8,128)(2,1)S(1)}, bf16[9,1600]{1,0:T(8,128)(2,1)S(1)}, u32[]{:S(2)}, u32[]{:S(2)}) collective-permute-start(bf16[9,1600]{1,0:T(8,128)(2,1)S(1)} %get-tuple-element.9), channel_id=1, source_target_pairs={{0,8},{1,9},{2,10},{3,11},{4,12},{5,13},{6,14},{7,15},{8,0},{9,1},... | collective-permute-start | bytes 86408 | tf_op jit(solution)/shard_map/ppermute | solution.py:290
  26.8 4.7 %collective-permute-done.7.refs_9_ = bf16[9,1600]{1,0:T(8,128)(2,1)S(1)} collective-permute-done((bf16[9,1600]{1,0:T(8,128)(2,1)S(1)}, bf16[9,1600]{1,0:T(8,128)(2,1)S(1)}, u32[]{:S(2)}, u32[]{:S(2)}) %collective-permute-start.7) | collective-permute-done | bytes 28832 | tf_op jit(solution)/shard_map/ppermute | solution.py:290
  31.5 0.0 collective-permute-start.5
  31.5 0.0 collective-permute-done.6.refs_8_
  31.5 0.0 collective-permute-start.14
  31.5 5.0 %collective-permute-done.5.refs_7_ = bf16[9,1600]{1,0:T(8,128)(2,1)S(1)} collective-permute-done((bf16[9,1600]{1,0:T(8,128)(2,1)S(1)}, bf16[9,1600]{1,0:T(8,128)(2,1)S(1)}, u32[]{:S(2)}, u32[]{:S(2)}) %collective-permute-start.5) | collective-permute-done | bytes 28832 | tf_op jit(solution)/shard_map/ppermute | solution.py:290
  36.5 0.5 collective-permute-start.12
  37.1 0.7 %collective-permute-done.13.refs_15_ = bf16[9,1600]{1,0:T(8,128)(2,1)S(1)} collective-permute-done((bf16[9,1600]{1,0:T(8,128)(2,1)S(1)}, bf16[9,1600]{1,0:T(8,128)(2,1)S(1)}, u32[]{:S(2)}, u32[]{:S(2)}) %collective-permute-start.13) | collective-permute-done | bytes 28832 | tf_op jit(solution)/shard_map/ppermute | solution.py:293
  37.8 0.2 collective-permute-start.11
  37.9 0.0 collective-permute-done.12.refs_14_
  37.9 0.3 collective-permute-start.10
  38.3 0.7 %collective-permute-done.11.refs_13_ = bf16[9,1600]{1,0:T(8,128)(2,1)S(1)} collective-permute-done((bf16[9,1600]{1,0:T(8,128)(2,1)S(1)}, bf16[9,1600]{1,0:T(8,128)(2,1)S(1)}, u32[]{:S(2)}, u32[]{:S(2)}) %collective-permute-start.11) | collective-permute-done | bytes 28832 | tf_op jit(solution)/shard_map/ppermute | solution.py:293
  39.0 0.2 collective-permute-done.10.refs_12_
  39.2 13.9 %shard_map.69 = (bf16[5,64,2048]{2,1,0:T(8,128)(2,1)}, bf16[64,512]{1,0:T(8,128)(2,1)}) custom-call(s32[1]{0:T(128)} %bitcast.index_ref.refs_0_, bf16[64,1600]{1,0:T(8,128)(2,1)} %refs_1_.1, bf16[64,1600]{1,0:T(8,128)(2,1)S(1)} %collective-permute-done.refs_2_, bf16[64,1600]{1,0:T(8,128)(2,1)S(1)} %collective-permute-done.1.refs_3_, ...), custom_call_target="tpu_custom_call" | custom-call | tf_op jit(solution)/shard_map/pallas_call | solution.py:344
  (8 shorter events, 0.0 us)
Async XLA Ops:
  0.6 11.1 %collective-permute-start.1 = (bf16[64,1600]{1,0:T(8,128)(2,1)}, bf16[64,1600]{1,0:T(8,128)(2,1)S(1)}, u32[]{:S(2)}, u32[]{:S(2)}) collective-permute-start(bf16[64,1600]{1,0:T(8,128)(2,1)} %refs_1_.1), channel_id=1, source_target_pairs={{0,12},{1,13},{2,14},{3,15},{4,0},{5,1},{6,2},{7,3},{8,4},{9,5},{1... | collective-permute-start | bytes 614408 | tf_op jit(solution)/shard_map/ppermute | solution.py:290
  5.8 9.4 %collective-permute-start = (bf16[64,1600]{1,0:T(8,128)(2,1)}, bf16[64,1600]{1,0:T(8,128)(2,1)S(1)}, u32[]{:S(2)}, u32[]{:S(2)}) collective-permute-start(bf16[64,1600]{1,0:T(8,128)(2,1)} %refs_1_.1), channel_id=1, source_target_pairs={{0,14},{1,15},{2,0},{3,1},{4,2},{5,3},{6,4},{7,5},{8,6},{9,7},{10,... | collective-permute-start | bytes 614408 | tf_op jit(solution)/shard_map/ppermute | solution.py:290
  7.2 32.0 %collective-permute-start.2 = (bf16[64,1600]{1,0:T(8,128)(2,1)}, bf16[64,1600]{1,0:T(8,128)(2,1)S(1)}, u32[]{:S(2)}, u32[]{:S(2)}) collective-permute-start(bf16[64,1600]{1,0:T(8,128)(2,1)} %refs_1_.1), channel_id=1, source_target_pairs={{0,1},{1,0},{2,3},{3,2},{4,5},{5,4},{6,7},{7,6},{8,9},{9,8},{10,11... | collective-permute-start | bytes 614408 | tf_op jit(solution)/shard_map/ppermute | solution.py:293
  11.7 27.5 %collective-permute-start.4 = (bf16[64,1600]{1,0:T(8,128)(2,1)S(1)}, bf16[64,1600]{1,0:T(8,128)(2,1)S(1)}, u32[]{:S(2)}, u32[]{:S(2)}) collective-permute-start(bf16[64,1600]{1,0:T(8,128)(2,1)S(1)} %collective-permute-done.1.refs_3_), channel_id=1, source_target_pairs={{0,1},{1,0},{2,3},{3,2},{4,5},{5,4},{6,7},{7,6},{8,9},{9,8},{10,11... | collective-permute-start | bytes 614408 | tf_op jit(solution)/shard_map/ppermute | solution.py:293
  15.2 24.0 %collective-permute-start.3 = (bf16[64,1600]{1,0:T(8,128)(2,1)S(1)}, bf16[64,1600]{1,0:T(8,128)(2,1)S(1)}, u32[]{:S(2)}, u32[]{:S(2)}) collective-permute-start(bf16[64,1600]{1,0:T(8,128)(2,1)S(1)} %collective-permute-done.refs_2_), channel_id=1, source_target_pairs={{0,1},{1,0},{2,3},{3,2},{4,5},{5,4},{6,7},{7,6},{8,9},{9,8},{10,11... | collective-permute-start | bytes 614408 | tf_op jit(solution)/shard_map/ppermute | solution.py:293
  16.9 7.8 %collective-permute-start.9 = (bf16[9,1600]{1,0:T(8,128)(2,1)S(1)}, bf16[9,1600]{1,0:T(8,128)(2,1)S(1)}, u32[]{:S(2)}, u32[]{:S(2)}) collective-permute-start(bf16[9,1600]{1,0:T(8,128)(2,1)S(1)} %get-tuple-element.9), channel_id=1, source_target_pairs={{0,2},{1,3},{2,4},{3,5},{4,6},{5,7},{6,8},{7,9},{8,10},{9,11},{10,... | collective-permute-start | bytes 86408 | tf_op jit(solution)/shard_map/ppermute | solution.py:290
  17.0 7.8 %collective-permute-start.8 = (bf16[9,1600]{1,0:T(8,128)(2,1)S(1)}, bf16[9,1600]{1,0:T(8,128)(2,1)S(1)}, u32[]{:S(2)}, u32[]{:S(2)}) collective-permute-start(bf16[9,1600]{1,0:T(8,128)(2,1)S(1)} %get-tuple-element.9), channel_id=1, source_target_pairs={{0,4},{1,5},{2,6},{3,7},{4,8},{5,9},{6,10},{7,11},{8,12},{9,13},{1... | collective-permute-start | bytes 86408 | tf_op jit(solution)/shard_map/ppermute | solution.py:290
  24.7 6.8 %collective-permute-start.7 = (bf16[9,1600]{1,0:T(8,128)(2,1)S(1)}, bf16[9,1600]{1,0:T(8,128)(2,1)S(1)}, u32[]{:S(2)}, u32[]{:S(2)}) collective-permute-start(bf16[9,1600]{1,0:T(8,128)(2,1)S(1)} %get-tuple-element.9), channel_id=1, source_target_pairs={{0,6},{1,7},{2,8},{3,9},{4,10},{5,11},{6,12},{7,13},{8,14},{9,15},... | collective-permute-start | bytes 86408 | tf_op jit(solution)/shard_map/ppermute | solution.py:290
  24.8 6.8 %collective-permute-start.6 = (bf16[9,1600]{1,0:T(8,128)(2,1)S(1)}, bf16[9,1600]{1,0:T(8,128)(2,1)S(1)}, u32[]{:S(2)}, u32[]{:S(2)}) collective-permute-start(bf16[9,1600]{1,0:T(8,128)(2,1)S(1)} %get-tuple-element.9), channel_id=1, source_target_pairs={{0,8},{1,9},{2,10},{3,11},{4,12},{5,13},{6,14},{7,15},{8,0},{9,1},... | collective-permute-start | bytes 86408 | tf_op jit(solution)/shard_map/ppermute | solution.py:290
  31.5 5.0 %collective-permute-start.5 = (bf16[9,1600]{1,0:T(8,128)(2,1)S(1)}, bf16[9,1600]{1,0:T(8,128)(2,1)S(1)}, u32[]{:S(2)}, u32[]{:S(2)}) collective-permute-start(bf16[9,1600]{1,0:T(8,128)(2,1)S(1)} %get-tuple-element.9), channel_id=1, source_target_pairs={{0,10},{1,11},{2,12},{3,13},{4,14},{5,15},{6,0},{7,1},{8,2},{9,3},... | collective-permute-start | bytes 86408 | tf_op jit(solution)/shard_map/ppermute | solution.py:290
  31.5 5.0 %collective-permute-start.14 = (bf16[9,1600]{1,0:T(8,128)(2,1)S(1)}, bf16[9,1600]{1,0:T(8,128)(2,1)S(1)}, u32[]{:S(2)}, u32[]{:S(2)}) collective-permute-start(bf16[9,1600]{1,0:T(8,128)(2,1)S(1)} %collective-permute-done.9.refs_11_), channel_id=1, source_target_pairs={{0,1},{1,0},{2,3},{3,2},{4,5},{5,4},{6,7},{7,6},{8,9},{9,8},{10,11... | collective-permute-start | bytes 86408 | tf_op jit(solution)/shard_map/ppermute | solution.py:293
  36.5 1.2 %collective-permute-start.13 = (bf16[9,1600]{1,0:T(8,128)(2,1)S(1)}, bf16[9,1600]{1,0:T(8,128)(2,1)S(1)}, u32[]{:S(2)}, u32[]{:S(2)}) collective-permute-start(bf16[9,1600]{1,0:T(8,128)(2,1)S(1)} %collective-permute-done.8.refs_10_), channel_id=1, source_target_pairs={{0,1},{1,0},{2,3},{3,2},{4,5},{5,4},{6,7},{7,6},{8,9},{9,8},{10,11... | collective-permute-start | bytes 86408 | tf_op jit(solution)/shard_map/ppermute | solution.py:293
  36.5 1.4 %collective-permute-start.12 = (bf16[9,1600]{1,0:T(8,128)(2,1)S(1)}, bf16[9,1600]{1,0:T(8,128)(2,1)S(1)}, u32[]{:S(2)}, u32[]{:S(2)}) collective-permute-start(bf16[9,1600]{1,0:T(8,128)(2,1)S(1)} %collective-permute-done.7.refs_9_), channel_id=1, source_target_pairs={{0,1},{1,0},{2,3},{3,2},{4,5},{5,4},{6,7},{7,6},{8,9},{9,8},{10,11... | collective-permute-start | bytes 86408 | tf_op jit(solution)/shard_map/ppermute | solution.py:293
  37.8 1.2 %collective-permute-start.11 = (bf16[9,1600]{1,0:T(8,128)(2,1)S(1)}, bf16[9,1600]{1,0:T(8,128)(2,1)S(1)}, u32[]{:S(2)}, u32[]{:S(2)}) collective-permute-start(bf16[9,1600]{1,0:T(8,128)(2,1)S(1)} %collective-permute-done.6.refs_8_), channel_id=1, source_target_pairs={{0,1},{1,0},{2,3},{3,2},{4,5},{5,4},{6,7},{7,6},{8,9},{9,8},{10,11... | collective-permute-start | bytes 86408 | tf_op jit(solution)/shard_map/ppermute | solution.py:293
  37.9 1.2 %collective-permute-start.10 = (bf16[9,1600]{1,0:T(8,128)(2,1)S(1)}, bf16[9,1600]{1,0:T(8,128)(2,1)S(1)}, u32[]{:S(2)}, u32[]{:S(2)}) collective-permute-start(bf16[9,1600]{1,0:T(8,128)(2,1)S(1)} %collective-permute-done.5.refs_7_), channel_id=1, source_target_pairs={{0,1},{1,0},{2,3},{3,2},{4,5},{5,4},{6,7},{7,6},{8,9},{9,8},{10,11... | collective-permute-start | bytes 86408 | tf_op jit(solution)/shard_map/ppermute | solution.py:293

commit v3 on v2

v3 whole, which is shorter than its diff:
```python
import functools

import jax
import jax.numpy as jnp
import numpy as np
from jax import lax
from jax.experimental import pallas as pl
from jax.experimental.pallas import tpu as pltpu
from jax.sharding import PartitionSpec as P


CB = 64
W = 4
F = 200
L = 400
TAPS = 63
SPAN = 9
LAGS = 32
BAND = 4
HALF = (SPAN - 1) // 2
SLOT = 16
HALO = 8
CHUNK = 128
NCHUNK = -(-W * L // CHUNK)
FP = 256
KP = W * 2 * FP
ROWS = (BAND + 1) * CB
SHIFT = L % CHUNK
COVER = 4 * CHUNK

VMEM_LIMIT = 28 << 20
PREP_LIMIT = 12 << 20
EDGE_LIMIT = 1 << 20
TABLE_LIMIT = 2 << 20

f32 = jnp.float32
bf16 = jnp.bfloat16


def dft_table():
    t = np.arange(L)
    taper = 0.5 - 0.5 * np.cos((t + 0.5) * (2.0 * np.pi / L))
    phase = (t[:, None] * np.arange(F)[None, :] % L) * (2.0 * np.pi / L)
    lead = (W - 1) * SHIFT
    table = np.zeros((lead + COVER, 2 * FP))
    table[lead : lead + L, :F] = taper[:, None] * np.cos(phase)
    table[lead : lead + L, FP : FP + F] = -taper[:, None] * np.sin(phase)
    return jnp.asarray(table.astype(np.float32), bf16)


def lag_tables():
    m = np.arange(LAGS) - LAGS // 2
    phase = (m[:, None] * np.arange(F)[None, :] % L) * (2.0 * np.pi / L)
    scale = 1.0 / np.sqrt(2.0 * L)
    tables = np.zeros((2, LAGS, FP))
    tables[0, :, :F] = np.cos(phase) * scale
    tables[1, :, :F] = -np.sin(phase) * scale
    return jnp.asarray(tables.astype(np.float32), bf16).astype(f32)


def start_loads(pairs, sems):
    loads = [pltpu.make_async_copy(source, target, sems.at[i]) for i, (source, target) in enumerate(pairs)]
    for load in loads:
        load.start()
    return loads


def edge_kernel(own_hbm, edge_ref, sems):
    last = (own_hbm.at[pl.ds(CB - HALO, HALO)], edge_ref.at[pl.ds(0, HALO)])
    first = (own_hbm.at[pl.ds(0, HALO)], edge_ref.at[pl.ds(HALO, HALO)])
    for load in start_loads((last, first), sems):
        load.wait()


def chunk(rows, j):
    piece = rows[:, j * CHUNK : min((j + 1) * CHUNK, W * L)]
    if piece.shape[1] < CHUNK:
        piece = jnp.concatenate([piece, jnp.zeros((piece.shape[0], CHUNK - piece.shape[1]), piece.dtype)], axis=1)
    return piece


def filter_row(row_at, seg_ref, centre, line, band_ref):
    own = seg_ref[centre : centre + 1, :]
    line[...] = jnp.zeros_like(line)
    for e in range(SPAN):
        at = centre - HALF + e
        keep = seg_ref[at : at + 1, :] == own
        for j in range(NCHUNK):
            line[j : j + 1, e * CHUNK : (e + 1) * CHUNK] = jnp.where(keep, row_at(e, j), 0.0)
    share = jnp.dot(line[...].astype(bf16), band_ref[...], preferred_element_type=f32)
    before = jnp.concatenate([jnp.zeros((1, CHUNK), f32), share[:-1, CHUNK:]], axis=0)
    return share[:, :CHUNK] + before


def prep_kernel(
    index_ref, edge_ref, halo_ref, sown_ref, taps_hbm, ids_hbm, source_ref, band_ref, seg_ref, pseg_ref,
    taps_ref, ids_ref, line, sems,
):
    loads = start_loads(((taps_hbm, taps_ref), (ids_hbm, ids_ref)), sems)
    device = index_ref[0]
    total = ids_ref.shape[1]
    count = total // CB
    loads[0].wait()
    wide = jnp.concatenate([taps_ref[...].astype(f32), jnp.zeros((SPAN, 2 * CHUNK - TAPS), f32)], axis=1)
    for e in range(SPAN):
        row = jnp.broadcast_to(wide[e : e + 1, :], (CHUNK, 2 * CHUNK))
        band_ref[e * CHUNK : (e + 1) * CHUNK, :] = pltpu.roll(row, 0, 1, stride=1, stride_axis=0).astype(bf16)

    loads[1].wait()
    ids = jnp.broadcast_to(ids_ref[...].astype(bf16), (CHUNK, total))
    channels = device * CB - HALO + lax.broadcasted_iota(jnp.int32, (ROWS + 2 * HALO, 1), 0)
    channels = jnp.where(channels < 0, channels + total, channels)
    channels = jnp.where(channels >= total, channels - total, channels)
    hit = lax.broadcasted_iota(jnp.int32, (ROWS + 2 * HALO, total), 1) == channels
    seg_ref[...] = lax.dot_general(
        jnp.where(hit, 1.0, 0.0).astype(bf16), ids, (((1,), (1,)), ((), ())), preferred_element_type=f32
    )
    for k in range(BAND + 1):
        block = seg_ref[HALO + k * CB : HALO + (k + 1) * CB, :]
        turned = jnp.transpose(jnp.concatenate([block, block], axis=0))
        pseg_ref[k : k + 1, :] = jnp.where(device + k < count, turned[:1], -1.0)
    pseg_ref[BAND + 1 :, :] = jnp.full((8 - BAND - 1, CHUNK), -1.0, f32)

    even = device % 2 == 0
    behind = jnp.where(even, halo_ref[:HALO].astype(f32), sown_ref[CB - HALO :].astype(f32))
    first = edge_ref[HALO:].astype(f32)

    def row_at(e, j):
        rows, at = (behind, HALO - HALF + e) if e < HALF else (first, e - HALF)
        return chunk(rows, j)[at : at + 1]

    source_ref[...] = filter_row(row_at, seg_ref, HALO, line, band_ref).astype(bf16)


def table_kernel(*refs):
    half = (len(refs) - 1) // 2
    for load in start_loads(tuple(zip(refs[:half], refs[half:-1])), refs[-1]):
        load.wait()


def main_kernel(pieces, count, *refs):
    index_ref, own_ref, two_ref, four_ref, sown_ref, stwo_ref, sfour_ref, halo_ref = refs[:8]
    part_refs, swapped_refs, refs = refs[8 : 8 + pieces], refs[8 + pieces : 9 + 2 * pieces], refs[9 + 2 * pieces :]
    seg_ref, pseg_ref, band_ref, dft_ref, lag_ref, out_ref, src_ref = refs[:7]
    rec, masked, filt, spec, turned, totals, line = refs[7:]
    even = index_ref[0] % 2 == 0

    def put(start, rows):
        for j in range(NCHUNK):
            rec[j, start : start + rows.shape[0], :] = chunk(rows, j)

    stwo, sfour = stwo_ref[...].astype(f32), sfour_ref[...].astype(f32)
    sown, halo = sown_ref[...].astype(f32), halo_ref[...].astype(f32)
    put(0, jnp.where(even, halo[:HALO], sown[CB - HALO :]))
    put(HALO, own_ref[...].astype(f32))
    put(HALO + CB, jnp.where(even, sown, stwo))
    put(HALO + 2 * CB, two_ref[...].astype(f32))
    put(HALO + 3 * CB, jnp.where(even, stwo, sfour))
    put(HALO + 4 * CB, four_ref[...].astype(f32))
    put(HALO + ROWS, jnp.where(even, sfour[:HALO], halo[HALO:]))

    def filtered(inputs, rows, start):
        share = jnp.dot(inputs[...], band_ref[...], preferred_element_type=f32)
        for j in range(NCHUNK):
            result = share[j * rows : (j + 1) * rows, :CHUNK]
            if j:
                result = result + share[(j - 1) * rows : j * rows, CHUNK:]
            filt[j, pl.ds(start, rows), :] = result.astype(bf16)

    for k in range(BAND + 1):
        base = k * CB
        held = masked.at[k % 2]
        centre = seg_ref[pl.ds(base + HALO, CB), :]
        for e in range(SPAN):
            first = base + (HALO - HALF + e)
            keep = seg_ref[pl.ds(first, CB), :] == centre
            for j in range(NCHUNK):
                rows = rec[j, pl.ds(first, CB), :]
                held[j * CB : (j + 1) * CB, e * CHUNK : (e + 1) * CHUNK] = jnp.where(keep, rows, 0.0).astype(bf16)
        filtered(held, CB, base)

    mine, theirs = [], []
    for refs, rows in ((part_refs, mine), (swapped_refs, theirs)):
        for ref in refs:
            value = ref[...].astype(f32)
            rows += [value[at : at + SLOT] for at in range(0, value.shape[0], SLOT)]
    lists = count // 2
    skip = lists - len(mine)
    theirs = [theirs[0]] + [None] * (skip - 1) + theirs[1:]

    def next_row(e, j):
        at = HALO + ROWS - HALF + e
        return rec[j, at : at + 1, :]

    for r in range(count):
        if r <= BAND:
            rows = [filt[j, r * CB : r * CB + 1, :] for j in range(NCHUNK)]
        else:
            if r == BAND + 1:
                value = filter_row(next_row, seg_ref, HALO + ROWS, line, band_ref)
            elif r % 2 == 0:
                value = mine[r // 2 - skip]
            else:
                value = jnp.where(even, theirs[r // 2], theirs[(r // 2 + 1) % lists])
            rows = [value[j : j + 1].astype(bf16) for j in range(NCHUNK)]
        for j in range(NCHUNK):
            filt[j, ROWS + r : ROWS + r + 1, :] = rows[j]

    for w in range(W):
        first = w * (L // CHUNK)
        lhs = jnp.concatenate([filt[first + q] for q in range(COVER // CHUNK)], axis=1)
        lead = (W - 1 - w) * SHIFT
        raw = jnp.dot(lhs, dft_ref[lead : lead + COVER, :], preferred_element_type=f32)
        power = jnp.sum(raw * raw, axis=-1, keepdims=True) * (1.0 / L)
        spec[:, w * 2 * FP : (w + 1) * 2 * FP] = (raw * lax.rsqrt(power + 1e-06)).astype(bf16)

    row = lax.broadcasted_iota(jnp.int32, (count, count), 0)
    column = lax.broadcasted_iota(jnp.int32, (count, count), 1)
    ahead = row - index_ref[0]
    ahead = jnp.where(ahead < 0, ahead + count, ahead)
    order = jnp.where(ahead == column, 1.0, 0.0).astype(bf16)
    spec[ROWS:, :] = jnp.dot(order, spec[ROWS:, :], preferred_element_type=f32).astype(bf16)

    group = turned.shape[0] // CB
    steps = LAGS // group
    own_seg = seg_ref[HALO : HALO + CB, :]

    def multiply(step, slot):
        start = pl.multiple_of(step * group, group)
        cosines = lag_ref[0, pl.ds(start, group), :]
        sines = lag_ref[1, pl.ds(start, group), :]
        for w in range(W):
            re_at, im_at = w * 2 * FP, w * 2 * FP + FP
            re = spec[:CB, re_at : re_at + FP].astype(f32)
            im = spec[:CB, im_at : im_at + FP].astype(f32)
            for g in range(group):
                c, s = cosines[g : g + 1, :], sines[g : g + 1, :]
                turned[g * CB : (g + 1) * CB, re_at : re_at + FP] = (re * c + im * s).astype(bf16)
                turned[g * CB : (g + 1) * CB, im_at : im_at + FP] = (im * c - re * s).astype(bf16)
        totals[slot] = lax.dot_general(
            turned[...], spec[...], (((1,), (1,)), ((), ())), preferred_element_type=f32
        )

    def write(step, slot):
        start = pl.multiple_of(step * group, group)
        for pair in range(group // 2):
            low, high = 2 * pair * CB, (2 * pair + 1) * CB
            lanes = pl.ds(pl.multiple_of(start * CB + pair * 2 * CB, 2 * CB), 2 * CB)
            for k in range(BAND + 1):
                both = jnp.concatenate(
                    [totals[slot, at : at + CB, k * CB : (k + 1) * CB] for at in (low, high)], axis=1
                )
                keep = own_seg == pseg_ref[k : k + 1, :]
                out_ref[k, :, lanes] = jnp.where(keep, both, 0.0).astype(bf16)
        sources = jnp.concatenate(
            [totals[slot, g * CB : (g + 1) * CB, ROWS : ROWS + count] for g in range(group)], axis=1
        )
        src_ref[:, pl.ds(pl.multiple_of(start * count, group * count), group * count)] = sources.astype(bf16)

    multiply(0, 0)

    @pl.loop(1, steps)
    def _(step):
        write(step - 1, (step - 1) % 2)
        multiply(step, step % 2)

    write(steps - 1, (steps - 1) % 2)


VMEM = pl.BlockSpec(memory_space=pltpu.VMEM)
SMEM = pl.BlockSpec(memory_space=pltpu.SMEM)
HBM = pl.BlockSpec(memory_space=pltpu.HBM)


def call(kernel, shapes, scratch, specs, **kwargs):
    return pl.pallas_call(
        kernel, out_shape=shapes, in_specs=specs, out_specs=jax.tree.map(lambda _: VMEM, shapes), scratch_shapes=scratch, **kwargs
    )


def per_device(records, filter_taps, segment_ids):
    count = lax.axis_size("fibre")
    device = lax.axis_index("fibre")

    def ahead(value, distance):
        return lax.ppermute(value, "fibre", [(i, (i - distance) % count) for i in range(count)])

    def swap(value):
        return lax.ppermute(value, "fibre", [(i, i ^ 1) for i in range(count)])

    index = device.reshape(1)
    few = count <= 16
    stay = functools.partial(pltpu.with_memory_space_constraint, memory_space=pltpu.HBM)

    edge = call(
        edge_kernel,
        jax.ShapeDtypeStruct((2 * HALO, W * L), bf16),
        [pltpu.SemaphoreType.DMA((2,))],
        [HBM],
        compiler_params=pltpu.CompilerParams(vmem_limit_bytes=EDGE_LIMIT),
    )(stay(records))
    route = [(i, (i + 1) % count if i % 2 else (i - BAND - 1) % count) for i in range(count)]
    halo = lax.ppermute(edge, "fibre", route)
    sown = swap(records)
    four = ahead(records, 4)
    two = ahead(records, 2)

    source, band, segs, pseg = call(
        prep_kernel,
        (
            jax.ShapeDtypeStruct((SLOT, CHUNK), bf16),
            jax.ShapeDtypeStruct((SPAN * CHUNK, 2 * CHUNK), bf16),
            jax.ShapeDtypeStruct((ROWS + 2 * HALO, CHUNK), f32),
            jax.ShapeDtypeStruct((8, CHUNK), f32),
        ),
        [
            pltpu.VMEM(filter_taps.shape, bf16),
            pltpu.VMEM((1,) + segment_ids.shape, jnp.int32),
            pltpu.VMEM((SLOT, SPAN * CHUNK), f32),
            pltpu.SemaphoreType.DMA((2,)),
        ],
        [SMEM] + [VMEM] * 3 + [HBM] * 2,
        compiler_params=pltpu.CompilerParams(vmem_limit_bytes=PREP_LIMIT if few else None),
    )(index, edge, halo, sown, stay(filter_taps), stay(segment_ids.reshape(1, -1)))
    tables = (records, dft_table(), lag_tables())
    own, dft, lags = call(
        table_kernel,
        tuple(jax.ShapeDtypeStruct(table.shape, table.dtype) for table in tables),
        [pltpu.SemaphoreType.DMA((len(tables),))],
        [HBM] * len(tables),
        compiler_params=pltpu.CompilerParams(vmem_limit_bytes=TABLE_LIMIT),
    )(*map(stay, tables))

    lists = count // 2
    first = BAND // 2 + 1 if lists <= 8 else 1
    parts = [ahead(source, 2 * s) for s in range(first, min(8, lists))]
    have = 8
    if have < lists:
        known = jnp.concatenate([source] + parts, axis=0)
    while have < lists:
        more = []
        for s in range(1, 8):
            left = lists - s * have
            if left > 0:
                more.append(ahead(known[: SLOT * left], 2 * s * have))
        parts += more
        known = jnp.concatenate([known] + more, axis=0)
        have = known.shape[0] // SLOT
    swapped = [swap(part) for part in [source] + parts]
    sfour, stwo = swap(four), swap(two)

    group = 8
    stacked, source_out = call(
        functools.partial(main_kernel, len(parts), count),
        (
            jax.ShapeDtypeStruct((BAND + 1, CB, LAGS * CB), bf16),
            jax.ShapeDtypeStruct((CB, LAGS * count), bf16),
        ),
        [
            pltpu.VMEM((NCHUNK, ROWS + 2 * HALO, CHUNK), f32),
            pltpu.VMEM((2, NCHUNK * CB, SPAN * CHUNK), bf16),
            pltpu.VMEM((NCHUNK, ROWS + count, CHUNK), bf16),
            pltpu.VMEM((ROWS + count, KP), bf16),
            pltpu.VMEM((group * CB, KP), bf16),
            pltpu.VMEM((2, group * CB, ROWS + count), f32),
            pltpu.VMEM((SLOT, SPAN * CHUNK), f32),
        ],
        [SMEM] + [VMEM] * (13 + 2 * len(parts)),
        compiler_params=pltpu.CompilerParams(vmem_limit_bytes=VMEM_LIMIT if few else None),
    )(
        index, own, two, four, sown, stwo, sfour, halo, *parts, *swapped, segs, pseg, band, dft, lags,
    )
    return (jnp.swapaxes(stacked, 0, 1), source_out)


def solution(mesh):
    return jax.shard_map(
        per_device,
        mesh=mesh,
        in_specs=(P(("runs", "fibre"), None), P(), P("runs")),
        out_specs=(P(("runs", "fibre"), None, None), P(("runs", "fibre"), None)),
        check_vma=False,
    )
```

time: 53.3 us -> 51.5 us (0.966)
  waiting for transfers between devices: 25.4 us -> 21 us
  starting transfers between devices: 11.5 us -> 13.2 us
  Pallas kernels: 15.6 us -> 16.3 us
    ppermute x7, waiting for transfers between devices: 23.8 us -> 14.6 us  [ahead(): lax.ppermute(value, 'fibre', [(i, (i - distance) % count) for i in range(...]
    ppermute x0 -> x1, waiting for transfers between devices: none -> 5.01 us  [per_device(): halo = lax.ppermute(edge, 'fibre', route)]
    ppermute x0 -> x1, starting transfers between devices: none -> 2.43 us  [per_device(): halo = lax.ppermute(edge, 'fibre', route)]
    pallas_call x2 -> x4, Pallas kernels: 15.6 us -> 16.3 us  [the longest x1 12.8 us: per_device(): call(functools.partial(main_kernel, len(parts), count), (jax.ShapeDtypeSt...]
    ppermute x8 -> x9, waiting for transfers between devices: 1.62 us -> 1.47 us  [swap(): return lax.ppermute(value, 'fibre', [(i, i ^ 1) for i in range(count)])]
  transfers between devices with their start and end apart: 15 -> 17, of which waited for: 9 -> 7; matrix products, arithmetic and copies ran while one was open for 0% -> 0% of each run, Pallas kernels for 3% -> 7%
where the time goes in v3:
time: 51.5 us; the launch traced here: 51.3 us
  waiting for transfers between devices  21 us (41%)
  Pallas kernels  16.3 us (32%)
  starting transfers between devices  13.2 us (26%)
  between operations  0.72 us (1%)
    ppermute x7, waiting for transfers between devices, ahead(): lax.ppermute(value, 'fibre', [(i, (i - distance) % count) for i in range(...  14.6 us
    pallas_call x1, Pallas kernels, per_device(): call(functools.partial(main_kernel, len(parts), count), (jax.ShapeDtypeSt...  12.8 us
    ppermute x7, starting transfers between devices, ahead(): lax.ppermute(value, 'fibre', [(i, (i - distance) % count) for i in range(...  9.93 us
    ppermute x1, waiting for transfers between devices, per_device(): halo = lax.ppermute(edge, 'fibre', route)  5.01 us
    ppermute x1, starting transfers between devices, per_device(): halo = lax.ppermute(edge, 'fibre', route)  2.43 us
    pallas_call x1, Pallas kernels, per_device(): call(prep_kernel, (jax.ShapeDtypeStruct((SLOT, CHUNK), bf16), jax.ShapeDt...  1.56 us
    ppermute x9, waiting for transfers between devices, swap(): return lax.ppermute(value, 'fibre', [(i, i ^ 1) for i in range(count)])  1.47 us
    pallas_call x1, Pallas kernels, per_device(): call(table_kernel, tuple((jax.ShapeDtypeStruct(table.shape, table.dtype)...  1.2 us
  transfers between devices with their start and end apart: 17, of which 7 were waited for; matrix products, arithmetic and copies ran while one was open for 0% of the time, Pallas kernels for 7%

profile of v3, /device:TPU:0, one launch (start us, length us, event | category | flops | bytes accessed | tf_op | source)
XLA Modules:
  0.0 51.3 jit_solution(33090865738205804)
XLA Ops:
  0.6 5.1 %collective-permute-start.1 = (bf16[64,1600]{1,0:T(8,128)(2,1)}, bf16[64,1600]{1,0:T(8,128)(2,1)S(1)}, u32[]{:S(2)}, u32[]{:S(2)}) collective-permute-start(bf16[64,1600]{1,0:T(8,128)(2,1)} %own_hbm.1), channel_id=1, source_target_pairs={{0,12},{1,13},{2,14},{3,15},{4,0},{5,1},{6,2},{7,3},{8,4},{9,5},{1... | collective-permute-start | bytes 614408 | tf_op jit(solution)/shard_map/ppermute | solution.py:286
  5.8 1.4 %collective-permute-start = (bf16[64,1600]{1,0:T(8,128)(2,1)}, bf16[64,1600]{1,0:T(8,128)(2,1)S(1)}, u32[]{:S(2)}, u32[]{:S(2)}) collective-permute-start(bf16[64,1600]{1,0:T(8,128)(2,1)} %own_hbm.1), channel_id=1, source_target_pairs={{0,14},{1,15},{2,0},{3,1},{4,2},{5,3},{6,4},{7,5},{8,6},{9,7},{10,... | collective-permute-start | bytes 614408 | tf_op jit(solution)/shard_map/ppermute | solution.py:286
  7.2 0.0 collective-permute-start.2
  7.2 4.5 %collective-permute-done.1.refs_3_ = bf16[64,1600]{1,0:T(8,128)(2,1)S(1)} collective-permute-done((bf16[64,1600]{1,0:T(8,128)(2,1)}, bf16[64,1600]{1,0:T(8,128)(2,1)S(1)}, u32[]{:S(2)}, u32[]{:S(2)}) %collective-permute-start.1) | collective-permute-done | bytes 204832 | tf_op jit(solution)/shard_map/ppermute | solution.py:286
  11.7 3.4 %collective-permute-done.refs_2_ = bf16[64,1600]{1,0:T(8,128)(2,1)S(1)} collective-permute-done((bf16[64,1600]{1,0:T(8,128)(2,1)}, bf16[64,1600]{1,0:T(8,128)(2,1)S(1)}, u32[]{:S(2)}, u32[]{:S(2)}) %collective-permute-start) | collective-permute-done | bytes 204832 | tf_op jit(solution)/shard_map/ppermute | solution.py:286
  15.2 0.8 %shard_map.69.edge_ref = bf16[16,1600]{1,0:T(8,128)(2,1)S(1)} custom-call(bf16[64,1600]{1,0:T(8,128)(2,1)} %own_hbm.1), custom_call_target="tpu_custom_call" | custom-call | tf_op jit(solution)/shard_map/pallas_call | solution.py:295
  15.9 2.4 %collective-permute-start.5 = (bf16[16,1600]{1,0:T(8,128)(2,1)S(1)}, bf16[16,1600]{1,0:T(8,128)(2,1)S(1)}, u32[]{:S(2)}, u32[]{:S(2)}) collective-permute-start(bf16[16,1600]{1,0:T(8,128)(2,1)S(1)} %shard_map.69.edge_ref), channel_id=1, source_target_pairs={{0,11},{1,2},{2,13},{3,4},{4,15},{5,6},{6,1},{7,8},{8,3},{9,10},{1... | collective-permute-start | bytes 153608 | tf_op jit(solution)/shard_map/ppermute | solution.py:303
  18.4 5.0 %collective-permute-done.5.halo_ref.refs_7_ = bf16[16,1600]{1,0:T(8,128)(2,1)S(1)} collective-permute-done((bf16[16,1600]{1,0:T(8,128)(2,1)S(1)}, bf16[16,1600]{1,0:T(8,128)(2,1)S(1)}, u32[]{:S(2)}, u32[]{:S(2)}) %collective-permute-start.5) | collective-permute-done | bytes 51232 | tf_op jit(solution)/shard_map/ppermute | solution.py:303
  23.4 1.6 %shard_map.70 = (bf16[16,128]{1,0:T(8,128)(2,1)S(1)}, bf16[1152,256]{1,0:T(8,128)(2,1)S(1)}, f32[336,128]{1,0:T(8,128)S(1)}, f32[8,128]{1,0:T(8,128)S(1)}) custom-call(s32[1]{0:T(128)} %bitcast.index_ref.refs_0_, bf16[16,1600]{1,0:T(8,128)(2,1)S(1)} %shard_map.69.edge_ref, bf16[16,1600]{1,0:T(8,128)(2,1)S(1)} %collective-permute-done.5.halo_ref.refs_7_, ...), custom_call_target="tpu_custom_call" | custom-call | tf_op jit(solution)/shard_map/pallas_call | solution.py:308
  24.9 0.1 collective-permute-start.11
  25.0 0.1 collective-permute-start.10
  25.1 0.2 collective-permute-start.9
  25.3 0.9 %collective-permute-done.11.refs_13_ = bf16[16,128]{1,0:T(8,128)(2,1)S(1)} collective-permute-done((bf16[16,128]{1,0:T(8,128)(2,1)S(1)}, bf16[16,128]{1,0:T(8,128)(2,1)S(1)}, u32[]{:S(2)}, u32[]{:S(2)}) %collective-permute-start.11) | collective-permute-done | bytes 4128 | tf_op jit(solution)/shard_map/ppermute | solution.py:289
  26.2 1.0 %collective-permute-start.8 = (bf16[16,128]{1,0:T(8,128)(2,1)S(1)}, bf16[16,128]{1,0:T(8,128)(2,1)S(1)}, u32[]{:S(2)}, u32[]{:S(2)}) collective-permute-start(bf16[16,128]{1,0:T(8,128)(2,1)S(1)} %get-tuple-element.12), channel_id=1, source_target_pairs={{0,6},{1,7},{2,8},{3,9},{4,10},{5,11},{6,12},{7,13},{8,14},{9,15},... | collective-permute-start | bytes 12296 | tf_op jit(solution)/shard_map/ppermute | solution.py:286
  27.2 4.2 %collective-permute-done.10.refs_12_ = bf16[16,128]{1,0:T(8,128)(2,1)S(1)} collective-permute-done((bf16[16,128]{1,0:T(8,128)(2,1)S(1)}, bf16[16,128]{1,0:T(8,128)(2,1)S(1)}, u32[]{:S(2)}, u32[]{:S(2)}) %collective-permute-start.10) | collective-permute-done | bytes 4128 | tf_op jit(solution)/shard_map/ppermute | solution.py:286
  31.4 2.1 %collective-permute-start.6 = (bf16[16,128]{1,0:T(8,128)(2,1)S(1)}, bf16[16,128]{1,0:T(8,128)(2,1)S(1)}, u32[]{:S(2)}, u32[]{:S(2)}) collective-permute-start(bf16[16,128]{1,0:T(8,128)(2,1)S(1)} %get-tuple-element.12), channel_id=1, source_target_pairs={{0,10},{1,11},{2,12},{3,13},{4,14},{5,15},{6,0},{7,1},{8,2},{9,3},... | collective-permute-start | bytes 12296 | tf_op jit(solution)/shard_map/ppermute | solution.py:286
  33.5 2.4 %collective-permute-done.7.refs_9_ = bf16[16,128]{1,0:T(8,128)(2,1)S(1)} collective-permute-done((bf16[16,128]{1,0:T(8,128)(2,1)S(1)}, bf16[16,128]{1,0:T(8,128)(2,1)S(1)}, u32[]{:S(2)}, u32[]{:S(2)}) %collective-permute-start.7) | collective-permute-done | bytes 4128 | tf_op jit(solution)/shard_map/ppermute | solution.py:286
  35.9 0.0 collective-permute-done.6.refs_8_
  35.9 0.5 collective-permute-start.14
  36.4 0.1 collective-permute-start.13
  36.5 0.6 %collective-permute-done.15.refs_17_ = bf16[16,128]{1,0:T(8,128)(2,1)S(1)} collective-permute-done((bf16[16,128]{1,0:T(8,128)(2,1)S(1)}, bf16[16,128]{1,0:T(8,128)(2,1)S(1)}, u32[]{:S(2)}, u32[]{:S(2)}) %collective-permute-start.15) | collective-permute-done | bytes 4128 | tf_op jit(solution)/shard_map/ppermute | solution.py:289
  37.1 0.2 collective-permute-start.12
  37.2 1.2 %shard_map.68 = (bf16[64,1600]{1,0:T(8,128)(2,1)S(1)}, bf16[560,512]{1,0:T(8,128)(2,1)S(1)}, f32[2,32,256]{2,1,0:T(8,128)S(1)}) custom-call(bf16[64,1600]{1,0:T(8,128)(2,1)} %own_hbm.1, bf16[560,512]{1,0:T(8,128)(2,1)} %constant.8.clone.refs_1_, f32[2,32,256]{2,1,0:T(8,128)} %constant.10.refs_2_), custom_call_target="tpu_custom_call" | custom-call | tf_op jit(solution)/shard_map/pallas_call | solution.py:326
  38.5 12.8 %shard_map.71 = (bf16[5,64,2048]{2,1,0:T(8,128)(2,1)}, bf16[64,512]{1,0:T(8,128)(2,1)}) custom-call(s32[1]{0:T(128)} %bitcast.index_ref.refs_0_, bf16[64,1600]{1,0:T(8,128)(2,1)S(1)} %get-tuple-element.11.refs_1_, bf16[64,1600]{1,0:T(8,128)(2,1)S(1)} %collective-permute-done.refs_2_, bf16[64,1600]{1,0:T(8,128)(2,1)S(1)} %collective-permute-done.1.refs_3_, ...), custom_call_target="tpu_custom_call" | custom-call | tf_op jit(solution)/shard_map/pallas_call | solution.py:353
  (14 shorter events, 0.0 us)
Async XLA Ops:
  0.6 11.1 %collective-permute-start.1 = (bf16[64,1600]{1,0:T(8,128)(2,1)}, bf16[64,1600]{1,0:T(8,128)(2,1)S(1)}, u32[]{:S(2)}, u32[]{:S(2)}) collective-permute-start(bf16[64,1600]{1,0:T(8,128)(2,1)} %own_hbm.1), channel_id=1, source_target_pairs={{0,12},{1,13},{2,14},{3,15},{4,0},{5,1},{6,2},{7,3},{8,4},{9,5},{1... | collective-permute-start | bytes 614408 | tf_op jit(solution)/shard_map/ppermute | solution.py:286
  5.8 9.4 %collective-permute-start = (bf16[64,1600]{1,0:T(8,128)(2,1)}, bf16[64,1600]{1,0:T(8,128)(2,1)S(1)}, u32[]{:S(2)}, u32[]{:S(2)}) collective-permute-start(bf16[64,1600]{1,0:T(8,128)(2,1)} %own_hbm.1), channel_id=1, source_target_pairs={{0,14},{1,15},{2,0},{3,1},{4,2},{5,3},{6,4},{7,5},{8,6},{9,7},{10,... | collective-permute-start | bytes 614408 | tf_op jit(solution)/shard_map/ppermute | solution.py:286
  7.2 16.2 %collective-permute-start.2 = (bf16[64,1600]{1,0:T(8,128)(2,1)}, bf16[64,1600]{1,0:T(8,128)(2,1)S(1)}, u32[]{:S(2)}, u32[]{:S(2)}) collective-permute-start(bf16[64,1600]{1,0:T(8,128)(2,1)} %own_hbm.1), channel_id=1, source_target_pairs={{0,1},{1,0},{2,3},{3,2},{4,5},{5,4},{6,7},{7,6},{8,9},{9,8},{10,11... | collective-permute-start | bytes 614408 | tf_op jit(solution)/shard_map/ppermute | solution.py:289
  11.7 26.7 %collective-permute-start.4 = (bf16[64,1600]{1,0:T(8,128)(2,1)S(1)}, bf16[64,1600]{1,0:T(8,128)(2,1)S(1)}, u32[]{:S(2)}, u32[]{:S(2)}) collective-permute-start(bf16[64,1600]{1,0:T(8,128)(2,1)S(1)} %collective-permute-done.1.refs_3_), channel_id=1, source_target_pairs={{0,1},{1,0},{2,3},{3,2},{4,5},{5,4},{6,7},{7,6},{8,9},{9,8},{10,11... | collective-permute-start | bytes 614408 | tf_op jit(solution)/shard_map/ppermute | solution.py:289
  15.2 23.3 %collective-permute-start.3 = (bf16[64,1600]{1,0:T(8,128)(2,1)S(1)}, bf16[64,1600]{1,0:T(8,128)(2,1)S(1)}, u32[]{:S(2)}, u32[]{:S(2)}) collective-permute-start(bf16[64,1600]{1,0:T(8,128)(2,1)S(1)} %collective-permute-done.refs_2_), channel_id=1, source_target_pairs={{0,1},{1,0},{2,3},{3,2},{4,5},{5,4},{6,7},{7,6},{8,9},{9,8},{10,11... | collective-permute-start | bytes 614408 | tf_op jit(solution)/shard_map/ppermute | solution.py:289
  15.9 7.4 %collective-permute-start.5 = (bf16[16,1600]{1,0:T(8,128)(2,1)S(1)}, bf16[16,1600]{1,0:T(8,128)(2,1)S(1)}, u32[]{:S(2)}, u32[]{:S(2)}) collective-permute-start(bf16[16,1600]{1,0:T(8,128)(2,1)S(1)} %shard_map.69.edge_ref), channel_id=1, source_target_pairs={{0,11},{1,2},{2,13},{3,4},{4,15},{5,6},{6,1},{7,8},{8,3},{9,10},{1... | collective-permute-start | bytes 153608 | tf_op jit(solution)/shard_map/ppermute | solution.py:303
  24.9 1.2 %collective-permute-start.11 = (bf16[16,128]{1,0:T(8,128)(2,1)S(1)}, bf16[16,128]{1,0:T(8,128)(2,1)S(1)}, u32[]{:S(2)}, u32[]{:S(2)}) collective-permute-start(bf16[16,128]{1,0:T(8,128)(2,1)S(1)} %get-tuple-element.12), channel_id=1, source_target_pairs={{0,1},{1,0},{2,3},{3,2},{4,5},{5,4},{6,7},{7,6},{8,9},{9,8},{10,11... | collective-permute-start | bytes 12296 | tf_op jit(solution)/shard_map/ppermute | solution.py:289
  25.0 6.4 %collective-permute-start.10 = (bf16[16,128]{1,0:T(8,128)(2,1)S(1)}, bf16[16,128]{1,0:T(8,128)(2,1)S(1)}, u32[]{:S(2)}, u32[]{:S(2)}) collective-permute-start(bf16[16,128]{1,0:T(8,128)(2,1)S(1)} %get-tuple-element.12), channel_id=1, source_target_pairs={{0,2},{1,3},{2,4},{3,5},{4,6},{5,7},{6,8},{7,9},{8,10},{9,11},{10,... | collective-permute-start | bytes 12296 | tf_op jit(solution)/shard_map/ppermute | solution.py:286
  25.1 6.3 %collective-permute-start.9 = (bf16[16,128]{1,0:T(8,128)(2,1)S(1)}, bf16[16,128]{1,0:T(8,128)(2,1)S(1)}, u32[]{:S(2)}, u32[]{:S(2)}) collective-permute-start(bf16[16,128]{1,0:T(8,128)(2,1)S(1)} %get-tuple-element.12), channel_id=1, source_target_pairs={{0,4},{1,5},{2,6},{3,7},{4,8},{5,9},{6,10},{7,11},{8,12},{9,13},{1... | collective-permute-start | bytes 12296 | tf_op jit(solution)/shard_map/ppermute | solution.py:286
  26.2 7.4 %collective-permute-start.8 = (bf16[16,128]{1,0:T(8,128)(2,1)S(1)}, bf16[16,128]{1,0:T(8,128)(2,1)S(1)}, u32[]{:S(2)}, u32[]{:S(2)}) collective-permute-start(bf16[16,128]{1,0:T(8,128)(2,1)S(1)} %get-tuple-element.12), channel_id=1, source_target_pairs={{0,6},{1,7},{2,8},{3,9},{4,10},{5,11},{6,12},{7,13},{8,14},{9,15},... | collective-permute-start | bytes 12296 | tf_op jit(solution)/shard_map/ppermute | solution.py:286
  31.4 4.5 %collective-permute-start.7 = (bf16[16,128]{1,0:T(8,128)(2,1)S(1)}, bf16[16,128]{1,0:T(8,128)(2,1)S(1)}, u32[]{:S(2)}, u32[]{:S(2)}) collective-permute-start(bf16[16,128]{1,0:T(8,128)(2,1)S(1)} %get-tuple-element.12), channel_id=1, source_target_pairs={{0,8},{1,9},{2,10},{3,11},{4,12},{5,13},{6,14},{7,15},{8,0},{9,1},... | collective-permute-start | bytes 12296 | tf_op jit(solution)/shard_map/ppermute | solution.py:286
  31.4 4.5 %collective-permute-start.6 = (bf16[16,128]{1,0:T(8,128)(2,1)S(1)}, bf16[16,128]{1,0:T(8,128)(2,1)S(1)}, u32[]{:S(2)}, u32[]{:S(2)}) collective-permute-start(bf16[16,128]{1,0:T(8,128)(2,1)S(1)} %get-tuple-element.12), channel_id=1, source_target_pairs={{0,10},{1,11},{2,12},{3,13},{4,14},{5,15},{6,0},{7,1},{8,2},{9,3},... | collective-permute-start | bytes 12296 | tf_op jit(solution)/shard_map/ppermute | solution.py:286
  33.5 2.9 %collective-permute-start.16 = (bf16[16,128]{1,0:T(8,128)(2,1)S(1)}, bf16[16,128]{1,0:T(8,128)(2,1)S(1)}, u32[]{:S(2)}, u32[]{:S(2)}) collective-permute-start(bf16[16,128]{1,0:T(8,128)(2,1)S(1)} %collective-permute-done.10.refs_12_), channel_id=1, source_target_pairs={{0,1},{1,0},{2,3},{3,2},{4,5},{5,4},{6,7},{7,6},{8,9},{9,8},{10,11... | collective-permute-start | bytes 12296 | tf_op jit(solution)/shard_map/ppermute | solution.py:289
  35.9 1.2 %collective-permute-start.15 = (bf16[16,128]{1,0:T(8,128)(2,1)S(1)}, bf16[16,128]{1,0:T(8,128)(2,1)S(1)}, u32[]{:S(2)}, u32[]{:S(2)}) collective-permute-start(bf16[16,128]{1,0:T(8,128)(2,1)S(1)} %collective-permute-done.9.refs_11_), channel_id=1, source_target_pairs={{0,1},{1,0},{2,3},{3,2},{4,5},{5,4},{6,7},{7,6},{8,9},{9,8},{10,11... | collective-permute-start | bytes 12296 | tf_op jit(solution)/shard_map/ppermute | solution.py:289
  35.9 2.5 %collective-permute-start.14 = (bf16[16,128]{1,0:T(8,128)(2,1)S(1)}, bf16[16,128]{1,0:T(8,128)(2,1)S(1)}, u32[]{:S(2)}, u32[]{:S(2)}) collective-permute-start(bf16[16,128]{1,0:T(8,128)(2,1)S(1)} %collective-permute-done.8.refs_10_), channel_id=1, source_target_pairs={{0,1},{1,0},{2,3},{3,2},{4,5},{5,4},{6,7},{7,6},{8,9},{9,8},{10,11... | collective-permute-start | bytes 12296 | tf_op jit(solution)/shard_map/ppermute | solution.py:289
  36.4 2.0 %collective-permute-start.13 = (bf16[16,128]{1,0:T(8,128)(2,1)S(1)}, bf16[16,128]{1,0:T(8,128)(2,1)S(1)}, u32[]{:S(2)}, u32[]{:S(2)}) collective-permute-start(bf16[16,128]{1,0:T(8,128)(2,1)S(1)} %collective-permute-done.7.refs_9_), channel_id=1, source_target_pairs={{0,1},{1,0},{2,3},{3,2},{4,5},{5,4},{6,7},{7,6},{8,9},{9,8},{10,11... | collective-permute-start | bytes 12296 | tf_op jit(solution)/shard_map/ppermute | solution.py:289
  37.1 1.4 %collective-permute-start.12 = (bf16[16,128]{1,0:T(8,128)(2,1)S(1)}, bf16[16,128]{1,0:T(8,128)(2,1)S(1)}, u32[]{:S(2)}, u32[]{:S(2)}) collective-permute-start(bf16[16,128]{1,0:T(8,128)(2,1)S(1)} %collective-permute-done.6.refs_8_), channel_id=1, source_target_pairs={{0,1},{1,0},{2,3},{3,2},{4,5},{5,4},{6,7},{7,6},{8,9},{9,8},{10,11... | collective-permute-start | bytes 12296 | tf_op jit(solution)/shard_map/ppermute | solution.py:289

commit v4 on v3

--- a/solution.py
+++ b/solution.py
@@ -93,13 +93,14 @@
 
 
 def prep_kernel(
-    index_ref, edge_ref, halo_ref, sown_ref, taps_hbm, ids_hbm, source_ref, band_ref, seg_ref, pseg_ref,
-    taps_ref, ids_ref, line, sems,
+    index_ref, edge_ref, halo_ref, sown_ref, taps_hbm, ids_hbm, own_hbm, dft_hbm, lag_hbm,
+    source_ref, band_ref, seg_ref, own_ref, dft_ref, lag_ref, taps_ref, ids_ref, line, sems,
 ):
-    loads = start_loads(((taps_hbm, taps_ref), (ids_hbm, ids_ref)), sems)
+    loads = start_loads(
+        ((taps_hbm, taps_ref), (ids_hbm, ids_ref), (own_hbm, own_ref), (dft_hbm, dft_ref), (lag_hbm, lag_ref)), sems
+    )
     device = index_ref[0]
     total = ids_ref.shape[1]
-    count = total // CB
     loads[0].wait()
     wide = jnp.concatenate([taps_ref[...].astype(f32), jnp.zeros((SPAN, 2 * CHUNK - TAPS), f32)], axis=1)
     for e in range(SPAN):
@@ -115,32 +116,31 @@
     seg_ref[...] = lax.dot_general(
         jnp.where(hit, 1.0, 0.0).astype(bf16), ids, (((1,), (1,)), ((), ())), preferred_element_type=f32
     )
+
+    even = device % 2 == 0
+    behind = jnp.where(even, halo_ref[:HALO].astype(f32), sown_ref[CB - HALO :].astype(f32))
+    first = edge_ref[HALO:].astype(f32)
+
+    def row_at(e, j):
+        rows, at = (behind, HALO - HALF + e) if e < HALF else (first, e - HALF)
+        return chunk(rows, j)[at : at + 1]
+
+    source_ref[...] = filter_row(row_at, seg_ref, HALO, line, band_ref).astype(bf16)
+    for load in loads[2:]:
+        load.wait()
+
+
+def partner_kernel(count, index_ref, seg_ref, pseg_ref):
     for k in range(BAND + 1):
         block = seg_ref[HALO + k * CB : HALO + (k + 1) * CB, :]
         turned = jnp.transpose(jnp.concatenate([block, block], axis=0))
-        pseg_ref[k : k + 1, :] = jnp.where(device + k < count, turned[:1], -1.0)
+        pseg_ref[k : k + 1, :] = jnp.where(index_ref[0] + k < count, turned[:1], -1.0)
     pseg_ref[BAND + 1 :, :] = jnp.full((8 - BAND - 1, CHUNK), -1.0, f32)
-
-    even = device % 2 == 0
-    behind = jnp.where(even, halo_ref[:HALO].astype(f32), sown_ref[CB - HALO :].astype(f32))
-    first = edge_ref[HALO:].astype(f32)
-
-    def row_at(e, j):
-        rows, at = (behind, HALO - HALF + e) if e < HALF else (first, e - HALF)
-        return chunk(rows, j)[at : at + 1]
-
-    source_ref[...] = filter_row(row_at, seg_ref, HALO, line, band_ref).astype(bf16)
-
-
-def table_kernel(*refs):
-    half = (len(refs) - 1) // 2
-    for load in start_loads(tuple(zip(refs[:half], refs[half:-1])), refs[-1]):
-        load.wait()
 
 
 def main_kernel(pieces, count, *refs):
     index_ref, own_ref, two_ref, four_ref, sown_ref, stwo_ref, sfour_ref, halo_ref = refs[:8]
-    part_refs, swapped_refs, refs = refs[8 : 8 + pieces], refs[8 + pieces : 9 + 2 * pieces], refs[9 + 2 * pieces :]
+    part_refs, refs = refs[8 : 8 + pieces], refs[8 + pieces :]
     seg_ref, pseg_ref, band_ref, dft_ref, lag_ref, out_ref, src_ref = refs[:7]
     rec, masked, filt, spec, turned, totals, line = refs[7:]
     even = index_ref[0] % 2 == 0
@@ -179,14 +179,14 @@
                 held[j * CB : (j + 1) * CB, e * CHUNK : (e + 1) * CHUNK] = jnp.where(keep, rows, 0.0).astype(bf16)
         filtered(held, CB, base)
 
-    mine, theirs = [], []
-    for refs, rows in ((part_refs, mine), (swapped_refs, theirs)):
-        for ref in refs:
-            value = ref[...].astype(f32)
-            rows += [value[at : at + SLOT] for at in range(0, value.shape[0], SLOT)]
+    rows = []
+    for ref in part_refs:
+        value = ref[...].astype(f32)
+        rows += [value[at : at + SLOT] for at in range(0, value.shape[0], SLOT)]
+    mine, theirs = rows[::2], rows[1::2]
     lists = count // 2
     skip = lists - len(mine)
-    theirs = [theirs[0]] + [None] * (skip - 1) + theirs[1:]
+    mine, theirs = ([part[0]] + [None] * skip + part[1:] for part in (mine, theirs))
 
     def next_row(e, j):
         at = HALO + ROWS - HALF + e
@@ -199,7 +199,7 @@
             if r == BAND + 1:
                 value = filter_row(next_row, seg_ref, HALO + ROWS, line, band_ref)
             elif r % 2 == 0:
-                value = mine[r // 2 - skip]
+                value = mine[r // 2]
             else:
                 value = jnp.where(even, theirs[r // 2], theirs[(r // 2 + 1) % lists])
             rows = [value[j : j + 1].astype(bf16) for j in range(NCHUNK)]
@@ -305,48 +305,46 @@
     four = ahead(records, 4)
     two = ahead(records, 2)
 
-    source, band, segs, pseg = call(
+    dft, lags = dft_table(), lag_tables()
+    source, band, segs, own, dft, lags = call(
         prep_kernel,
         (
             jax.ShapeDtypeStruct((SLOT, CHUNK), bf16),
             jax.ShapeDtypeStruct((SPAN * CHUNK, 2 * CHUNK), bf16),
             jax.ShapeDtypeStruct((ROWS + 2 * HALO, CHUNK), f32),
-            jax.ShapeDtypeStruct((8, CHUNK), f32),
+            jax.ShapeDtypeStruct(records.shape, bf16),
+            jax.ShapeDtypeStruct(dft.shape, bf16),
+            jax.ShapeDtypeStruct(lags.shape, f32),
         ),
         [
             pltpu.VMEM(filter_taps.shape, bf16),
             pltpu.VMEM((1,) + segment_ids.shape, jnp.int32),
             pltpu.VMEM((SLOT, SPAN * CHUNK), f32),
-            pltpu.SemaphoreType.DMA((2,)),
+            pltpu.SemaphoreType.DMA((5,)),
         ],
-        [SMEM] + [VMEM] * 3 + [HBM] * 2,
+        [SMEM] + [VMEM] * 3 + [HBM] * 5,
         compiler_params=pltpu.CompilerParams(vmem_limit_bytes=PREP_LIMIT if few else None),
-    )(index, edge, halo, sown, stay(filter_taps), stay(segment_ids.reshape(1, -1)))
-    tables = (records, dft_table(), lag_tables())
-    own, dft, lags = call(
-        table_kernel,
-        tuple(jax.ShapeDtypeStruct(table.shape, table.dtype) for table in tables),
-        [pltpu.SemaphoreType.DMA((len(tables),))],
-        [HBM] * len(tables),
-        compiler_params=pltpu.CompilerParams(vmem_limit_bytes=TABLE_LIMIT),
-    )(*map(stay, tables))
+    )(
+        index, edge, halo, sown, stay(filter_taps), stay(segment_ids.reshape(1, -1)), stay(records), stay(dft),
+        stay(lags),
+    )
 
     lists = count // 2
+    pair = jnp.concatenate([source, swap(source)], axis=0)
     first = BAND // 2 + 1 if lists <= 8 else 1
-    parts = [ahead(source, 2 * s) for s in range(first, min(8, lists))]
+    parts = [pair] + [ahead(pair, 2 * s) for s in range(first, min(8, lists))]
     have = 8
-    if have < lists:
-        known = jnp.concatenate([source] + parts, axis=0)
     while have < lists:
-        more = []
+        known = jnp.concatenate(parts, axis=0)
         for s in range(1, 8):
             left = lists - s * have
             if left > 0:
-                more.append(ahead(known[: SLOT * left], 2 * s * have))
-        parts += more
-        known = jnp.concatenate([known] + more, axis=0)
-        have = known.shape[0] // SLOT
-    swapped = [swap(part) for part in [source] + parts]
+                parts.append(ahead(known[: 2 * SLOT * left], 2 * s * have))
+        have = min(8 * have, lists)
+    pseg = call(
+        functools.partial(partner_kernel, count), jax.ShapeDtypeStruct((8, CHUNK), f32), (), [SMEM, VMEM],
+        compiler_params=pltpu.CompilerParams(vmem_limit_bytes=TABLE_LIMIT),
+    )(index, segs)
     sfour, stwo = swap(four), swap(two)
 
     group = 8
@@ -365,10 +363,10 @@
             pltpu.VMEM((2, group * CB, ROWS + count), f32),
             pltpu.VMEM((SLOT, SPAN * CHUNK), f32),
         ],
-        [SMEM] + [VMEM] * (13 + 2 * len(parts)),
+        [SMEM] + [VMEM] * (12 + len(parts)),
         compiler_params=pltpu.CompilerParams(vmem_limit_bytes=VMEM_LIMIT if few else None),
     )(
-        index, own, two, four, sown, stwo, sfour, halo, *parts, *swapped, segs, pseg, band, dft, lags,
+        index, own, two, four, sown, stwo, sfour, halo, *parts, segs, pseg, band, dft, lags,
     )
     return (jnp.swapaxes(stacked, 0, 1), source_out)
 

time: 51.5 us -> 44 us (0.85)
  waiting for transfers between devices: 21 us -> 13 us
  starting transfers between devices: 13.2 us -> 14.9 us
  Pallas kernels: 16.3 us -> 15.2 us
    ppermute x7, waiting for transfers between devices: 14.6 us -> 4.2 us  [ahead(): lax.ppermute(value, 'fibre', [(i, (i - distance) % count) for i in range(...]
    ppermute x7, starting transfers between devices: 9.93 us -> 13.7 us  [ahead(): lax.ppermute(value, 'fibre', [(i, (i - distance) % count) for i in range(...]
    ppermute x1, waiting for transfers between devices: 5.01 us -> 8.23 us  [per_device(): halo = lax.ppermute(edge, 'fibre', route)]
    ppermute x1, starting transfers between devices: 2.43 us -> 0.06 us  [per_device(): halo = lax.ppermute(edge, 'fibre', route)]
    pallas_call x1, Pallas kernels: 1.2 us -> 0.11 us  [per_device(): call(functools.partial(partner_kernel, count), jax.ShapeDtypeStruct((8, C...]
    ppermute x9 -> x4, waiting for transfers between devices: 1.47 us -> 0.57 us  [swap(): return lax.ppermute(value, 'fibre', [(i, i ^ 1) for i in range(count)])]
    ppermute x9 -> x4, starting transfers between devices: 0.83 us -> 1.2 us  [swap(): return lax.ppermute(value, 'fibre', [(i, i ^ 1) for i in range(count)])]
  transfers between devices with their start and end apart: 17 -> 12, of which waited for: 7 -> 6; matrix products, arithmetic and copies ran while one was open for 0% -> 0% of each run, Pallas kernels for 7% -> 6%
where the time goes in v4:
time: 44 us; the launch traced here: 43.8 us
  Pallas kernels  15.2 us (35%)
  starting transfers between devices  14.9 us (34%)
  waiting for transfers between devices  13 us (30%)
  between operations  0.69 us (2%)
    ppermute x7, starting transfers between devices, ahead(): lax.ppermute(value, 'fibre', [(i, (i - distance) % count) for i in range(...  13.7 us
    pallas_call x1, Pallas kernels, per_device(): call(functools.partial(main_kernel, len(parts), count), (jax.ShapeDtypeSt...  12.7 us
    ppermute x1, waiting for transfers between devices, per_device(): halo = lax.ppermute(edge, 'fibre', route)  8.23 us
    ppermute x7, waiting for transfers between devices, ahead(): lax.ppermute(value, 'fibre', [(i, (i - distance) % count) for i in range(...  4.2 us
    pallas_call x1, Pallas kernels, per_device(): call(prep_kernel, (jax.ShapeDtypeStruct((SLOT, CHUNK), bf16), jax.ShapeDt...  1.58 us
    ppermute x4, starting transfers between devices, swap(): return lax.ppermute(value, 'fibre', [(i, i ^ 1) for i in range(count)])  1.2 us
  transfers between devices with their start and end apart: 12, of which 6 were waited for; matrix products, arithmetic and copies ran while one was open for 0% of the time, Pallas kernels for 6%

profile of v4, /device:TPU:0, one launch (start us, length us, event | category | flops | bytes accessed | tf_op | source)
XLA Modules:
  0.0 43.8 jit_solution(4490403114368940277)
XLA Ops:
  0.6 0.6 %collective-permute-start.1 = (bf16[64,1600]{1,0:T(8,128)(2,1)}, bf16[64,1600]{1,0:T(8,128)(2,1)S(1)}, u32[]{:S(2)}, u32[]{:S(2)}) collective-permute-start(bf16[64,1600]{1,0:T(8,128)(2,1)} %own_hbm.3), channel_id=1, source_target_pairs={{0,1},{1,0},{2,3},{3,2},{4,5},{5,4},{6,7},{7,6},{8,9},{9,8},{10,11... | collective-permute-start | bytes 614408 | tf_op jit(solution)/shard_map/ppermute | solution.py:289
  1.2 4.7 %collective-permute-start.3 = (bf16[64,1600]{1,0:T(8,128)(2,1)}, bf16[64,1600]{1,0:T(8,128)(2,1)S(1)}, u32[]{:S(2)}, u32[]{:S(2)}) collective-permute-start(bf16[64,1600]{1,0:T(8,128)(2,1)} %own_hbm.3), channel_id=1, source_target_pairs={{0,12},{1,13},{2,14},{3,15},{4,0},{5,1},{6,2},{7,3},{8,4},{9,5},{1... | collective-permute-start | bytes 614408 | tf_op jit(solution)/shard_map/ppermute | solution.py:286
  5.8 1.4 %collective-permute-start.2 = (bf16[64,1600]{1,0:T(8,128)(2,1)}, bf16[64,1600]{1,0:T(8,128)(2,1)S(1)}, u32[]{:S(2)}, u32[]{:S(2)}) collective-permute-start(bf16[64,1600]{1,0:T(8,128)(2,1)} %own_hbm.3), channel_id=1, source_target_pairs={{0,14},{1,15},{2,0},{3,1},{4,2},{5,3},{6,4},{7,5},{8,6},{9,7},{10,... | collective-permute-start | bytes 614408 | tf_op jit(solution)/shard_map/ppermute | solution.py:286
  7.2 0.8 %shard_map.68.edge_ref = bf16[16,1600]{1,0:T(8,128)(2,1)S(1)} custom-call(bf16[64,1600]{1,0:T(8,128)(2,1)} %own_hbm.3), custom_call_target="tpu_custom_call" | custom-call | tf_op jit(solution)/shard_map/pallas_call | solution.py:295
  8.0 0.1 collective-permute-start
  8.1 8.2 %collective-permute-done.halo_ref.refs_7_ = bf16[16,1600]{1,0:T(8,128)(2,1)S(1)} collective-permute-done((bf16[16,1600]{1,0:T(8,128)(2,1)S(1)}, bf16[16,1600]{1,0:T(8,128)(2,1)S(1)}, u32[]{:S(2)}, u32[]{:S(2)}) %collective-permute-start) | collective-permute-done | bytes 51232 | tf_op jit(solution)/shard_map/ppermute | solution.py:303
  16.4 1.6 %shard_map.69 = (bf16[16,128]{1,0:T(8,128)(2,1)S(1)}, bf16[1152,256]{1,0:T(8,128)(2,1)S(1)}, f32[336,128]{1,0:T(8,128)S(1)}, bf16[64,1600]{1,0:T(8,128)(2,1)S(1)...) custom-call(s32[1]{0:T(128)} %bitcast.index_ref.refs_0_, bf16[16,1600]{1,0:T(8,128)(2,1)S(1)} %shard_map.68.edge_ref, ...), custom_call_target="tpu_custom_call" | custom-call | tf_op jit(solution)/shard_map/pallas_call | solution.py:309
  17.9 0.1 collective-permute-start.6
  18.0 0.0 collective-permute-done.3.refs_3_
  18.0 0.5 %collective-permute-start.5 = (bf16[64,1600]{1,0:T(8,128)(2,1)S(1)}, bf16[64,1600]{1,0:T(8,128)(2,1)S(1)}, u32[]{:S(2)}, u32[]{:S(2)}) collective-permute-start(bf16[64,1600]{1,0:T(8,128)(2,1)S(1)} %collective-permute-done.3.refs_3_), channel_id=1, source_target_pairs={{0,1},{1,0},{2,3},{3,2},{4,5},{5,4},{6,7},{7,6},{8,9},{9,8},{10,11... | collective-permute-start | bytes 614408 | tf_op jit(solution)/shard_map/ppermute | solution.py:289
  18.5 0.1 collective-permute-start.4
  18.6 0.6 %collective-permute-done.6 = bf16[16,128]{1,0:T(8,128)(2,1)S(1)} collective-permute-done((bf16[16,128]{1,0:T(8,128)(2,1)S(1)}, bf16[16,128]{1,0:T(8,128)(2,1)S(1)}, u32[]{:S(2)}, u32[]{:S(2)}) %collective-permute-start.6) | collective-permute-done | bytes 4128 | tf_op jit(solution)/shard_map/ppermute | solution.py:289
  19.2 0.8 %collective-permute-start.11 = (bf16[32,128]{1,0:T(8,128)(2,1)S(1)}, bf16[32,128]{1,0:T(8,128)(2,1)S(1)}, u32[]{:S(2)}, u32[]{:S(2)}) collective-permute-start(bf16[32,128]{1,0:T(8,128)(2,1)S(1)} %constant_dynamic-update-slice_fusion.refs_8_), channel_id=1, source_target_pairs={{0,2},{1,3},{2,4},{3,5},{4,6},{5,7},{6,8},{7,9},{8,10},{9,11},{10,... | collective-permute-start | bytes 24584 | tf_op jit(solution)/shard_map/ppermute | solution.py:286
  20.0 1.6 %collective-permute-start.10 = (bf16[32,128]{1,0:T(8,128)(2,1)S(1)}, bf16[32,128]{1,0:T(8,128)(2,1)S(1)}, u32[]{:S(2)}, u32[]{:S(2)}) collective-permute-start(bf16[32,128]{1,0:T(8,128)(2,1)S(1)} %constant_dynamic-update-slice_fusion.refs_8_), channel_id=1, source_target_pairs={{0,4},{1,5},{2,6},{3,7},{4,8},{5,9},{6,10},{7,11},{8,12},{9,13},{1... | collective-permute-start | bytes 24584 | tf_op jit(solution)/shard_map/ppermute | solution.py:286
  21.5 2.0 %collective-permute-start.9 = (bf16[32,128]{1,0:T(8,128)(2,1)S(1)}, bf16[32,128]{1,0:T(8,128)(2,1)S(1)}, u32[]{:S(2)}, u32[]{:S(2)}) collective-permute-start(bf16[32,128]{1,0:T(8,128)(2,1)S(1)} %constant_dynamic-update-slice_fusion.refs_8_), channel_id=1, source_target_pairs={{0,6},{1,7},{2,8},{3,9},{4,10},{5,11},{6,12},{7,13},{8,14},{9,15},... | collective-permute-start | bytes 24584 | tf_op jit(solution)/shard_map/ppermute | solution.py:286
  23.6 2.5 %collective-permute-done.11.refs_13_ = bf16[32,128]{1,0:T(8,128)(2,1)S(1)} collective-permute-done((bf16[32,128]{1,0:T(8,128)(2,1)S(1)}, bf16[32,128]{1,0:T(8,128)(2,1)S(1)}, u32[]{:S(2)}, u32[]{:S(2)}) %collective-permute-start.11) | collective-permute-done | bytes 8224 | tf_op jit(solution)/shard_map/ppermute | solution.py:286
  26.0 0.5 %collective-permute-start.8 = (bf16[32,128]{1,0:T(8,128)(2,1)S(1)}, bf16[32,128]{1,0:T(8,128)(2,1)S(1)}, u32[]{:S(2)}, u32[]{:S(2)}) collective-permute-start(bf16[32,128]{1,0:T(8,128)(2,1)S(1)} %constant_dynamic-update-slice_fusion.refs_8_), channel_id=1, source_target_pairs={{0,8},{1,9},{2,10},{3,11},{4,12},{5,13},{6,14},{7,15},{8,0},{9,1},... | collective-permute-start | bytes 24584 | tf_op jit(solution)/shard_map/ppermute | solution.py:286
  26.5 0.1 collective-permute-done.10.refs_12_
  26.6 2.8 %collective-permute-start.7 = (bf16[32,128]{1,0:T(8,128)(2,1)S(1)}, bf16[32,128]{1,0:T(8,128)(2,1)S(1)}, u32[]{:S(2)}, u32[]{:S(2)}) collective-permute-start(bf16[32,128]{1,0:T(8,128)(2,1)S(1)} %constant_dynamic-update-slice_fusion.refs_8_), channel_id=1, source_target_pairs={{0,10},{1,11},{2,12},{3,13},{4,14},{5,15},{6,0},{7,1},{8,2},{9,3},... | collective-permute-start | bytes 24584 | tf_op jit(solution)/shard_map/ppermute | solution.py:286
  29.3 0.1 shard_map.70.refs_15_
  29.4 1.2 %collective-permute-done.8.refs_10_ = bf16[32,128]{1,0:T(8,128)(2,1)S(1)} collective-permute-done((bf16[32,128]{1,0:T(8,128)(2,1)S(1)}, bf16[32,128]{1,0:T(8,128)(2,1)S(1)}, u32[]{:S(2)}, u32[]{:S(2)}) %collective-permute-start.8) | collective-permute-done | bytes 8224 | tf_op jit(solution)/shard_map/ppermute | solution.py:286
  30.6 0.5 %collective-permute-done.7.refs_9_ = bf16[32,128]{1,0:T(8,128)(2,1)S(1)} collective-permute-done((bf16[32,128]{1,0:T(8,128)(2,1)S(1)}, bf16[32,128]{1,0:T(8,128)(2,1)S(1)}, u32[]{:S(2)}, u32[]{:S(2)}) %collective-permute-start.7) | collective-permute-done | bytes 8224 | tf_op jit(solution)/shard_map/ppermute | solution.py:286
  31.1 0.0 collective-permute-done.5.refs_6_
  31.1 12.7 %shard_map.71 = (bf16[5,64,2048]{2,1,0:T(8,128)(2,1)}, bf16[64,512]{1,0:T(8,128)(2,1)}) custom-call(s32[1]{0:T(128)} %bitcast.index_ref.refs_0_, bf16[64,1600]{1,0:T(8,128)(2,1)S(1)} %get-tuple-element.10.refs_1_, bf16[64,1600]{1,0:T(8,128)(2,1)S(1)} %collective-permute-done.2.refs_2_, bf16[64,1600]{1,0:T(8,128)(2,1)S(1)} %collective-permute-done.3.refs_3_, ...), custom_call_target="tpu_custom_call" | custom-call | tf_op jit(solution)/shard_map/pallas_call | solution.py:351
  (6 shorter events, 0.0 us)
Async XLA Ops:
  0.6 15.7 %collective-permute-start.1 = (bf16[64,1600]{1,0:T(8,128)(2,1)}, bf16[64,1600]{1,0:T(8,128)(2,1)S(1)}, u32[]{:S(2)}, u32[]{:S(2)}) collective-permute-start(bf16[64,1600]{1,0:T(8,128)(2,1)} %own_hbm.3), channel_id=1, source_target_pairs={{0,1},{1,0},{2,3},{3,2},{4,5},{5,4},{6,7},{7,6},{8,9},{9,8},{10,11... | collective-permute-start | bytes 614408 | tf_op jit(solution)/shard_map/ppermute | solution.py:289
  1.2 16.8 %collective-permute-start.3 = (bf16[64,1600]{1,0:T(8,128)(2,1)}, bf16[64,1600]{1,0:T(8,128)(2,1)S(1)}, u32[]{:S(2)}, u32[]{:S(2)}) collective-permute-start(bf16[64,1600]{1,0:T(8,128)(2,1)} %own_hbm.3), channel_id=1, source_target_pairs={{0,12},{1,13},{2,14},{3,15},{4,0},{5,1},{6,2},{7,3},{8,4},{9,5},{1... | collective-permute-start | bytes 614408 | tf_op jit(solution)/shard_map/ppermute | solution.py:286
  5.8 12.7 %collective-permute-start.2 = (bf16[64,1600]{1,0:T(8,128)(2,1)}, bf16[64,1600]{1,0:T(8,128)(2,1)S(1)}, u32[]{:S(2)}, u32[]{:S(2)}) collective-permute-start(bf16[64,1600]{1,0:T(8,128)(2,1)} %own_hbm.3), channel_id=1, source_target_pairs={{0,14},{1,15},{2,0},{3,1},{4,2},{5,3},{6,4},{7,5},{8,6},{9,7},{10,... | collective-permute-start | bytes 614408 | tf_op jit(solution)/shard_map/ppermute | solution.py:286
  8.0 8.3 %collective-permute-start = (bf16[16,1600]{1,0:T(8,128)(2,1)S(1)}, bf16[16,1600]{1,0:T(8,128)(2,1)S(1)}, u32[]{:S(2)}, u32[]{:S(2)}) collective-permute-start(bf16[16,1600]{1,0:T(8,128)(2,1)S(1)} %shard_map.68.edge_ref), channel_id=1, source_target_pairs={{0,11},{1,2},{2,13},{3,4},{4,15},{5,6},{6,1},{7,8},{8,3},{9,10},{1... | collective-permute-start | bytes 153608 | tf_op jit(solution)/shard_map/ppermute | solution.py:303
  17.9 1.2 %collective-permute-start.6 = (bf16[16,128]{1,0:T(8,128)(2,1)S(1)}, bf16[16,128]{1,0:T(8,128)(2,1)S(1)}, u32[]{:S(2)}, u32[]{:S(2)}) collective-permute-start(bf16[16,128]{1,0:T(8,128)(2,1)S(1)} %get-tuple-element.11), channel_id=1, source_target_pairs={{0,1},{1,0},{2,3},{3,2},{4,5},{5,4},{6,7},{7,6},{8,9},{9,8},{10,11... | collective-permute-start | bytes 12296 | tf_op jit(solution)/shard_map/ppermute | solution.py:289
  18.0 13.1 %collective-permute-start.5 = (bf16[64,1600]{1,0:T(8,128)(2,1)S(1)}, bf16[64,1600]{1,0:T(8,128)(2,1)S(1)}, u32[]{:S(2)}, u32[]{:S(2)}) collective-permute-start(bf16[64,1600]{1,0:T(8,128)(2,1)S(1)} %collective-permute-done.3.refs_3_), channel_id=1, source_target_pairs={{0,1},{1,0},{2,3},{3,2},{4,5},{5,4},{6,7},{7,6},{8,9},{9,8},{10,11... | collective-permute-start | bytes 614408 | tf_op jit(solution)/shard_map/ppermute | solution.py:289
  18.5 12.6 %collective-permute-start.4 = (bf16[64,1600]{1,0:T(8,128)(2,1)S(1)}, bf16[64,1600]{1,0:T(8,128)(2,1)S(1)}, u32[]{:S(2)}, u32[]{:S(2)}) collective-permute-start(bf16[64,1600]{1,0:T(8,128)(2,1)S(1)} %collective-permute-done.2.refs_2_), channel_id=1, source_target_pairs={{0,1},{1,0},{2,3},{3,2},{4,5},{5,4},{6,7},{7,6},{8,9},{9,8},{10,11... | collective-permute-start | bytes 614408 | tf_op jit(solution)/shard_map/ppermute | solution.py:289
  19.2 6.8 %collective-permute-start.11 = (bf16[32,128]{1,0:T(8,128)(2,1)S(1)}, bf16[32,128]{1,0:T(8,128)(2,1)S(1)}, u32[]{:S(2)}, u32[]{:S(2)}) collective-permute-start(bf16[32,128]{1,0:T(8,128)(2,1)S(1)} %constant_dynamic-update-slice_fusion.refs_8_), channel_id=1, source_target_pairs={{0,2},{1,3},{2,4},{3,5},{4,6},{5,7},{6,8},{7,9},{8,10},{9,11},{10,... | collective-permute-start | bytes 24584 | tf_op jit(solution)/shard_map/ppermute | solution.py:286
  20.0 6.6 %collective-permute-start.10 = (bf16[32,128]{1,0:T(8,128)(2,1)S(1)}, bf16[32,128]{1,0:T(8,128)(2,1)S(1)}, u32[]{:S(2)}, u32[]{:S(2)}) collective-permute-start(bf16[32,128]{1,0:T(8,128)(2,1)S(1)} %constant_dynamic-update-slice_fusion.refs_8_), channel_id=1, source_target_pairs={{0,4},{1,5},{2,6},{3,7},{4,8},{5,9},{6,10},{7,11},{8,12},{9,13},{1... | collective-permute-start | bytes 24584 | tf_op jit(solution)/shard_map/ppermute | solution.py:286
  21.5 7.9 %collective-permute-start.9 = (bf16[32,128]{1,0:T(8,128)(2,1)S(1)}, bf16[32,128]{1,0:T(8,128)(2,1)S(1)}, u32[]{:S(2)}, u32[]{:S(2)}) collective-permute-start(bf16[32,128]{1,0:T(8,128)(2,1)S(1)} %constant_dynamic-update-slice_fusion.refs_8_), channel_id=1, source_target_pairs={{0,6},{1,7},{2,8},{3,9},{4,10},{5,11},{6,12},{7,13},{8,14},{9,15},... | collective-permute-start | bytes 24584 | tf_op jit(solution)/shard_map/ppermute | solution.py:286
  26.0 4.6 %collective-permute-start.8 = (bf16[32,128]{1,0:T(8,128)(2,1)S(1)}, bf16[32,128]{1,0:T(8,128)(2,1)S(1)}, u32[]{:S(2)}, u32[]{:S(2)}) collective-permute-start(bf16[32,128]{1,0:T(8,128)(2,1)S(1)} %constant_dynamic-update-slice_fusion.refs_8_), channel_id=1, source_target_pairs={{0,8},{1,9},{2,10},{3,11},{4,12},{5,13},{6,14},{7,15},{8,0},{9,1},... | collective-permute-start | bytes 24584 | tf_op jit(solution)/shard_map/ppermute | solution.py:286
  26.6 4.5 %collective-permute-start.7 = (bf16[32,128]{1,0:T(8,128)(2,1)S(1)}, bf16[32,128]{1,0:T(8,128)(2,1)S(1)}, u32[]{:S(2)}, u32[]{:S(2)}) collective-permute-start(bf16[32,128]{1,0:T(8,128)(2,1)S(1)} %constant_dynamic-update-slice_fusion.refs_8_), channel_id=1, source_target_pairs={{0,10},{1,11},{2,12},{3,13},{4,14},{5,15},{6,0},{7,1},{8,2},{9,3},... | collective-permute-start | bytes 24584 | tf_op jit(solution)/shard_map/ppermute | solution.py:286

commit v5 on v4

--- a/solution.py
+++ b/solution.py
@@ -22,8 +22,7 @@
 HALO = 8
 CHUNK = 128
 NCHUNK = -(-W * L // CHUNK)
-FP = 256
-KP = W * 2 * FP
+KP = -(-W * L // CHUNK) * CHUNK
 ROWS = (BAND + 1) * CB
 SHIFT = L % CHUNK
 COVER = 4 * CHUNK
@@ -37,24 +36,25 @@
 bf16 = jnp.bfloat16
 
 
-def dft_table():
+def dft_tables():
     t = np.arange(L)
     taper = 0.5 - 0.5 * np.cos((t + 0.5) * (2.0 * np.pi / L))
     phase = (t[:, None] * np.arange(F)[None, :] % L) * (2.0 * np.pi / L)
-    lead = (W - 1) * SHIFT
-    table = np.zeros((lead + COVER, 2 * FP))
-    table[lead : lead + L, :F] = taper[:, None] * np.cos(phase)
-    table[lead : lead + L, FP : FP + F] = -taper[:, None] * np.sin(phase)
-    return jnp.asarray(table.astype(np.float32), bf16)
+    table = np.concatenate([taper[:, None] * np.cos(phase), -taper[:, None] * np.sin(phase)], axis=1)
+    tables = np.zeros((W, COVER, COVER))
+    for w in range(W):
+        tables[w, w * SHIFT : w * SHIFT + L, w * SHIFT : w * SHIFT + L] = table
+    return jnp.asarray(tables.astype(np.float32), bf16)
 
 
 def lag_tables():
     m = np.arange(LAGS) - LAGS // 2
     phase = (m[:, None] * np.arange(F)[None, :] % L) * (2.0 * np.pi / L)
     scale = 1.0 / np.sqrt(2.0 * L)
-    tables = np.zeros((2, LAGS, FP))
-    tables[0, :, :F] = np.cos(phase) * scale
-    tables[1, :, :F] = -np.sin(phase) * scale
+    straight, crossed = np.cos(phase) * scale, -np.sin(phase) * scale
+    tables = np.zeros((2, LAGS, KP))
+    tables[0, :, : W * L] = np.tile(np.concatenate([straight, straight], axis=1), (1, W))
+    tables[1, :, : W * L] = np.tile(np.concatenate([crossed, -crossed], axis=1), (1, W))
     return jnp.asarray(tables.astype(np.float32), bf16).astype(f32)
 
 
@@ -142,7 +142,7 @@
     index_ref, own_ref, two_ref, four_ref, sown_ref, stwo_ref, sfour_ref, halo_ref = refs[:8]
     part_refs, refs = refs[8 : 8 + pieces], refs[8 + pieces :]
     seg_ref, pseg_ref, band_ref, dft_ref, lag_ref, out_ref, src_ref = refs[:7]
-    rec, masked, filt, spec, turned, totals, line = refs[7:]
+    rec, masked, filt, spec, turned, totals, line, swapped = refs[7:]
     even = index_ref[0] % 2 == 0
 
     def put(start, rows):
@@ -173,10 +173,10 @@
         centre = seg_ref[pl.ds(base + HALO, CB), :]
         for e in range(SPAN):
             first = base + (HALO - HALF + e)
-            keep = seg_ref[pl.ds(first, CB), :] == centre
+            keep = jnp.where(seg_ref[pl.ds(first, CB), :] == centre, 1.0, 0.0)
             for j in range(NCHUNK):
                 rows = rec[j, pl.ds(first, CB), :]
-                held[j * CB : (j + 1) * CB, e * CHUNK : (e + 1) * CHUNK] = jnp.where(keep, rows, 0.0).astype(bf16)
+                held[j * CB : (j + 1) * CB, e * CHUNK : (e + 1) * CHUNK] = (rows * keep).astype(bf16)
         filtered(held, CB, base)
 
     rows = []
@@ -206,13 +206,18 @@
         for j in range(NCHUNK):
             filt[j, ROWS + r : ROWS + r + 1, :] = rows[j]
 
+    tiles = COVER // CHUNK - 1
+    tail = None
     for w in range(W):
-        first = w * (L // CHUNK)
-        lhs = jnp.concatenate([filt[first + q] for q in range(COVER // CHUNK)], axis=1)
-        lead = (W - 1 - w) * SHIFT
-        raw = jnp.dot(lhs, dft_ref[lead : lead + COVER, :], preferred_element_type=f32)
+        lhs = jnp.concatenate([filt[w * tiles + q] for q in range(tiles + 1)], axis=1)
+        raw = jnp.dot(lhs, dft_ref[w], preferred_element_type=f32)
         power = jnp.sum(raw * raw, axis=-1, keepdims=True) * (1.0 / L)
-        spec[:, w * 2 * FP : (w + 1) * 2 * FP] = (raw * lax.rsqrt(power + 1e-06)).astype(bf16)
+        whitened = raw * lax.rsqrt(power + 1e-06)
+        head = whitened[:, :CHUNK] if tail is None else tail + whitened[:, :CHUNK]
+        spec[:, w * tiles * CHUNK : (w * tiles + 1) * CHUNK] = head.astype(bf16)
+        spec[:, (w * tiles + 1) * CHUNK : (w + 1) * tiles * CHUNK] = whitened[:, CHUNK : tiles * CHUNK].astype(bf16)
+        tail = whitened[:, tiles * CHUNK :]
+    spec[:, W * tiles * CHUNK :] = tail.astype(bf16)
 
     row = lax.broadcasted_iota(jnp.int32, (count, count), 0)
     column = lax.broadcasted_iota(jnp.int32, (count, count), 1)
@@ -221,22 +226,26 @@
     order = jnp.where(ahead == column, 1.0, 0.0).astype(bf16)
     spec[ROWS:, :] = jnp.dot(order, spec[ROWS:, :], preferred_element_type=f32).astype(bf16)
 
+    own = spec[:CB, :].astype(f32)
+    pieces = []
+    for w in range(W):
+        pieces += [own[:, w * L + F : (w + 1) * L], own[:, w * L : w * L + F]]
+    swapped[...] = jnp.concatenate(pieces + [jnp.zeros((CB, KP - W * L), f32)], axis=1)
+
     group = turned.shape[0] // CB
     steps = LAGS // group
     own_seg = seg_ref[HALO : HALO + CB, :]
 
     def multiply(step, slot):
         start = pl.multiple_of(step * group, group)
-        cosines = lag_ref[0, pl.ds(start, group), :]
-        sines = lag_ref[1, pl.ds(start, group), :]
-        for w in range(W):
-            re_at, im_at = w * 2 * FP, w * 2 * FP + FP
-            re = spec[:CB, re_at : re_at + FP].astype(f32)
-            im = spec[:CB, im_at : im_at + FP].astype(f32)
+        for at in range(0, KP, CHUNK):
+            lanes = slice(at, at + CHUNK)
+            straight, crossed = lag_ref[0, pl.ds(start, group), lanes], lag_ref[1, pl.ds(start, group), lanes]
+            own, other = spec[:CB, lanes].astype(f32), swapped[:, lanes]
             for g in range(group):
-                c, s = cosines[g : g + 1, :], sines[g : g + 1, :]
-                turned[g * CB : (g + 1) * CB, re_at : re_at + FP] = (re * c + im * s).astype(bf16)
-                turned[g * CB : (g + 1) * CB, im_at : im_at + FP] = (im * c - re * s).astype(bf16)
+                turned[g * CB : (g + 1) * CB, lanes] = (
+                    own * straight[g : g + 1, :] + other * crossed[g : g + 1, :]
+                ).astype(bf16)
         totals[slot] = lax.dot_general(
             turned[...], spec[...], (((1,), (1,)), ((), ())), preferred_element_type=f32
         )
@@ -305,7 +314,7 @@
     four = ahead(records, 4)
     two = ahead(records, 2)
 
-    dft, lags = dft_table(), lag_tables()
+    dft, lags = dft_tables(), lag_tables()
     source, band, segs, own, dft, lags = call(
         prep_kernel,
         (
@@ -362,6 +371,7 @@
             pltpu.VMEM((group * CB, KP), bf16),
             pltpu.VMEM((2, group * CB, ROWS + count), f32),
             pltpu.VMEM((SLOT, SPAN * CHUNK), f32),
+            pltpu.VMEM((CB, KP), f32),
         ],
         [SMEM] + [VMEM] * (12 + len(parts)),
         compiler_params=pltpu.CompilerParams(vmem_limit_bytes=VMEM_LIMIT if few else None),

time: 44 us -> 43.6 us (level)
    pallas_call x1, Pallas kernels: 12.7 us -> 12 us  [per_device(): call(functools.partial(main_kernel, len(parts), count), (jax.ShapeDtypeSt...]
where the time goes in v5:
time: 43.6 us; the launch traced here: 43.4 us
  starting transfers between devices  14.9 us (34%)
  Pallas kernels  14.8 us (34%)
  waiting for transfers between devices  13 us (30%)
  between operations  0.69 us (2%)
    ppermute x7, starting transfers between devices, ahead(): lax.ppermute(value, 'fibre', [(i, (i - distance) % count) for i in range(...  13.7 us
    pallas_call x1, Pallas kernels, per_device(): call(functools.partial(main_kernel, len(parts), count), (jax.ShapeDtypeSt...  12 us
    ppermute x1, waiting for transfers between devices, per_device(): halo = lax.ppermute(edge, 'fibre', route)  8.23 us
    ppermute x7, waiting for transfers between devices, ahead(): lax.ppermute(value, 'fibre', [(i, (i - distance) % count) for i in range(...  4.2 us
    pallas_call x1, Pallas kernels, per_device(): call(prep_kernel, (jax.ShapeDtypeStruct((SLOT, CHUNK), bf16), jax.ShapeDt...  1.82 us
    ppermute x4, starting transfers between devices, swap(): return lax.ppermute(value, 'fibre', [(i, i ^ 1) for i in range(count)])  1.2 us
  transfers between devices with their start and end apart: 12, of which 6 were waited for; matrix products, arithmetic and copies ran while one was open for 0% of the time, Pallas kernels for 6%

profile of v5, /device:TPU:0, one launch (start us, length us, event | category | flops | bytes accessed | tf_op | source)
XLA Modules:
  0.0 43.4 jit_solution(2194514426483051113)
XLA Ops:
  0.6 0.6 %collective-permute-start.1 = (bf16[64,1600]{1,0:T(8,128)(2,1)}, bf16[64,1600]{1,0:T(8,128)(2,1)S(1)}, u32[]{:S(2)}, u32[]{:S(2)}) collective-permute-start(bf16[64,1600]{1,0:T(8,128)(2,1)} %own_hbm.3), channel_id=1, source_target_pairs={{0,1},{1,0},{2,3},{3,2},{4,5},{5,4},{6,7},{7,6},{8,9},{9,8},{10,11... | collective-permute-start | bytes 614408 | tf_op jit(solution)/shard_map/ppermute | solution.py:298
  1.2 4.7 %collective-permute-start.3 = (bf16[64,1600]{1,0:T(8,128)(2,1)}, bf16[64,1600]{1,0:T(8,128)(2,1)S(1)}, u32[]{:S(2)}, u32[]{:S(2)}) collective-permute-start(bf16[64,1600]{1,0:T(8,128)(2,1)} %own_hbm.3), channel_id=1, source_target_pairs={{0,12},{1,13},{2,14},{3,15},{4,0},{5,1},{6,2},{7,3},{8,4},{9,5},{1... | collective-permute-start | bytes 614408 | tf_op jit(solution)/shard_map/ppermute | solution.py:295
  5.8 1.4 %collective-permute-start.2 = (bf16[64,1600]{1,0:T(8,128)(2,1)}, bf16[64,1600]{1,0:T(8,128)(2,1)S(1)}, u32[]{:S(2)}, u32[]{:S(2)}) collective-permute-start(bf16[64,1600]{1,0:T(8,128)(2,1)} %own_hbm.3), channel_id=1, source_target_pairs={{0,14},{1,15},{2,0},{3,1},{4,2},{5,3},{6,4},{7,5},{8,6},{9,7},{10,... | collective-permute-start | bytes 614408 | tf_op jit(solution)/shard_map/ppermute | solution.py:295
  7.2 0.8 %shard_map.68.edge_ref = bf16[16,1600]{1,0:T(8,128)(2,1)S(1)} custom-call(bf16[64,1600]{1,0:T(8,128)(2,1)} %own_hbm.3), custom_call_target="tpu_custom_call" | custom-call | tf_op jit(solution)/shard_map/pallas_call | solution.py:304
  8.0 0.1 collective-permute-start
  8.1 8.2 %collective-permute-done.halo_ref.refs_7_ = bf16[16,1600]{1,0:T(8,128)(2,1)S(1)} collective-permute-done((bf16[16,1600]{1,0:T(8,128)(2,1)S(1)}, bf16[16,1600]{1,0:T(8,128)(2,1)S(1)}, u32[]{:S(2)}, u32[]{:S(2)}) %collective-permute-start) | collective-permute-done | bytes 51232 | tf_op jit(solution)/shard_map/ppermute | solution.py:312
  16.3 0.0 collective-permute-done.1.sown_ref.refs_4_
  16.4 1.8 %shard_map.69 = (bf16[16,128]{1,0:T(8,128)(2,1)S(1)}, bf16[1152,256]{1,0:T(8,128)(2,1)S(1)}, f32[336,128]{1,0:T(8,128)S(1)}, bf16[64,1600]{1,0:T(8,128)(2,1)S(1)...) custom-call(s32[1]{0:T(128)} %bitcast.index_ref.refs_0_, bf16[16,1600]{1,0:T(8,128)(2,1)S(1)} %shard_map.68.edge_ref, ...), custom_call_target="tpu_custom_call" | custom-call | tf_op jit(solution)/shard_map/pallas_call | solution.py:318
  18.2 0.1 collective-permute-start.6
  18.3 0.5 %collective-permute-start.5 = (bf16[64,1600]{1,0:T(8,128)(2,1)S(1)}, bf16[64,1600]{1,0:T(8,128)(2,1)S(1)}, u32[]{:S(2)}, u32[]{:S(2)}) collective-permute-start(bf16[64,1600]{1,0:T(8,128)(2,1)S(1)} %collective-permute-done.3.refs_3_), channel_id=1, source_target_pairs={{0,1},{1,0},{2,3},{3,2},{4,5},{5,4},{6,7},{7,6},{8,9},{9,8},{10,11... | collective-permute-start | bytes 614408 | tf_op jit(solution)/shard_map/ppermute | solution.py:298
  18.8 0.0 collective-permute-done.2.refs_2_
  18.8 0.1 collective-permute-start.4
  18.9 0.6 %collective-permute-done.6 = bf16[16,128]{1,0:T(8,128)(2,1)S(1)} collective-permute-done((bf16[16,128]{1,0:T(8,128)(2,1)S(1)}, bf16[16,128]{1,0:T(8,128)(2,1)S(1)}, u32[]{:S(2)}, u32[]{:S(2)}) %collective-permute-start.6) | collective-permute-done | bytes 4128 | tf_op jit(solution)/shard_map/ppermute | solution.py:298
  19.4 0.8 %collective-permute-start.11 = (bf16[32,128]{1,0:T(8,128)(2,1)S(1)}, bf16[32,128]{1,0:T(8,128)(2,1)S(1)}, u32[]{:S(2)}, u32[]{:S(2)}) collective-permute-start(bf16[32,128]{1,0:T(8,128)(2,1)S(1)} %constant_dynamic-update-slice_fusion.refs_8_), channel_id=1, source_target_pairs={{0,2},{1,3},{2,4},{3,5},{4,6},{5,7},{6,8},{7,9},{8,10},{9,11},{10,... | collective-permute-start | bytes 24584 | tf_op jit(solution)/shard_map/ppermute | solution.py:295
  20.2 1.6 %collective-permute-start.10 = (bf16[32,128]{1,0:T(8,128)(2,1)S(1)}, bf16[32,128]{1,0:T(8,128)(2,1)S(1)}, u32[]{:S(2)}, u32[]{:S(2)}) collective-permute-start(bf16[32,128]{1,0:T(8,128)(2,1)S(1)} %constant_dynamic-update-slice_fusion.refs_8_), channel_id=1, source_target_pairs={{0,4},{1,5},{2,6},{3,7},{4,8},{5,9},{6,10},{7,11},{8,12},{9,13},{1... | collective-permute-start | bytes 24584 | tf_op jit(solution)/shard_map/ppermute | solution.py:295
  21.8 2.0 %collective-permute-start.9 = (bf16[32,128]{1,0:T(8,128)(2,1)S(1)}, bf16[32,128]{1,0:T(8,128)(2,1)S(1)}, u32[]{:S(2)}, u32[]{:S(2)}) collective-permute-start(bf16[32,128]{1,0:T(8,128)(2,1)S(1)} %constant_dynamic-update-slice_fusion.refs_8_), channel_id=1, source_target_pairs={{0,6},{1,7},{2,8},{3,9},{4,10},{5,11},{6,12},{7,13},{8,14},{9,15},... | collective-permute-start | bytes 24584 | tf_op jit(solution)/shard_map/ppermute | solution.py:295
  23.8 2.5 %collective-permute-done.11.refs_13_ = bf16[32,128]{1,0:T(8,128)(2,1)S(1)} collective-permute-done((bf16[32,128]{1,0:T(8,128)(2,1)S(1)}, bf16[32,128]{1,0:T(8,128)(2,1)S(1)}, u32[]{:S(2)}, u32[]{:S(2)}) %collective-permute-start.11) | collective-permute-done | bytes 8224 | tf_op jit(solution)/shard_map/ppermute | solution.py:295
  26.3 0.5 %collective-permute-start.8 = (bf16[32,128]{1,0:T(8,128)(2,1)S(1)}, bf16[32,128]{1,0:T(8,128)(2,1)S(1)}, u32[]{:S(2)}, u32[]{:S(2)}) collective-permute-start(bf16[32,128]{1,0:T(8,128)(2,1)S(1)} %constant_dynamic-update-slice_fusion.refs_8_), channel_id=1, source_target_pairs={{0,8},{1,9},{2,10},{3,11},{4,12},{5,13},{6,14},{7,15},{8,0},{9,1},... | collective-permute-start | bytes 24584 | tf_op jit(solution)/shard_map/ppermute | solution.py:295
  26.7 0.1 collective-permute-done.10.refs_12_
  26.8 2.8 %collective-permute-start.7 = (bf16[32,128]{1,0:T(8,128)(2,1)S(1)}, bf16[32,128]{1,0:T(8,128)(2,1)S(1)}, u32[]{:S(2)}, u32[]{:S(2)}) collective-permute-start(bf16[32,128]{1,0:T(8,128)(2,1)S(1)} %constant_dynamic-update-slice_fusion.refs_8_), channel_id=1, source_target_pairs={{0,10},{1,11},{2,12},{3,13},{4,14},{5,15},{6,0},{7,1},{8,2},{9,3},... | collective-permute-start | bytes 24584 | tf_op jit(solution)/shard_map/ppermute | solution.py:295
  29.6 0.1 shard_map.70.refs_15_
  29.7 1.2 %collective-permute-done.8.refs_10_ = bf16[32,128]{1,0:T(8,128)(2,1)S(1)} collective-permute-done((bf16[32,128]{1,0:T(8,128)(2,1)S(1)}, bf16[32,128]{1,0:T(8,128)(2,1)S(1)}, u32[]{:S(2)}, u32[]{:S(2)}) %collective-permute-start.8) | collective-permute-done | bytes 8224 | tf_op jit(solution)/shard_map/ppermute | solution.py:295
  30.8 0.5 %collective-permute-done.7.refs_9_ = bf16[32,128]{1,0:T(8,128)(2,1)S(1)} collective-permute-done((bf16[32,128]{1,0:T(8,128)(2,1)S(1)}, bf16[32,128]{1,0:T(8,128)(2,1)S(1)}, u32[]{:S(2)}, u32[]{:S(2)}) %collective-permute-start.7) | collective-permute-done | bytes 8224 | tf_op jit(solution)/shard_map/ppermute | solution.py:295
  31.4 12.0 %shard_map.71 = (bf16[5,64,2048]{2,1,0:T(8,128)(2,1)}, bf16[64,512]{1,0:T(8,128)(2,1)}) custom-call(s32[1]{0:T(128)} %bitcast.index_ref.refs_0_, bf16[64,1600]{1,0:T(8,128)(2,1)S(1)} %get-tuple-element.10.refs_1_, bf16[64,1600]{1,0:T(8,128)(2,1)S(1)} %collective-permute-done.2.refs_2_, bf16[64,1600]{1,0:T(8,128)(2,1)S(1)} %collective-permute-done.3.refs_3_, ...), custom_call_target="tpu_custom_call" | custom-call | tf_op jit(solution)/shard_map/pallas_call | solution.py:360
  (6 shorter events, 0.0 us)
Async XLA Ops:
  0.6 15.7 %collective-permute-start.1 = (bf16[64,1600]{1,0:T(8,128)(2,1)}, bf16[64,1600]{1,0:T(8,128)(2,1)S(1)}, u32[]{:S(2)}, u32[]{:S(2)}) collective-permute-start(bf16[64,1600]{1,0:T(8,128)(2,1)} %own_hbm.3), channel_id=1, source_target_pairs={{0,1},{1,0},{2,3},{3,2},{4,5},{5,4},{6,7},{7,6},{8,9},{9,8},{10,11... | collective-permute-start | bytes 614408 | tf_op jit(solution)/shard_map/ppermute | solution.py:298
  1.2 17.1 %collective-permute-start.3 = (bf16[64,1600]{1,0:T(8,128)(2,1)}, bf16[64,1600]{1,0:T(8,128)(2,1)S(1)}, u32[]{:S(2)}, u32[]{:S(2)}) collective-permute-start(bf16[64,1600]{1,0:T(8,128)(2,1)} %own_hbm.3), channel_id=1, source_target_pairs={{0,12},{1,13},{2,14},{3,15},{4,0},{5,1},{6,2},{7,3},{8,4},{9,5},{1... | collective-permute-start | bytes 614408 | tf_op jit(solution)/shard_map/ppermute | solution.py:295
  5.8 12.9 %collective-permute-start.2 = (bf16[64,1600]{1,0:T(8,128)(2,1)}, bf16[64,1600]{1,0:T(8,128)(2,1)S(1)}, u32[]{:S(2)}, u32[]{:S(2)}) collective-permute-start(bf16[64,1600]{1,0:T(8,128)(2,1)} %own_hbm.3), channel_id=1, source_target_pairs={{0,14},{1,15},{2,0},{3,1},{4,2},{5,3},{6,4},{7,5},{8,6},{9,7},{10,... | collective-permute-start | bytes 614408 | tf_op jit(solution)/shard_map/ppermute | solution.py:295
  8.0 8.3 %collective-permute-start = (bf16[16,1600]{1,0:T(8,128)(2,1)S(1)}, bf16[16,1600]{1,0:T(8,128)(2,1)S(1)}, u32[]{:S(2)}, u32[]{:S(2)}) collective-permute-start(bf16[16,1600]{1,0:T(8,128)(2,1)S(1)} %shard_map.68.edge_ref), channel_id=1, source_target_pairs={{0,11},{1,2},{2,13},{3,4},{4,15},{5,6},{6,1},{7,8},{8,3},{9,10},{1... | collective-permute-start | bytes 153608 | tf_op jit(solution)/shard_map/ppermute | solution.py:312
  18.2 1.2 %collective-permute-start.6 = (bf16[16,128]{1,0:T(8,128)(2,1)S(1)}, bf16[16,128]{1,0:T(8,128)(2,1)S(1)}, u32[]{:S(2)}, u32[]{:S(2)}) collective-permute-start(bf16[16,128]{1,0:T(8,128)(2,1)S(1)} %get-tuple-element.11), channel_id=1, source_target_pairs={{0,1},{1,0},{2,3},{3,2},{4,5},{5,4},{6,7},{7,6},{8,9},{9,8},{10,11... | collective-permute-start | bytes 12296 | tf_op jit(solution)/shard_map/ppermute | solution.py:298
  18.3 13.1 %collective-permute-start.5 = (bf16[64,1600]{1,0:T(8,128)(2,1)S(1)}, bf16[64,1600]{1,0:T(8,128)(2,1)S(1)}, u32[]{:S(2)}, u32[]{:S(2)}) collective-permute-start(bf16[64,1600]{1,0:T(8,128)(2,1)S(1)} %collective-permute-done.3.refs_3_), channel_id=1, source_target_pairs={{0,1},{1,0},{2,3},{3,2},{4,5},{5,4},{6,7},{7,6},{8,9},{9,8},{10,11... | collective-permute-start | bytes 614408 | tf_op jit(solution)/shard_map/ppermute | solution.py:298
  18.8 12.6 %collective-permute-start.4 = (bf16[64,1600]{1,0:T(8,128)(2,1)S(1)}, bf16[64,1600]{1,0:T(8,128)(2,1)S(1)}, u32[]{:S(2)}, u32[]{:S(2)}) collective-permute-start(bf16[64,1600]{1,0:T(8,128)(2,1)S(1)} %collective-permute-done.2.refs_2_), channel_id=1, source_target_pairs={{0,1},{1,0},{2,3},{3,2},{4,5},{5,4},{6,7},{7,6},{8,9},{9,8},{10,11... | collective-permute-start | bytes 614408 | tf_op jit(solution)/shard_map/ppermute | solution.py:298
  19.4 6.8 %collective-permute-start.11 = (bf16[32,128]{1,0:T(8,128)(2,1)S(1)}, bf16[32,128]{1,0:T(8,128)(2,1)S(1)}, u32[]{:S(2)}, u32[]{:S(2)}) collective-permute-start(bf16[32,128]{1,0:T(8,128)(2,1)S(1)} %constant_dynamic-update-slice_fusion.refs_8_), channel_id=1, source_target_pairs={{0,2},{1,3},{2,4},{3,5},{4,6},{5,7},{6,8},{7,9},{8,10},{9,11},{10,... | collective-permute-start | bytes 24584 | tf_op jit(solution)/shard_map/ppermute | solution.py:295
  20.2 6.6 %collective-permute-start.10 = (bf16[32,128]{1,0:T(8,128)(2,1)S(1)}, bf16[32,128]{1,0:T(8,128)(2,1)S(1)}, u32[]{:S(2)}, u32[]{:S(2)}) collective-permute-start(bf16[32,128]{1,0:T(8,128)(2,1)S(1)} %constant_dynamic-update-slice_fusion.refs_8_), channel_id=1, source_target_pairs={{0,4},{1,5},{2,6},{3,7},{4,8},{5,9},{6,10},{7,11},{8,12},{9,13},{1... | collective-permute-start | bytes 24584 | tf_op jit(solution)/shard_map/ppermute | solution.py:295
  21.8 7.9 %collective-permute-start.9 = (bf16[32,128]{1,0:T(8,128)(2,1)S(1)}, bf16[32,128]{1,0:T(8,128)(2,1)S(1)}, u32[]{:S(2)}, u32[]{:S(2)}) collective-permute-start(bf16[32,128]{1,0:T(8,128)(2,1)S(1)} %constant_dynamic-update-slice_fusion.refs_8_), channel_id=1, source_target_pairs={{0,6},{1,7},{2,8},{3,9},{4,10},{5,11},{6,12},{7,13},{8,14},{9,15},... | collective-permute-start | bytes 24584 | tf_op jit(solution)/shard_map/ppermute | solution.py:295
  26.3 4.6 %collective-permute-start.8 = (bf16[32,128]{1,0:T(8,128)(2,1)S(1)}, bf16[32,128]{1,0:T(8,128)(2,1)S(1)}, u32[]{:S(2)}, u32[]{:S(2)}) collective-permute-start(bf16[32,128]{1,0:T(8,128)(2,1)S(1)} %constant_dynamic-update-slice_fusion.refs_8_), channel_id=1, source_target_pairs={{0,8},{1,9},{2,10},{3,11},{4,12},{5,13},{6,14},{7,15},{8,0},{9,1},... | collective-permute-start | bytes 24584 | tf_op jit(solution)/shard_map/ppermute | solution.py:295
  26.8 4.5 %collective-permute-start.7 = (bf16[32,128]{1,0:T(8,128)(2,1)S(1)}, bf16[32,128]{1,0:T(8,128)(2,1)S(1)}, u32[]{:S(2)}, u32[]{:S(2)}) collective-permute-start(bf16[32,128]{1,0:T(8,128)(2,1)S(1)} %constant_dynamic-update-slice_fusion.refs_8_), channel_id=1, source_target_pairs={{0,10},{1,11},{2,12},{3,13},{4,14},{5,15},{6,0},{7,1},{8,2},{9,3},... | collective-permute-start | bytes 24584 | tf_op jit(solution)/shard_map/ppermute | solution.py:295

commit v6 on v5

--- a/solution.py
+++ b/solution.py
@@ -24,10 +24,12 @@
 NCHUNK = -(-W * L // CHUNK)
 KP = -(-W * L // CHUNK) * CHUNK
 ROWS = (BAND + 1) * CB
+NEAR = BAND // 2 + 1
+GROUP = 8
 SHIFT = L % CHUNK
 COVER = 4 * CHUNK
 
-VMEM_LIMIT = 28 << 20
+MAIN_LIMIT = 20 << 20
 PREP_LIMIT = 12 << 20
 EDGE_LIMIT = 1 << 20
 TABLE_LIMIT = 2 << 20
@@ -79,17 +81,22 @@
     return piece
 
 
-def filter_row(row_at, seg_ref, centre, line, band_ref):
-    own = seg_ref[centre : centre + 1, :]
+def filter_rows(row_at, seg_ref, centres, line, band_ref):
     line[...] = jnp.zeros_like(line)
-    for e in range(SPAN):
-        at = centre - HALF + e
-        keep = seg_ref[at : at + 1, :] == own
-        for j in range(NCHUNK):
-            line[j : j + 1, e * CHUNK : (e + 1) * CHUNK] = jnp.where(keep, row_at(e, j), 0.0)
+    for i, centre in enumerate(centres):
+        own = seg_ref[centre : centre + 1, :]
+        for e in range(SPAN):
+            at = centre - HALF + e
+            keep = jnp.where(seg_ref[at : at + 1, :] == own, 1.0, 0.0)
+            for j in range(NCHUNK):
+                line[i * SLOT + j : i * SLOT + j + 1, e * CHUNK : (e + 1) * CHUNK] = row_at(i, e, j) * keep
     share = jnp.dot(line[...].astype(bf16), band_ref[...], preferred_element_type=f32)
-    before = jnp.concatenate([jnp.zeros((1, CHUNK), f32), share[:-1, CHUNK:]], axis=0)
-    return share[:, :CHUNK] + before
+    results = []
+    for i in range(len(centres)):
+        part = share[i * SLOT : (i + 1) * SLOT]
+        before = jnp.concatenate([jnp.zeros((1, CHUNK), f32), part[:-1, CHUNK:]], axis=0)
+        results.append(part[:, :CHUNK] + before)
+    return results
 
 
 def prep_kernel(
@@ -121,11 +128,11 @@
     behind = jnp.where(even, halo_ref[:HALO].astype(f32), sown_ref[CB - HALO :].astype(f32))
     first = edge_ref[HALO:].astype(f32)
 
-    def row_at(e, j):
+    def row_at(_, e, j):
         rows, at = (behind, HALO - HALF + e) if e < HALF else (first, e - HALF)
         return chunk(rows, j)[at : at + 1]
 
-    source_ref[...] = filter_row(row_at, seg_ref, HALO, line, band_ref).astype(bf16)
+    source_ref[...] = filter_rows(row_at, seg_ref, (HALO,), line, band_ref)[0].astype(bf16)
     for load in loads[2:]:
         load.wait()
 
@@ -138,11 +145,10 @@
     pseg_ref[BAND + 1 :, :] = jnp.full((8 - BAND - 1, CHUNK), -1.0, f32)
 
 
-def main_kernel(pieces, count, *refs):
+def spectra_kernel(pieces, count, *refs):
     index_ref, own_ref, two_ref, four_ref, sown_ref, stwo_ref, sfour_ref, halo_ref = refs[:8]
     part_refs, refs = refs[8 : 8 + pieces], refs[8 + pieces :]
-    seg_ref, pseg_ref, band_ref, dft_ref, lag_ref, out_ref, src_ref = refs[:7]
-    rec, masked, filt, spec, turned, totals, line, swapped = refs[7:]
+    seg_ref, band_ref, dft_ref, spec, give_ref, rec, masked, filt, line = refs
     even = index_ref[0] % 2 == 0
 
     def put(start, rows):
@@ -153,31 +159,31 @@
     sown, halo = sown_ref[...].astype(f32), halo_ref[...].astype(f32)
     put(0, jnp.where(even, halo[:HALO], sown[CB - HALO :]))
     put(HALO, own_ref[...].astype(f32))
-    put(HALO + CB, jnp.where(even, sown, stwo))
+    put(HALO + CB, jnp.where(even, sown[:HALO], stwo[:HALO]))
+    put(2 * CB, jnp.where(even, sown[CB - HALO :], stwo[CB - HALO :]))
     put(HALO + 2 * CB, two_ref[...].astype(f32))
-    put(HALO + 3 * CB, jnp.where(even, stwo, sfour))
+    put(HALO + 3 * CB, jnp.where(even, stwo[:HALO], sfour[:HALO]))
+    put(4 * CB, jnp.where(even, stwo[CB - HALO :], sfour[CB - HALO :]))
     put(HALO + 4 * CB, four_ref[...].astype(f32))
     put(HALO + ROWS, jnp.where(even, sfour[:HALO], halo[HALO:]))
 
-    def filtered(inputs, rows, start):
-        share = jnp.dot(inputs[...], band_ref[...], preferred_element_type=f32)
+    for i in range(NEAR):
+        base = 2 * i * CB
+        held = masked.at[i % 2]
+        centre = seg_ref[base + HALO : base + HALO + CB, :]
+        for e in range(SPAN):
+            first = base + HALO - HALF + e
+            keep = jnp.where(seg_ref[first : first + CB, :] == centre, 1.0, 0.0)
+            for j in range(NCHUNK):
+                held[j * CB : (j + 1) * CB, e * CHUNK : (e + 1) * CHUNK] = (
+                    rec[j, first : first + CB, :] * keep
+                ).astype(bf16)
+        share = jnp.dot(held[...], band_ref[...], preferred_element_type=f32)
         for j in range(NCHUNK):
-            result = share[j * rows : (j + 1) * rows, :CHUNK]
+            result = share[j * CB : (j + 1) * CB, :CHUNK]
             if j:
-                result = result + share[(j - 1) * rows : j * rows, CHUNK:]
-            filt[j, pl.ds(start, rows), :] = result.astype(bf16)
-
-    for k in range(BAND + 1):
-        base = k * CB
-        held = masked.at[k % 2]
-        centre = seg_ref[pl.ds(base + HALO, CB), :]
-        for e in range(SPAN):
-            first = base + (HALO - HALF + e)
-            keep = jnp.where(seg_ref[pl.ds(first, CB), :] == centre, 1.0, 0.0)
-            for j in range(NCHUNK):
-                rows = rec[j, pl.ds(first, CB), :]
-                held[j * CB : (j + 1) * CB, e * CHUNK : (e + 1) * CHUNK] = (rows * keep).astype(bf16)
-        filtered(held, CB, base)
+                result = result + share[(j - 1) * CB : j * CB, CHUNK:]
+            filt[j, i * CB : (i + 1) * CB, :] = result.astype(bf16)
 
     rows = []
     for ref in part_refs:
@@ -187,84 +193,126 @@
     lists = count // 2
     skip = lists - len(mine)
     mine, theirs = ([part[0]] + [None] * skip + part[1:] for part in (mine, theirs))
-
-    def next_row(e, j):
-        at = HALO + ROWS - HALF + e
+    between = [HALO + r * CB for r in range(1, BAND + 2, 2)]
+
+    def row_at(i, e, j):
+        at = between[i] - HALF + e
         return rec[j, at : at + 1, :]
 
+    local = filter_rows(row_at, seg_ref, between, line, band_ref)
     for r in range(count):
-        if r <= BAND:
-            rows = [filt[j, r * CB : r * CB + 1, :] for j in range(NCHUNK)]
+        if r <= BAND and r % 2 == 0:
+            rows = [filt[j, r // 2 * CB : r // 2 * CB + 1, :] for j in range(NCHUNK)]
         else:
-            if r == BAND + 1:
-                value = filter_row(next_row, seg_ref, HALO + ROWS, line, band_ref)
+            if r <= BAND + 1:
+                value = local[r // 2]
             elif r % 2 == 0:
                 value = mine[r // 2]
             else:
                 value = jnp.where(even, theirs[r // 2], theirs[(r // 2 + 1) % lists])
             rows = [value[j : j + 1].astype(bf16) for j in range(NCHUNK)]
         for j in range(NCHUNK):
-            filt[j, ROWS + r : ROWS + r + 1, :] = rows[j]
-
-    tiles = COVER // CHUNK - 1
-    tail = None
-    for w in range(W):
-        lhs = jnp.concatenate([filt[w * tiles + q] for q in range(tiles + 1)], axis=1)
-        raw = jnp.dot(lhs, dft_ref[w], preferred_element_type=f32)
-        power = jnp.sum(raw * raw, axis=-1, keepdims=True) * (1.0 / L)
-        whitened = raw * lax.rsqrt(power + 1e-06)
-        head = whitened[:, :CHUNK] if tail is None else tail + whitened[:, :CHUNK]
-        spec[:, w * tiles * CHUNK : (w * tiles + 1) * CHUNK] = head.astype(bf16)
-        spec[:, (w * tiles + 1) * CHUNK : (w + 1) * tiles * CHUNK] = whitened[:, CHUNK : tiles * CHUNK].astype(bf16)
-        tail = whitened[:, tiles * CHUNK :]
-    spec[:, W * tiles * CHUNK :] = tail.astype(bf16)
-
+            filt[j, NEAR * CB + r : NEAR * CB + r + 1, :] = rows[j]
+
+    @pl.when(index_ref[0] >= 0)
+    def _():
+        tiles = COVER // CHUNK - 1
+        tail = None
+        for w in range(W):
+            lhs = jnp.concatenate([filt[w * tiles + q] for q in range(tiles + 1)], axis=1)
+            raw = jnp.dot(lhs, dft_ref[w], preferred_element_type=f32)
+            power = jnp.sum(raw * raw, axis=-1, keepdims=True) * (1.0 / L)
+            whitened = raw * lax.rsqrt(power + 1e-06)
+            head = whitened[:, :CHUNK] if tail is None else tail + whitened[:, :CHUNK]
+            spec[:, w * tiles * CHUNK : (w * tiles + 1) * CHUNK] = head.astype(bf16)
+            spec[:, (w * tiles + 1) * CHUNK : (w + 1) * tiles * CHUNK] = whitened[:, CHUNK : tiles * CHUNK].astype(bf16)
+            tail = whitened[:, tiles * CHUNK :]
+        spec[:, W * tiles * CHUNK :] = tail.astype(bf16)
+
+    give_ref[...] = jnp.where(even, spec[CB : 3 * CB, :].astype(f32), spec[: 2 * CB, :].astype(f32)).astype(bf16)
     row = lax.broadcasted_iota(jnp.int32, (count, count), 0)
     column = lax.broadcasted_iota(jnp.int32, (count, count), 1)
     ahead = row - index_ref[0]
     ahead = jnp.where(ahead < 0, ahead + count, ahead)
     order = jnp.where(ahead == column, 1.0, 0.0).astype(bf16)
-    spec[ROWS:, :] = jnp.dot(order, spec[ROWS:, :], preferred_element_type=f32).astype(bf16)
-
+    spec[NEAR * CB :, :] = jnp.dot(order, spec[NEAR * CB :, :], preferred_element_type=f32).astype(bf16)
+
+
+def turn_kernel(seg_ref, pseg_ref, spec, lag_ref, out_ref, src_ref, turned, totals, swapped):
+    count = spec.shape[0] - NEAR * CB
     own = spec[:CB, :].astype(f32)
     pieces = []
     for w in range(W):
         pieces += [own[:, w * L + F : (w + 1) * L], own[:, w * L : w * L + F]]
     swapped[...] = jnp.concatenate(pieces + [jnp.zeros((CB, KP - W * L), f32)], axis=1)
-
-    group = turned.shape[0] // CB
-    steps = LAGS // group
     own_seg = seg_ref[HALO : HALO + CB, :]
 
     def multiply(step, slot):
-        start = pl.multiple_of(step * group, group)
+        start = pl.multiple_of(step * GROUP, GROUP)
+        first = pl.multiple_of(step * GROUP * CB, GROUP * CB)
         for at in range(0, KP, CHUNK):
             lanes = slice(at, at + CHUNK)
-            straight, crossed = lag_ref[0, pl.ds(start, group), lanes], lag_ref[1, pl.ds(start, group), lanes]
+            straight, crossed = lag_ref[0, pl.ds(start, GROUP), lanes], lag_ref[1, pl.ds(start, GROUP), lanes]
             own, other = spec[:CB, lanes].astype(f32), swapped[:, lanes]
-            for g in range(group):
-                turned[g * CB : (g + 1) * CB, lanes] = (
+            for g in range(GROUP):
+                turned[pl.ds(first + g * CB, CB), lanes] = (
                     own * straight[g : g + 1, :] + other * crossed[g : g + 1, :]
                 ).astype(bf16)
         totals[slot] = lax.dot_general(
-            turned[...], spec[...], (((1,), (1,)), ((), ())), preferred_element_type=f32
+            turned[pl.ds(first, GROUP * CB), :], spec[...], (((1,), (1,)), ((), ())), preferred_element_type=f32
         )
 
     def write(step, slot):
-        start = pl.multiple_of(step * group, group)
-        for pair in range(group // 2):
-            low, high = 2 * pair * CB, (2 * pair + 1) * CB
-            lanes = pl.ds(pl.multiple_of(start * CB + pair * 2 * CB, 2 * CB), 2 * CB)
-            for k in range(BAND + 1):
-                both = jnp.concatenate(
-                    [totals[slot, at : at + CB, k * CB : (k + 1) * CB] for at in (low, high)], axis=1
-                )
-                keep = own_seg == pseg_ref[k : k + 1, :]
-                out_ref[k, :, lanes] = jnp.where(keep, both, 0.0).astype(bf16)
+        start = pl.multiple_of(step * GROUP, GROUP)
+        write_pairs(totals.at[slot], step, own_seg, pseg_ref, out_ref, range(0, BAND + 1, 2))
         sources = jnp.concatenate(
-            [totals[slot, g * CB : (g + 1) * CB, ROWS : ROWS + count] for g in range(group)], axis=1
+            [totals[slot, g * CB : (g + 1) * CB, NEAR * CB :] for g in range(GROUP)], axis=1
         )
-        src_ref[:, pl.ds(pl.multiple_of(start * count, group * count), group * count)] = sources.astype(bf16)
+        src_ref[:, pl.ds(pl.multiple_of(start * count, GROUP * count), GROUP * count)] = sources.astype(bf16)
+
+    multiply(0, 0)
+
+    @pl.loop(1, LAGS // GROUP)
+    def _(step):
+        write(step - 1, (step - 1) % 2)
+        multiply(step, step % 2)
+
+    write(LAGS // GROUP - 1, (LAGS // GROUP - 1) % 2)
+
+
+def write_pairs(total, step, own_seg, pseg_ref, out_ref, blocks):
+    for pair in range(GROUP // 2):
+        low, high = 2 * pair * CB, (2 * pair + 1) * CB
+        lanes = pl.ds(pl.multiple_of(step * GROUP * CB + pair * 2 * CB, 2 * CB), 2 * CB)
+        for i, k in enumerate(blocks):
+            both = jnp.concatenate([total[at : at + CB, i * CB : (i + 1) * CB] for at in (low, high)], axis=1)
+            keep = own_seg == pseg_ref[k : k + 1, :]
+            out_ref[i, :, lanes] = jnp.where(keep, both, 0.0).astype(bf16)
+
+
+def rest_kernel(seg_ref, pseg_ref, turned, take, even_ref, out_hbm, odd_ref, totals, even_sems, odd_sems):
+    early = start_loads(
+        tuple((even_ref.at[i], out_hbm.at[k]) for i, k in enumerate(range(0, BAND + 1, 2))), even_sems
+    )
+    own_seg = seg_ref[HALO : HALO + CB, :]
+    steps = LAGS // GROUP
+
+    def store(step, i):
+        lanes = pl.ds(pl.multiple_of(step * GROUP * CB, GROUP * CB), GROUP * CB)
+        return pltpu.make_async_copy(
+            odd_ref.at[i, :, lanes], out_hbm.at[2 * i + 1, :, lanes], odd_sems.at[step, i]
+        )
+
+    def multiply(step, slot):
+        rows = pl.ds(pl.multiple_of(step * GROUP * CB, GROUP * CB), GROUP * CB)
+        totals[slot] = lax.dot_general(
+            turned[rows, :], take[...], (((1,), (1,)), ((), ())), preferred_element_type=f32
+        )
+
+    def write(step, slot):
+        write_pairs(totals.at[slot], step, own_seg, pseg_ref, odd_ref, range(1, BAND + 1, 2))
+        for i in range(BAND // 2):
+            store(step, i).start()
 
     multiply(0, 0)
 
@@ -274,6 +322,11 @@
         multiply(step, step % 2)
 
     write(steps - 1, (steps - 1) % 2)
+    for step in range(steps):
+        for i in range(BAND // 2):
+            store(step, i).wait()
+    for load in early:
+        load.wait()
 
 
 VMEM = pl.BlockSpec(memory_space=pltpu.VMEM)
@@ -356,28 +409,50 @@
     )(index, segs)
     sfour, stwo = swap(four), swap(two)
 
-    group = 8
-    stacked, source_out = call(
-        functools.partial(main_kernel, len(parts), count),
+    limit = pltpu.CompilerParams(vmem_limit_bytes=MAIN_LIMIT if few else None)
+    spec, give = call(
+        functools.partial(spectra_kernel, len(parts), count),
         (
-            jax.ShapeDtypeStruct((BAND + 1, CB, LAGS * CB), bf16),
-            jax.ShapeDtypeStruct((CB, LAGS * count), bf16),
+            jax.ShapeDtypeStruct((NEAR * CB + count, KP), bf16),
+            jax.ShapeDtypeStruct((2 * CB, KP), bf16),
         ),
         [
             pltpu.VMEM((NCHUNK, ROWS + 2 * HALO, CHUNK), f32),
             pltpu.VMEM((2, NCHUNK * CB, SPAN * CHUNK), bf16),
-            pltpu.VMEM((NCHUNK, ROWS + count, CHUNK), bf16),
-            pltpu.VMEM((ROWS + count, KP), bf16),
-            pltpu.VMEM((group * CB, KP), bf16),
-            pltpu.VMEM((2, group * CB, ROWS + count), f32),
-            pltpu.VMEM((SLOT, SPAN * CHUNK), f32),
+            pltpu.VMEM((NCHUNK, NEAR * CB + count, CHUNK), bf16),
+            pltpu.VMEM((NEAR * SLOT, SPAN * CHUNK), f32),
+        ],
+        [SMEM] + [VMEM] * (10 + len(parts)),
+        compiler_params=limit,
+    )(index, own, two, four, sown, stwo, sfour, halo, *parts, segs, band, dft)
+    take = swap(give)
+    even_blocks, source_out, turned = call(
+        turn_kernel,
+        (
+            jax.ShapeDtypeStruct((NEAR, CB, LAGS * CB), bf16),
+            jax.ShapeDtypeStruct((CB, LAGS * count), bf16),
+            jax.ShapeDtypeStruct((LAGS * CB, KP), bf16),
+        ),
+        [
+            pltpu.VMEM((2, GROUP * CB, NEAR * CB + count), f32),
             pltpu.VMEM((CB, KP), f32),
         ],
-        [SMEM] + [VMEM] * (12 + len(parts)),
-        compiler_params=pltpu.CompilerParams(vmem_limit_bytes=VMEM_LIMIT if few else None),
-    )(
-        index, own, two, four, sown, stwo, sfour, halo, *parts, segs, pseg, band, dft, lags,
-    )
+        [VMEM] * 4,
+        compiler_params=limit,
+    )(segs, pseg, spec, lags)
+    stacked = pl.pallas_call(
+        rest_kernel,
+        out_shape=jax.ShapeDtypeStruct((BAND + 1, CB, LAGS * CB), bf16),
+        in_specs=[VMEM] * 5,
+        out_specs=HBM,
+        scratch_shapes=[
+            pltpu.VMEM((BAND // 2, CB, LAGS * CB), bf16),
+            pltpu.VMEM((2, GROUP * CB, 2 * CB), f32),
+            pltpu.SemaphoreType.DMA((NEAR,)),
+            pltpu.SemaphoreType.DMA((LAGS // GROUP, BAND // 2)),
+        ],
+        compiler_params=limit,
+    )(segs, pseg, turned, take, even_blocks)
     return (jnp.swapaxes(stacked, 0, 1), source_out)
 
 

time: 43.6 us -> 44.2 us (1.014)
  the two profiles are of different devices: /device:TPU:0 before, /device:TPU:5 now
where the time goes in v6:
time: 44.2 us; the launch traced here: 44 us
  starting transfers between devices  18.6 us (42%)
  Pallas kernels  15 us (34%)
  waiting for transfers between devices  9.67 us (22%)
  between operations  0.68 us (2%)
    ppermute x7, starting transfers between devices, ahead(): lax.ppermute(value, 'fibre', [(i, (i - distance) % count) for i in range(...  11.5 us
    ppermute x1, waiting for transfers between devices, per_device(): halo = lax.ppermute(edge, 'fibre', route)  6.22 us
    pallas_call x1, Pallas kernels, per_device(): call(turn_kernel, (jax.ShapeDtypeStruct((NEAR, CB, LAGS * CB), bf16), jax...  5.24 us
    ppermute x5, starting transfers between devices, swap(): return lax.ppermute(value, 'fibre', [(i, i ^ 1) for i in range(count)])  4.37 us
    pallas_call x1, Pallas kernels, per_device(): call(functools.partial(spectra_kernel, len(parts), count), (jax.ShapeDtyp...  3.75 us
    pallas_call x1, Pallas kernels, per_device(): pl.pallas_call(rest_kernel, out_shape=jax.ShapeDtypeStruct((BAND + 1, CB,...  3.3 us
    ppermute x7, waiting for transfers between devices, ahead(): lax.ppermute(value, 'fibre', [(i, (i - distance) % count) for i in range(...  2.87 us
    ppermute x1, starting transfers between devices, per_device(): halo = lax.ppermute(edge, 'fibre', route)  2.7 us
  transfers between devices with their start and end apart: 13, of which 5 were waited for; matrix products, arithmetic and copies ran while one was open for 0% of the time, Pallas kernels for 18%

profile of v6, /device:TPU:5, one launch (start us, length us, event | category | flops | bytes accessed | tf_op | source)
XLA Modules:
  0.0 44.0 jit_solution(16346637730924383989)
XLA Ops:
  0.6 0.7 %collective-permute-start.1 = (bf16[64,1600]{1,0:T(8,128)(2,1)}, bf16[64,1600]{1,0:T(8,128)(2,1)S(1)}, u32[]{:S(2)}, u32[]{:S(2)}) collective-permute-start(bf16[64,1600]{1,0:T(8,128)(2,1)} %own_hbm.3), channel_id=1, source_target_pairs={{0,1},{1,0},{2,3},{3,2},{4,5},{5,4},{6,7},{7,6},{8,9},{9,8},{10,11... | collective-permute-start | bytes 614408 | tf_op jit(solution)/shard_map/ppermute | solution.py:351
  1.4 3.3 %collective-permute-start.3 = (bf16[64,1600]{1,0:T(8,128)(2,1)}, bf16[64,1600]{1,0:T(8,128)(2,1)S(1)}, u32[]{:S(2)}, u32[]{:S(2)}) collective-permute-start(bf16[64,1600]{1,0:T(8,128)(2,1)} %own_hbm.3), channel_id=1, source_target_pairs={{0,12},{1,13},{2,14},{3,15},{4,0},{5,1},{6,2},{7,3},{8,4},{9,5},{1... | collective-permute-start | bytes 614408 | tf_op jit(solution)/shard_map/ppermute | solution.py:348
  4.7 0.2 collective-permute-start.2
  4.9 0.8 %shard_map.68.edge_ref = bf16[16,1600]{1,0:T(8,128)(2,1)S(1)} custom-call(bf16[64,1600]{1,0:T(8,128)(2,1)} %own_hbm.3), custom_call_target="tpu_custom_call" | custom-call | tf_op jit(solution)/shard_map/pallas_call | solution.py:357
  5.7 2.7 %collective-permute-start = (bf16[16,1600]{1,0:T(8,128)(2,1)S(1)}, bf16[16,1600]{1,0:T(8,128)(2,1)S(1)}, u32[]{:S(2)}, u32[]{:S(2)}) collective-permute-start(bf16[16,1600]{1,0:T(8,128)(2,1)S(1)} %shard_map.68.edge_ref), channel_id=1, source_target_pairs={{0,11},{1,2},{2,13},{3,4},{4,15},{5,6},{6,1},{7,8},{8,3},{9,10},{1... | collective-permute-start | bytes 153608 | tf_op jit(solution)/shard_map/ppermute | solution.py:365
  8.4 6.2 %collective-permute-done.halo_ref.refs_7_ = bf16[16,1600]{1,0:T(8,128)(2,1)S(1)} collective-permute-done((bf16[16,1600]{1,0:T(8,128)(2,1)S(1)}, bf16[16,1600]{1,0:T(8,128)(2,1)S(1)}, u32[]{:S(2)}, u32[]{:S(2)}) %collective-permute-start) | collective-permute-done | bytes 51232 | tf_op jit(solution)/shard_map/ppermute | solution.py:365
  14.7 1.8 %shard_map.69 = (bf16[16,128]{1,0:T(8,128)(2,1)S(1)}, bf16[1152,256]{1,0:T(8,128)(2,1)S(1)}, f32[336,128]{1,0:T(8,128)S(1)}, bf16[64,1600]{1,0:T(8,128)(2,1)S(1)...) custom-call(s32[1]{0:T(128)} %bitcast.index_ref.refs_0_, bf16[16,1600]{1,0:T(8,128)(2,1)S(1)} %shard_map.68.edge_ref, ...), custom_call_target="tpu_custom_call" | custom-call | tf_op jit(solution)/shard_map/pallas_call | solution.py:371
  16.5 0.1 collective-permute-start.6
  16.6 0.0 collective-permute-done.3.refs_3_
  16.6 0.5 %collective-permute-start.5 = (bf16[64,1600]{1,0:T(8,128)(2,1)S(1)}, bf16[64,1600]{1,0:T(8,128)(2,1)S(1)}, u32[]{:S(2)}, u32[]{:S(2)}) collective-permute-start(bf16[64,1600]{1,0:T(8,128)(2,1)S(1)} %collective-permute-done.3.refs_3_), channel_id=1, source_target_pairs={{0,1},{1,0},{2,3},{3,2},{4,5},{5,4},{6,7},{7,6},{8,9},{9,8},{10,11... | collective-permute-start | bytes 614408 | tf_op jit(solution)/shard_map/ppermute | solution.py:351
  17.1 0.1 collective-permute-start.4
  17.2 0.6 %collective-permute-done.6 = bf16[16,128]{1,0:T(8,128)(2,1)S(1)} collective-permute-done((bf16[16,128]{1,0:T(8,128)(2,1)S(1)}, bf16[16,128]{1,0:T(8,128)(2,1)S(1)}, u32[]{:S(2)}, u32[]{:S(2)}) %collective-permute-start.6) | collective-permute-done | bytes 4128 | tf_op jit(solution)/shard_map/ppermute | solution.py:351
  17.7 2.2 %collective-permute-start.11 = (bf16[32,128]{1,0:T(8,128)(2,1)S(1)}, bf16[32,128]{1,0:T(8,128)(2,1)S(1)}, u32[]{:S(2)}, u32[]{:S(2)}) collective-permute-start(bf16[32,128]{1,0:T(8,128)(2,1)S(1)} %constant_dynamic-update-slice_fusion.refs_8_), channel_id=1, source_target_pairs={{0,2},{1,3},{2,4},{3,5},{4,6},{5,7},{6,8},{7,9},{8,10},{9,11},{10,... | collective-permute-start | bytes 24584 | tf_op jit(solution)/shard_map/ppermute | solution.py:348
  20.0 0.0 collective-permute-start.10
  20.0 3.9 %collective-permute-start.9 = (bf16[32,128]{1,0:T(8,128)(2,1)S(1)}, bf16[32,128]{1,0:T(8,128)(2,1)S(1)}, u32[]{:S(2)}, u32[]{:S(2)}) collective-permute-start(bf16[32,128]{1,0:T(8,128)(2,1)S(1)} %constant_dynamic-update-slice_fusion.refs_8_), channel_id=1, source_target_pairs={{0,6},{1,7},{2,8},{3,9},{4,10},{5,11},{6,12},{7,13},{8,14},{9,15},... | collective-permute-start | bytes 24584 | tf_op jit(solution)/shard_map/ppermute | solution.py:348
  23.9 0.4 collective-permute-done.10.refs_12_
  24.3 1.8 %collective-permute-start.7 = (bf16[32,128]{1,0:T(8,128)(2,1)S(1)}, bf16[32,128]{1,0:T(8,128)(2,1)S(1)}, u32[]{:S(2)}, u32[]{:S(2)}) collective-permute-start(bf16[32,128]{1,0:T(8,128)(2,1)S(1)} %constant_dynamic-update-slice_fusion.refs_8_), channel_id=1, source_target_pairs={{0,10},{1,11},{2,12},{3,13},{4,14},{5,15},{6,0},{7,1},{8,2},{9,3},... | collective-permute-start | bytes 24584 | tf_op jit(solution)/shard_map/ppermute | solution.py:348
  26.1 1.2 %collective-permute-done.8.refs_10_ = bf16[32,128]{1,0:T(8,128)(2,1)S(1)} collective-permute-done((bf16[32,128]{1,0:T(8,128)(2,1)S(1)}, bf16[32,128]{1,0:T(8,128)(2,1)S(1)}, u32[]{:S(2)}, u32[]{:S(2)}) %collective-permute-start.8) | collective-permute-done | bytes 8224 | tf_op jit(solution)/shard_map/ppermute | solution.py:348
  27.3 1.3 %collective-permute-done.7.refs_9_ = bf16[32,128]{1,0:T(8,128)(2,1)S(1)} collective-permute-done((bf16[32,128]{1,0:T(8,128)(2,1)S(1)}, bf16[32,128]{1,0:T(8,128)(2,1)S(1)}, u32[]{:S(2)}, u32[]{:S(2)}) %collective-permute-start.7) | collective-permute-done | bytes 8224 | tf_op jit(solution)/shard_map/ppermute | solution.py:348
  28.6 3.8 %shard_map.71 = (bf16[208,1664]{1,0:T(8,128)(2,1)S(1)}, bf16[128,1664]{1,0:T(8,128)(2,1)S(1)}) custom-call(s32[1]{0:T(128)} %bitcast.index_ref.refs_0_, bf16[64,1600]{1,0:T(8,128)(2,1)S(1)} %get-tuple-element.14.refs_1_, bf16[64,1600]{1,0:T(8,128)(2,1)S(1)} %collective-permute-done.2.refs_2_, bf16[64,1600]{1,0:T(8,128)(2,1)S(1)} %collective-permute-done.3.refs_3_, ...), custom_call_target="tpu_custom_call" | custom-call | tf_op jit(solution)/shard_map/pallas_call | solution.py:413
  32.3 3.0 %collective-permute-start.12 = (bf16[128,1664]{1,0:T(8,128)(2,1)S(1)}, bf16[128,1664]{1,0:T(8,128)(2,1)S(1)}, u32[]{:S(2)}, u32[]{:S(2)}) collective-permute-start(bf16[128,1664]{1,0:T(8,128)(2,1)S(1)} %get-tuple-element.21), channel_id=1, source_target_pairs={{0,1},{1,0},{2,3},{3,2},{4,5},{5,4},{6,7},{7,6},{8,9},{9,8},{10,11... | collective-permute-start | bytes 1277960 | tf_op jit(solution)/shard_map/ppermute | solution.py:351
  35.3 0.1 shard_map.70.pseg_ref
  35.4 5.2 %shard_map.72 = (bf16[3,64,2048]{2,1,0:T(8,128)(2,1)S(1)}, bf16[64,512]{1,0:T(8,128)(2,1)}, bf16[2048,1664]{1,0:T(8,128)(2,1)S(1)}) custom-call(f32[336,128]{1,0:T(8,128)S(1)} %get-tuple-element.13.seg_ref.refs_14_, f32[8,128]{1,0:T(8,128)S(1)} %shard_map.70.pseg_ref, bf16[208,1664]{1,0:T(8,128)(2,1)S(1)} %get-tuple-element.18.spec, ...), custom_call_target="tpu_custom_call" | custom-call | tf_op jit(solution)/shard_map/pallas_call | solution.py:429
  40.7 3.3 %shard_map.73 = bf16[5,64,2048]{2,1,0:T(8,128)(2,1)} custom-call(f32[336,128]{1,0:T(8,128)S(1)} %get-tuple-element.13.seg_ref.refs_14_, f32[8,128]{1,0:T(8,128)S(1)} %shard_map.70.pseg_ref, bf16[2048,1664]{1,0:T(8,128)(2,1)S(1)} %get-tuple-element.20.turned, bf16[128,1664]{1,0:T(8,128)(2,1)S(1)} %collective-permute-done.12.take, ...), custom_call_target="tpu_custom_call" | custom-call | tf_op jit(solution)/shard_map/pallas_call | solution.py:443
  (10 shorter events, 0.0 us)
Async XLA Ops:
  0.6 14.0 %collective-permute-start.1 = (bf16[64,1600]{1,0:T(8,128)(2,1)}, bf16[64,1600]{1,0:T(8,128)(2,1)S(1)}, u32[]{:S(2)}, u32[]{:S(2)}) collective-permute-start(bf16[64,1600]{1,0:T(8,128)(2,1)} %own_hbm.3), channel_id=1, source_target_pairs={{0,1},{1,0},{2,3},{3,2},{4,5},{5,4},{6,7},{7,6},{8,9},{9,8},{10,11... | collective-permute-start | bytes 614408 | tf_op jit(solution)/shard_map/ppermute | solution.py:351
  1.4 15.2 %collective-permute-start.3 = (bf16[64,1600]{1,0:T(8,128)(2,1)}, bf16[64,1600]{1,0:T(8,128)(2,1)S(1)}, u32[]{:S(2)}, u32[]{:S(2)}) collective-permute-start(bf16[64,1600]{1,0:T(8,128)(2,1)} %own_hbm.3), channel_id=1, source_target_pairs={{0,12},{1,13},{2,14},{3,15},{4,0},{5,1},{6,2},{7,3},{8,4},{9,5},{1... | collective-permute-start | bytes 614408 | tf_op jit(solution)/shard_map/ppermute | solution.py:348
  4.7 12.4 %collective-permute-start.2 = (bf16[64,1600]{1,0:T(8,128)(2,1)}, bf16[64,1600]{1,0:T(8,128)(2,1)S(1)}, u32[]{:S(2)}, u32[]{:S(2)}) collective-permute-start(bf16[64,1600]{1,0:T(8,128)(2,1)} %own_hbm.3), channel_id=1, source_target_pairs={{0,14},{1,15},{2,0},{3,1},{4,2},{5,3},{6,4},{7,5},{8,6},{9,7},{10,... | collective-permute-start | bytes 614408 | tf_op jit(solution)/shard_map/ppermute | solution.py:348
  5.7 8.9 %collective-permute-start = (bf16[16,1600]{1,0:T(8,128)(2,1)S(1)}, bf16[16,1600]{1,0:T(8,128)(2,1)S(1)}, u32[]{:S(2)}, u32[]{:S(2)}) collective-permute-start(bf16[16,1600]{1,0:T(8,128)(2,1)S(1)} %shard_map.68.edge_ref), channel_id=1, source_target_pairs={{0,11},{1,2},{2,13},{3,4},{4,15},{5,6},{6,1},{7,8},{8,3},{9,10},{1... | collective-permute-start | bytes 153608 | tf_op jit(solution)/shard_map/ppermute | solution.py:365
  16.5 1.2 %collective-permute-start.6 = (bf16[16,128]{1,0:T(8,128)(2,1)S(1)}, bf16[16,128]{1,0:T(8,128)(2,1)S(1)}, u32[]{:S(2)}, u32[]{:S(2)}) collective-permute-start(bf16[16,128]{1,0:T(8,128)(2,1)S(1)} %get-tuple-element.15), channel_id=1, source_target_pairs={{0,1},{1,0},{2,3},{3,2},{4,5},{5,4},{6,7},{7,6},{8,9},{9,8},{10,11... | collective-permute-start | bytes 12296 | tf_op jit(solution)/shard_map/ppermute | solution.py:351
  16.6 12.0 %collective-permute-start.5 = (bf16[64,1600]{1,0:T(8,128)(2,1)S(1)}, bf16[64,1600]{1,0:T(8,128)(2,1)S(1)}, u32[]{:S(2)}, u32[]{:S(2)}) collective-permute-start(bf16[64,1600]{1,0:T(8,128)(2,1)S(1)} %collective-permute-done.3.refs_3_), channel_id=1, source_target_pairs={{0,1},{1,0},{2,3},{3,2},{4,5},{5,4},{6,7},{7,6},{8,9},{9,8},{10,11... | collective-permute-start | bytes 614408 | tf_op jit(solution)/shard_map/ppermute | solution.py:351
  17.1 11.5 %collective-permute-start.4 = (bf16[64,1600]{1,0:T(8,128)(2,1)S(1)}, bf16[64,1600]{1,0:T(8,128)(2,1)S(1)}, u32[]{:S(2)}, u32[]{:S(2)}) collective-permute-start(bf16[64,1600]{1,0:T(8,128)(2,1)S(1)} %collective-permute-done.2.refs_2_), channel_id=1, source_target_pairs={{0,1},{1,0},{2,3},{3,2},{4,5},{5,4},{6,7},{7,6},{8,9},{9,8},{10,11... | collective-permute-start | bytes 614408 | tf_op jit(solution)/shard_map/ppermute | solution.py:351
  17.7 6.1 %collective-permute-start.11 = (bf16[32,128]{1,0:T(8,128)(2,1)S(1)}, bf16[32,128]{1,0:T(8,128)(2,1)S(1)}, u32[]{:S(2)}, u32[]{:S(2)}) collective-permute-start(bf16[32,128]{1,0:T(8,128)(2,1)S(1)} %constant_dynamic-update-slice_fusion.refs_8_), channel_id=1, source_target_pairs={{0,2},{1,3},{2,4},{3,5},{4,6},{5,7},{6,8},{7,9},{8,10},{9,11},{10,... | collective-permute-start | bytes 24584 | tf_op jit(solution)/shard_map/ppermute | solution.py:348
  20.0 4.3 %collective-permute-start.10 = (bf16[32,128]{1,0:T(8,128)(2,1)S(1)}, bf16[32,128]{1,0:T(8,128)(2,1)S(1)}, u32[]{:S(2)}, u32[]{:S(2)}) collective-permute-start(bf16[32,128]{1,0:T(8,128)(2,1)S(1)} %constant_dynamic-update-slice_fusion.refs_8_), channel_id=1, source_target_pairs={{0,4},{1,5},{2,6},{3,7},{4,8},{5,9},{6,10},{7,11},{8,12},{9,13},{1... | collective-permute-start | bytes 24584 | tf_op jit(solution)/shard_map/ppermute | solution.py:348
  20.0 6.1 %collective-permute-start.9 = (bf16[32,128]{1,0:T(8,128)(2,1)S(1)}, bf16[32,128]{1,0:T(8,128)(2,1)S(1)}, u32[]{:S(2)}, u32[]{:S(2)}) collective-permute-start(bf16[32,128]{1,0:T(8,128)(2,1)S(1)} %constant_dynamic-update-slice_fusion.refs_8_), channel_id=1, source_target_pairs={{0,6},{1,7},{2,8},{3,9},{4,10},{5,11},{6,12},{7,13},{8,14},{9,15},... | collective-permute-start | bytes 24584 | tf_op jit(solution)/shard_map/ppermute | solution.py:348
  23.9 3.4 %collective-permute-start.8 = (bf16[32,128]{1,0:T(8,128)(2,1)S(1)}, bf16[32,128]{1,0:T(8,128)(2,1)S(1)}, u32[]{:S(2)}, u32[]{:S(2)}) collective-permute-start(bf16[32,128]{1,0:T(8,128)(2,1)S(1)} %constant_dynamic-update-slice_fusion.refs_8_), channel_id=1, source_target_pairs={{0,8},{1,9},{2,10},{3,11},{4,12},{5,13},{6,14},{7,15},{8,0},{9,1},... | collective-permute-start | bytes 24584 | tf_op jit(solution)/shard_map/ppermute | solution.py:348
  24.3 4.3 %collective-permute-start.7 = (bf16[32,128]{1,0:T(8,128)(2,1)S(1)}, bf16[32,128]{1,0:T(8,128)(2,1)S(1)}, u32[]{:S(2)}, u32[]{:S(2)}) collective-permute-start(bf16[32,128]{1,0:T(8,128)(2,1)S(1)} %constant_dynamic-update-slice_fusion.refs_8_), channel_id=1, source_target_pairs={{0,10},{1,11},{2,12},{3,13},{4,14},{5,15},{6,0},{7,1},{8,2},{9,3},... | collective-permute-start | bytes 24584 | tf_op jit(solution)/shard_map/ppermute | solution.py:348
  32.3 8.3 %collective-permute-start.12 = (bf16[128,1664]{1,0:T(8,128)(2,1)S(1)}, bf16[128,1664]{1,0:T(8,128)(2,1)S(1)}, u32[]{:S(2)}, u32[]{:S(2)}) collective-permute-start(bf16[128,1664]{1,0:T(8,128)(2,1)S(1)} %get-tuple-element.21), channel_id=1, source_target_pairs={{0,1},{1,0},{2,3},{3,2},{4,5},{5,4},{6,7},{7,6},{8,9},{9,8},{10,11... | collective-permute-start | bytes 1277960 | tf_op jit(solution)/shard_map/ppermute | solution.py:351

commit v7 on v6

--- a/solution.py
+++ b/solution.py
@@ -248,44 +248,41 @@
     own_seg = seg_ref[HALO : HALO + CB, :]
 
     def multiply(step, slot):
-        start = pl.multiple_of(step * GROUP, GROUP)
-        first = pl.multiple_of(step * GROUP * CB, GROUP * CB)
+        start, first = step * GROUP, step * GROUP * CB
         for at in range(0, KP, CHUNK):
             lanes = slice(at, at + CHUNK)
-            straight, crossed = lag_ref[0, pl.ds(start, GROUP), lanes], lag_ref[1, pl.ds(start, GROUP), lanes]
+            straight, crossed = lag_ref[0, start : start + GROUP, lanes], lag_ref[1, start : start + GROUP, lanes]
             own, other = spec[:CB, lanes].astype(f32), swapped[:, lanes]
             for g in range(GROUP):
-                turned[pl.ds(first + g * CB, CB), lanes] = (
+                turned[first + g * CB : first + (g + 1) * CB, lanes] = (
                     own * straight[g : g + 1, :] + other * crossed[g : g + 1, :]
                 ).astype(bf16)
         totals[slot] = lax.dot_general(
-            turned[pl.ds(first, GROUP * CB), :], spec[...], (((1,), (1,)), ((), ())), preferred_element_type=f32
+            turned[first : first + GROUP * CB, :], spec[...], (((1,), (1,)), ((), ())), preferred_element_type=f32
         )
 
     def write(step, slot):
-        start = pl.multiple_of(step * GROUP, GROUP)
+        start = step * GROUP
         write_pairs(totals.at[slot], step, own_seg, pseg_ref, out_ref, range(0, BAND + 1, 2))
         sources = jnp.concatenate(
             [totals[slot, g * CB : (g + 1) * CB, NEAR * CB :] for g in range(GROUP)], axis=1
         )
-        src_ref[:, pl.ds(pl.multiple_of(start * count, GROUP * count), GROUP * count)] = sources.astype(bf16)
-
-    multiply(0, 0)
-
-    @pl.loop(1, LAGS // GROUP)
-    def _(step):
-        write(step - 1, (step - 1) % 2)
+        src_ref[:, start * count : (start + GROUP) * count] = sources.astype(bf16)
+
+    for step in range(LAGS // GROUP):
         multiply(step, step % 2)
-
+        if step:
+            write(step - 1, (step - 1) % 2)
     write(LAGS // GROUP - 1, (LAGS // GROUP - 1) % 2)
 
 
 def write_pairs(total, step, own_seg, pseg_ref, out_ref, blocks):
     for pair in range(GROUP // 2):
         low, high = 2 * pair * CB, (2 * pair + 1) * CB
-        lanes = pl.ds(pl.multiple_of(step * GROUP * CB + pair * 2 * CB, 2 * CB), 2 * CB)
+        at = step * GROUP * CB + pair * 2 * CB
+        lanes = slice(at, at + 2 * CB)
         for i, k in enumerate(blocks):
-            both = jnp.concatenate([total[at : at + CB, i * CB : (i + 1) * CB] for at in (low, high)], axis=1)
+            both = jnp.concatenate([total[row : row + CB, i * CB : (i + 1) * CB] for row in (low, high)], axis=1)
             keep = own_seg == pseg_ref[k : k + 1, :]
             out_ref[i, :, lanes] = jnp.where(keep, both, 0.0).astype(bf16)
 
@@ -298,15 +295,15 @@
     steps = LAGS // GROUP
 
     def store(step, i):
-        lanes = pl.ds(pl.multiple_of(step * GROUP * CB, GROUP * CB), GROUP * CB)
+        lanes = pl.ds(step * GROUP * CB, GROUP * CB)
         return pltpu.make_async_copy(
             odd_ref.at[i, :, lanes], out_hbm.at[2 * i + 1, :, lanes], odd_sems.at[step, i]
         )
 
     def multiply(step, slot):
-        rows = pl.ds(pl.multiple_of(step * GROUP * CB, GROUP * CB), GROUP * CB)
+        first = step * GROUP * CB
         totals[slot] = lax.dot_general(
-            turned[rows, :], take[...], (((1,), (1,)), ((), ())), preferred_element_type=f32
+            turned[first : first + GROUP * CB, :], take[...], (((1,), (1,)), ((), ())), preferred_element_type=f32
         )
 
     def write(step, slot):
@@ -314,13 +311,10 @@
         for i in range(BAND // 2):
             store(step, i).start()
 
-    multiply(0, 0)
-
-    @pl.loop(1, steps)
-    def _(step):
-        write(step - 1, (step - 1) % 2)
+    for step in range(steps):
         multiply(step, step % 2)
-
+        if step:
+            write(step - 1, (step - 1) % 2)
     write(steps - 1, (steps - 1) % 2)
     for step in range(steps):
         for i in range(BAND // 2):

time: 44.2 us -> 42.3 us (0.957)
  Pallas kernels: 15 us -> 13.1 us
    pallas_call x1, Pallas kernels: 5.24 us -> 3.86 us  [per_device(): call(turn_kernel, (jax.ShapeDtypeStruct((NEAR, CB, LAGS * CB), bf16), jax...]
    pallas_call x1, Pallas kernels: 3.3 us -> 2.77 us  [per_device(): pl.pallas_call(rest_kernel, out_shape=jax.ShapeDtypeStruct((BAND + 1, CB,...]
  transfers between devices with their start and end apart: 13 -> 13, of which waited for: 5 -> 5; matrix products, arithmetic and copies ran while one was open for 0% -> 0% of each run, Pallas kernels for 18% -> 16%
where the time goes in v7:
time: 42.3 us; the launch traced here: 42.1 us
  starting transfers between devices  18.6 us (44%)
  Pallas kernels  13.1 us (31%)
  waiting for transfers between devices  9.67 us (23%)
  between operations  0.68 us (2%)
    ppermute x7, starting transfers between devices, ahead(): lax.ppermute(value, 'fibre', [(i, (i - distance) % count) for i in range(...  11.5 us
    ppermute x1, waiting for transfers between devices, per_device(): halo = lax.ppermute(edge, 'fibre', route)  6.22 us
    ppermute x5, starting transfers between devices, swap(): return lax.ppermute(value, 'fibre', [(i, i ^ 1) for i in range(count)])  4.37 us
    pallas_call x1, Pallas kernels, per_device(): call(turn_kernel, (jax.ShapeDtypeStruct((NEAR, CB, LAGS * CB), bf16), jax...  3.86 us
    pallas_call x1, Pallas kernels, per_device(): call(functools.partial(spectra_kernel, len(parts), count), (jax.ShapeDtyp...  3.75 us
    ppermute x7, waiting for transfers between devices, ahead(): lax.ppermute(value, 'fibre', [(i, (i - distance) % count) for i in range(...  2.87 us
    pallas_call x1, Pallas kernels, per_device(): pl.pallas_call(rest_kernel, out_shape=jax.ShapeDtypeStruct((BAND + 1, CB,...  2.77 us
    ppermute x1, starting transfers between devices, per_device(): halo = lax.ppermute(edge, 'fibre', route)  2.7 us
  transfers between devices with their start and end apart: 13, of which 5 were waited for; matrix products, arithmetic and copies ran while one was open for 0% of the time, Pallas kernels for 16%

profile of v7, /device:TPU:5, one launch (start us, length us, event | category | flops | bytes accessed | tf_op | source)
XLA Modules:
  0.0 42.1 jit_solution(12630113701661517220)
XLA Ops:
  0.6 0.7 %collective-permute-start.1 = (bf16[64,1600]{1,0:T(8,128)(2,1)}, bf16[64,1600]{1,0:T(8,128)(2,1)S(1)}, u32[]{:S(2)}, u32[]{:S(2)}) collective-permute-start(bf16[64,1600]{1,0:T(8,128)(2,1)} %own_hbm.3), channel_id=1, source_target_pairs={{0,1},{1,0},{2,3},{3,2},{4,5},{5,4},{6,7},{7,6},{8,9},{9,8},{10,11... | collective-permute-start | bytes 614408 | tf_op jit(solution)/shard_map/ppermute | solution.py:345
  1.4 3.3 %collective-permute-start.3 = (bf16[64,1600]{1,0:T(8,128)(2,1)}, bf16[64,1600]{1,0:T(8,128)(2,1)S(1)}, u32[]{:S(2)}, u32[]{:S(2)}) collective-permute-start(bf16[64,1600]{1,0:T(8,128)(2,1)} %own_hbm.3), channel_id=1, source_target_pairs={{0,12},{1,13},{2,14},{3,15},{4,0},{5,1},{6,2},{7,3},{8,4},{9,5},{1... | collective-permute-start | bytes 614408 | tf_op jit(solution)/shard_map/ppermute | solution.py:342
  4.7 0.2 collective-permute-start.2
  4.9 0.8 %shard_map.68.edge_ref = bf16[16,1600]{1,0:T(8,128)(2,1)S(1)} custom-call(bf16[64,1600]{1,0:T(8,128)(2,1)} %own_hbm.3), custom_call_target="tpu_custom_call" | custom-call | tf_op jit(solution)/shard_map/pallas_call | solution.py:351
  5.7 2.7 %collective-permute-start = (bf16[16,1600]{1,0:T(8,128)(2,1)S(1)}, bf16[16,1600]{1,0:T(8,128)(2,1)S(1)}, u32[]{:S(2)}, u32[]{:S(2)}) collective-permute-start(bf16[16,1600]{1,0:T(8,128)(2,1)S(1)} %shard_map.68.edge_ref), channel_id=1, source_target_pairs={{0,11},{1,2},{2,13},{3,4},{4,15},{5,6},{6,1},{7,8},{8,3},{9,10},{1... | collective-permute-start | bytes 153608 | tf_op jit(solution)/shard_map/ppermute | solution.py:359
  8.4 6.2 %collective-permute-done.halo_ref.refs_7_ = bf16[16,1600]{1,0:T(8,128)(2,1)S(1)} collective-permute-done((bf16[16,1600]{1,0:T(8,128)(2,1)S(1)}, bf16[16,1600]{1,0:T(8,128)(2,1)S(1)}, u32[]{:S(2)}, u32[]{:S(2)}) %collective-permute-start) | collective-permute-done | bytes 51232 | tf_op jit(solution)/shard_map/ppermute | solution.py:359
  14.7 1.8 %shard_map.69 = (bf16[16,128]{1,0:T(8,128)(2,1)S(1)}, bf16[1152,256]{1,0:T(8,128)(2,1)S(1)}, f32[336,128]{1,0:T(8,128)S(1)}, bf16[64,1600]{1,0:T(8,128)(2,1)S(1)...) custom-call(s32[1]{0:T(128)} %bitcast.index_ref.refs_0_, bf16[16,1600]{1,0:T(8,128)(2,1)S(1)} %shard_map.68.edge_ref, ...), custom_call_target="tpu_custom_call" | custom-call | tf_op jit(solution)/shard_map/pallas_call | solution.py:365
  16.5 0.1 collective-permute-start.6
  16.6 0.0 collective-permute-done.3.refs_3_
  16.6 0.5 %collective-permute-start.5 = (bf16[64,1600]{1,0:T(8,128)(2,1)S(1)}, bf16[64,1600]{1,0:T(8,128)(2,1)S(1)}, u32[]{:S(2)}, u32[]{:S(2)}) collective-permute-start(bf16[64,1600]{1,0:T(8,128)(2,1)S(1)} %collective-permute-done.3.refs_3_), channel_id=1, source_target_pairs={{0,1},{1,0},{2,3},{3,2},{4,5},{5,4},{6,7},{7,6},{8,9},{9,8},{10,11... | collective-permute-start | bytes 614408 | tf_op jit(solution)/shard_map/ppermute | solution.py:345
  17.1 0.1 collective-permute-start.4
  17.2 0.6 %collective-permute-done.6 = bf16[16,128]{1,0:T(8,128)(2,1)S(1)} collective-permute-done((bf16[16,128]{1,0:T(8,128)(2,1)S(1)}, bf16[16,128]{1,0:T(8,128)(2,1)S(1)}, u32[]{:S(2)}, u32[]{:S(2)}) %collective-permute-start.6) | collective-permute-done | bytes 4128 | tf_op jit(solution)/shard_map/ppermute | solution.py:345
  17.7 2.2 %collective-permute-start.11 = (bf16[32,128]{1,0:T(8,128)(2,1)S(1)}, bf16[32,128]{1,0:T(8,128)(2,1)S(1)}, u32[]{:S(2)}, u32[]{:S(2)}) collective-permute-start(bf16[32,128]{1,0:T(8,128)(2,1)S(1)} %constant_dynamic-update-slice_fusion.refs_8_), channel_id=1, source_target_pairs={{0,2},{1,3},{2,4},{3,5},{4,6},{5,7},{6,8},{7,9},{8,10},{9,11},{10,... | collective-permute-start | bytes 24584 | tf_op jit(solution)/shard_map/ppermute | solution.py:342
  20.0 0.0 collective-permute-start.10
  20.0 3.9 %collective-permute-start.9 = (bf16[32,128]{1,0:T(8,128)(2,1)S(1)}, bf16[32,128]{1,0:T(8,128)(2,1)S(1)}, u32[]{:S(2)}, u32[]{:S(2)}) collective-permute-start(bf16[32,128]{1,0:T(8,128)(2,1)S(1)} %constant_dynamic-update-slice_fusion.refs_8_), channel_id=1, source_target_pairs={{0,6},{1,7},{2,8},{3,9},{4,10},{5,11},{6,12},{7,13},{8,14},{9,15},... | collective-permute-start | bytes 24584 | tf_op jit(solution)/shard_map/ppermute | solution.py:342
  23.9 0.4 collective-permute-done.10.refs_12_
  24.3 1.8 %collective-permute-start.7 = (bf16[32,128]{1,0:T(8,128)(2,1)S(1)}, bf16[32,128]{1,0:T(8,128)(2,1)S(1)}, u32[]{:S(2)}, u32[]{:S(2)}) collective-permute-start(bf16[32,128]{1,0:T(8,128)(2,1)S(1)} %constant_dynamic-update-slice_fusion.refs_8_), channel_id=1, source_target_pairs={{0,10},{1,11},{2,12},{3,13},{4,14},{5,15},{6,0},{7,1},{8,2},{9,3},... | collective-permute-start | bytes 24584 | tf_op jit(solution)/shard_map/ppermute | solution.py:342
  26.1 1.2 %collective-permute-done.8.refs_10_ = bf16[32,128]{1,0:T(8,128)(2,1)S(1)} collective-permute-done((bf16[32,128]{1,0:T(8,128)(2,1)S(1)}, bf16[32,128]{1,0:T(8,128)(2,1)S(1)}, u32[]{:S(2)}, u32[]{:S(2)}) %collective-permute-start.8) | collective-permute-done | bytes 8224 | tf_op jit(solution)/shard_map/ppermute | solution.py:342
  27.3 1.3 %collective-permute-done.7.refs_9_ = bf16[32,128]{1,0:T(8,128)(2,1)S(1)} collective-permute-done((bf16[32,128]{1,0:T(8,128)(2,1)S(1)}, bf16[32,128]{1,0:T(8,128)(2,1)S(1)}, u32[]{:S(2)}, u32[]{:S(2)}) %collective-permute-start.7) | collective-permute-done | bytes 8224 | tf_op jit(solution)/shard_map/ppermute | solution.py:342
  28.6 3.8 %shard_map.71 = (bf16[208,1664]{1,0:T(8,128)(2,1)S(1)}, bf16[128,1664]{1,0:T(8,128)(2,1)S(1)}) custom-call(s32[1]{0:T(128)} %bitcast.index_ref.refs_0_, bf16[64,1600]{1,0:T(8,128)(2,1)S(1)} %get-tuple-element.14.refs_1_, bf16[64,1600]{1,0:T(8,128)(2,1)S(1)} %collective-permute-done.2.refs_2_, bf16[64,1600]{1,0:T(8,128)(2,1)S(1)} %collective-permute-done.3.refs_3_, ...), custom_call_target="tpu_custom_call" | custom-call | tf_op jit(solution)/shard_map/pallas_call | solution.py:407
  32.3 3.0 %collective-permute-start.12 = (bf16[128,1664]{1,0:T(8,128)(2,1)S(1)}, bf16[128,1664]{1,0:T(8,128)(2,1)S(1)}, u32[]{:S(2)}, u32[]{:S(2)}) collective-permute-start(bf16[128,1664]{1,0:T(8,128)(2,1)S(1)} %get-tuple-element.21), channel_id=1, source_target_pairs={{0,1},{1,0},{2,3},{3,2},{4,5},{5,4},{6,7},{7,6},{8,9},{9,8},{10,11... | collective-permute-start | bytes 1277960 | tf_op jit(solution)/shard_map/ppermute | solution.py:345
  35.3 0.1 shard_map.70.pseg_ref
  35.4 3.9 %shard_map.72 = (bf16[3,64,2048]{2,1,0:T(8,128)(2,1)S(1)}, bf16[64,512]{1,0:T(8,128)(2,1)}, bf16[2048,1664]{1,0:T(8,128)(2,1)S(1)}) custom-call(f32[336,128]{1,0:T(8,128)S(1)} %get-tuple-element.13.seg_ref.refs_14_, f32[8,128]{1,0:T(8,128)S(1)} %shard_map.70.pseg_ref, bf16[208,1664]{1,0:T(8,128)(2,1)S(1)} %get-tuple-element.18.spec, ...), custom_call_target="tpu_custom_call" | custom-call | tf_op jit(solution)/shard_map/pallas_call | solution.py:423
  39.3 2.8 %shard_map.73 = bf16[5,64,2048]{2,1,0:T(8,128)(2,1)} custom-call(f32[336,128]{1,0:T(8,128)S(1)} %get-tuple-element.13.seg_ref.refs_14_, f32[8,128]{1,0:T(8,128)S(1)} %shard_map.70.pseg_ref, bf16[2048,1664]{1,0:T(8,128)(2,1)S(1)} %get-tuple-element.20.turned, bf16[128,1664]{1,0:T(8,128)(2,1)S(1)} %collective-permute-done.12.take, ...), custom_call_target="tpu_custom_call" | custom-call | tf_op jit(solution)/shard_map/pallas_call | solution.py:437
  (10 shorter events, 0.0 us)
Async XLA Ops:
  0.6 14.0 %collective-permute-start.1 = (bf16[64,1600]{1,0:T(8,128)(2,1)}, bf16[64,1600]{1,0:T(8,128)(2,1)S(1)}, u32[]{:S(2)}, u32[]{:S(2)}) collective-permute-start(bf16[64,1600]{1,0:T(8,128)(2,1)} %own_hbm.3), channel_id=1, source_target_pairs={{0,1},{1,0},{2,3},{3,2},{4,5},{5,4},{6,7},{7,6},{8,9},{9,8},{10,11... | collective-permute-start | bytes 614408 | tf_op jit(solution)/shard_map/ppermute | solution.py:345
  1.4 15.2 %collective-permute-start.3 = (bf16[64,1600]{1,0:T(8,128)(2,1)}, bf16[64,1600]{1,0:T(8,128)(2,1)S(1)}, u32[]{:S(2)}, u32[]{:S(2)}) collective-permute-start(bf16[64,1600]{1,0:T(8,128)(2,1)} %own_hbm.3), channel_id=1, source_target_pairs={{0,12},{1,13},{2,14},{3,15},{4,0},{5,1},{6,2},{7,3},{8,4},{9,5},{1... | collective-permute-start | bytes 614408 | tf_op jit(solution)/shard_map/ppermute | solution.py:342
  4.7 12.4 %collective-permute-start.2 = (bf16[64,1600]{1,0:T(8,128)(2,1)}, bf16[64,1600]{1,0:T(8,128)(2,1)S(1)}, u32[]{:S(2)}, u32[]{:S(2)}) collective-permute-start(bf16[64,1600]{1,0:T(8,128)(2,1)} %own_hbm.3), channel_id=1, source_target_pairs={{0,14},{1,15},{2,0},{3,1},{4,2},{5,3},{6,4},{7,5},{8,6},{9,7},{10,... | collective-permute-start | bytes 614408 | tf_op jit(solution)/shard_map/ppermute | solution.py:342
  5.7 8.9 %collective-permute-start = (bf16[16,1600]{1,0:T(8,128)(2,1)S(1)}, bf16[16,1600]{1,0:T(8,128)(2,1)S(1)}, u32[]{:S(2)}, u32[]{:S(2)}) collective-permute-start(bf16[16,1600]{1,0:T(8,128)(2,1)S(1)} %shard_map.68.edge_ref), channel_id=1, source_target_pairs={{0,11},{1,2},{2,13},{3,4},{4,15},{5,6},{6,1},{7,8},{8,3},{9,10},{1... | collective-permute-start | bytes 153608 | tf_op jit(solution)/shard_map/ppermute | solution.py:359
  16.5 1.2 %collective-permute-start.6 = (bf16[16,128]{1,0:T(8,128)(2,1)S(1)}, bf16[16,128]{1,0:T(8,128)(2,1)S(1)}, u32[]{:S(2)}, u32[]{:S(2)}) collective-permute-start(bf16[16,128]{1,0:T(8,128)(2,1)S(1)} %get-tuple-element.15), channel_id=1, source_target_pairs={{0,1},{1,0},{2,3},{3,2},{4,5},{5,4},{6,7},{7,6},{8,9},{9,8},{10,11... | collective-permute-start | bytes 12296 | tf_op jit(solution)/shard_map/ppermute | solution.py:345
  16.6 12.0 %collective-permute-start.5 = (bf16[64,1600]{1,0:T(8,128)(2,1)S(1)}, bf16[64,1600]{1,0:T(8,128)(2,1)S(1)}, u32[]{:S(2)}, u32[]{:S(2)}) collective-permute-start(bf16[64,1600]{1,0:T(8,128)(2,1)S(1)} %collective-permute-done.3.refs_3_), channel_id=1, source_target_pairs={{0,1},{1,0},{2,3},{3,2},{4,5},{5,4},{6,7},{7,6},{8,9},{9,8},{10,11... | collective-permute-start | bytes 614408 | tf_op jit(solution)/shard_map/ppermute | solution.py:345
  17.1 11.5 %collective-permute-start.4 = (bf16[64,1600]{1,0:T(8,128)(2,1)S(1)}, bf16[64,1600]{1,0:T(8,128)(2,1)S(1)}, u32[]{:S(2)}, u32[]{:S(2)}) collective-permute-start(bf16[64,1600]{1,0:T(8,128)(2,1)S(1)} %collective-permute-done.2.refs_2_), channel_id=1, source_target_pairs={{0,1},{1,0},{2,3},{3,2},{4,5},{5,4},{6,7},{7,6},{8,9},{9,8},{10,11... | collective-permute-start | bytes 614408 | tf_op jit(solution)/shard_map/ppermute | solution.py:345
  17.7 6.1 %collective-permute-start.11 = (bf16[32,128]{1,0:T(8,128)(2,1)S(1)}, bf16[32,128]{1,0:T(8,128)(2,1)S(1)}, u32[]{:S(2)}, u32[]{:S(2)}) collective-permute-start(bf16[32,128]{1,0:T(8,128)(2,1)S(1)} %constant_dynamic-update-slice_fusion.refs_8_), channel_id=1, source_target_pairs={{0,2},{1,3},{2,4},{3,5},{4,6},{5,7},{6,8},{7,9},{8,10},{9,11},{10,... | collective-permute-start | bytes 24584 | tf_op jit(solution)/shard_map/ppermute | solution.py:342
  20.0 4.3 %collective-permute-start.10 = (bf16[32,128]{1,0:T(8,128)(2,1)S(1)}, bf16[32,128]{1,0:T(8,128)(2,1)S(1)}, u32[]{:S(2)}, u32[]{:S(2)}) collective-permute-start(bf16[32,128]{1,0:T(8,128)(2,1)S(1)} %constant_dynamic-update-slice_fusion.refs_8_), channel_id=1, source_target_pairs={{0,4},{1,5},{2,6},{3,7},{4,8},{5,9},{6,10},{7,11},{8,12},{9,13},{1... | collective-permute-start | bytes 24584 | tf_op jit(solution)/shard_map/ppermute | solution.py:342
  20.0 6.1 %collective-permute-start.9 = (bf16[32,128]{1,0:T(8,128)(2,1)S(1)}, bf16[32,128]{1,0:T(8,128)(2,1)S(1)}, u32[]{:S(2)}, u32[]{:S(2)}) collective-permute-start(bf16[32,128]{1,0:T(8,128)(2,1)S(1)} %constant_dynamic-update-slice_fusion.refs_8_), channel_id=1, source_target_pairs={{0,6},{1,7},{2,8},{3,9},{4,10},{5,11},{6,12},{7,13},{8,14},{9,15},... | collective-permute-start | bytes 24584 | tf_op jit(solution)/shard_map/ppermute | solution.py:342
  23.9 3.4 %collective-permute-start.8 = (bf16[32,128]{1,0:T(8,128)(2,1)S(1)}, bf16[32,128]{1,0:T(8,128)(2,1)S(1)}, u32[]{:S(2)}, u32[]{:S(2)}) collective-permute-start(bf16[32,128]{1,0:T(8,128)(2,1)S(1)} %constant_dynamic-update-slice_fusion.refs_8_), channel_id=1, source_target_pairs={{0,8},{1,9},{2,10},{3,11},{4,12},{5,13},{6,14},{7,15},{8,0},{9,1},... | collective-permute-start | bytes 24584 | tf_op jit(solution)/shard_map/ppermute | solution.py:342
  24.3 4.3 %collective-permute-start.7 = (bf16[32,128]{1,0:T(8,128)(2,1)S(1)}, bf16[32,128]{1,0:T(8,128)(2,1)S(1)}, u32[]{:S(2)}, u32[]{:S(2)}) collective-permute-start(bf16[32,128]{1,0:T(8,128)(2,1)S(1)} %constant_dynamic-update-slice_fusion.refs_8_), channel_id=1, source_target_pairs={{0,10},{1,11},{2,12},{3,13},{4,14},{5,15},{6,0},{7,1},{8,2},{9,3},... | collective-permute-start | bytes 24584 | tf_op jit(solution)/shard_map/ppermute | solution.py:342
  32.3 7.0 %collective-permute-start.12 = (bf16[128,1664]{1,0:T(8,128)(2,1)S(1)}, bf16[128,1664]{1,0:T(8,128)(2,1)S(1)}, u32[]{:S(2)}, u32[]{:S(2)}) collective-permute-start(bf16[128,1664]{1,0:T(8,128)(2,1)S(1)} %get-tuple-element.21), channel_id=1, source_target_pairs={{0,1},{1,0},{2,3},{3,2},{4,5},{5,4},{6,7},{7,6},{8,9},{9,8},{10,11... | collective-permute-start | bytes 1277960 | tf_op jit(solution)/shard_map/ppermute | solution.py:345

commit v8 on v7

--- a/solution.py
+++ b/solution.py
@@ -145,10 +145,24 @@
     pseg_ref[BAND + 1 :, :] = jnp.full((8 - BAND - 1, CHUNK), -1.0, f32)
 
 
-def spectra_kernel(pieces, count, *refs):
+def whiten(filt, dft_ref, spec):
+    tiles = COVER // CHUNK - 1
+    tail = None
+    for w in range(W):
+        lhs = jnp.concatenate([filt[w * tiles + q] for q in range(tiles + 1)], axis=1)
+        raw = jnp.dot(lhs, dft_ref[w], preferred_element_type=f32)
+        power = jnp.sum(raw * raw, axis=-1, keepdims=True) * (1.0 / L)
+        whitened = raw * lax.rsqrt(power + 1e-06)
+        head = whitened[:, :CHUNK] if tail is None else tail + whitened[:, :CHUNK]
+        spec[:, w * tiles * CHUNK : (w * tiles + 1) * CHUNK] = head.astype(bf16)
+        spec[:, (w * tiles + 1) * CHUNK : (w + 1) * tiles * CHUNK] = whitened[:, CHUNK : tiles * CHUNK].astype(bf16)
+        tail = whitened[:, tiles * CHUNK :]
+    spec[:, W * tiles * CHUNK :] = tail.astype(bf16)
+
+
+def spectra_kernel(*refs):
     index_ref, own_ref, two_ref, four_ref, sown_ref, stwo_ref, sfour_ref, halo_ref = refs[:8]
-    part_refs, refs = refs[8 : 8 + pieces], refs[8 + pieces :]
-    seg_ref, band_ref, dft_ref, spec, give_ref, rec, masked, filt, line = refs
+    seg_ref, band_ref, dft_ref, spec, give_ref, near_ref, rec, masked, filt, line = refs[8:]
     even = index_ref[0] % 2 == 0
 
     def put(start, rows):
@@ -185,6 +199,34 @@
                 result = result + share[(j - 1) * CB : j * CB, CHUNK:]
             filt[j, i * CB : (i + 1) * CB, :] = result.astype(bf16)
 
+    between = [HALO + r * CB for r in range(1, BAND + 2, 2)]
+
+    def row_at(i, e, j):
+        at = between[i] - HALF + e
+        return rec[j, at : at + 1, :]
+
+    local = filter_rows(row_at, seg_ref, between, line, band_ref)
+    near_ref[...] = jnp.zeros_like(near_ref)
+    for r in range(BAND + 2):
+        for j in range(NCHUNK):
+            if r % 2 == 0:
+                near_ref[j, r : r + 1, :] = filt[j, r // 2 * CB : r // 2 * CB + 1, :]
+            else:
+                near_ref[j, r : r + 1, :] = local[r // 2][j : j + 1].astype(bf16)
+
+    @pl.when(index_ref[0] >= 0)
+    def _():
+        whiten(filt, dft_ref, spec)
+
+    give_ref[...] = jnp.where(even, spec[CB:, :].astype(f32), spec[: 2 * CB, :].astype(f32)).astype(bf16)
+
+
+def turn_kernel(count, *refs):
+    index_ref, seg_ref, pseg_ref, spec, lag_ref, dft_ref, near_ref = refs[:7]
+    part_refs, refs = refs[7:-7], refs[-7:]
+    out_ref, src_ref, turned, totals, swapped, filt, ahead_spec = refs
+    even = index_ref[0] % 2 == 0
+
     rows = []
     for ref in part_refs:
         value = ref[...].astype(f32)
@@ -193,53 +235,19 @@
     lists = count // 2
     skip = lists - len(mine)
     mine, theirs = ([part[0]] + [None] * skip + part[1:] for part in (mine, theirs))
-    between = [HALO + r * CB for r in range(1, BAND + 2, 2)]
-
-    def row_at(i, e, j):
-        at = between[i] - HALF + e
-        return rec[j, at : at + 1, :]
-
-    local = filter_rows(row_at, seg_ref, between, line, band_ref)
-    for r in range(count):
-        if r <= BAND and r % 2 == 0:
-            rows = [filt[j, r // 2 * CB : r // 2 * CB + 1, :] for j in range(NCHUNK)]
-        else:
-            if r <= BAND + 1:
-                value = local[r // 2]
-            elif r % 2 == 0:
-                value = mine[r // 2]
-            else:
-                value = jnp.where(even, theirs[r // 2], theirs[(r // 2 + 1) % lists])
-            rows = [value[j : j + 1].astype(bf16) for j in range(NCHUNK)]
+    filt[:, :SLOT, :] = near_ref[...]
+    for r in range(BAND + 2, count):
+        value = mine[r // 2] if r % 2 == 0 else jnp.where(even, theirs[r // 2], theirs[(r // 2 + 1) % lists])
         for j in range(NCHUNK):
-            filt[j, NEAR * CB + r : NEAR * CB + r + 1, :] = rows[j]
-
-    @pl.when(index_ref[0] >= 0)
-    def _():
-        tiles = COVER // CHUNK - 1
-        tail = None
-        for w in range(W):
-            lhs = jnp.concatenate([filt[w * tiles + q] for q in range(tiles + 1)], axis=1)
-            raw = jnp.dot(lhs, dft_ref[w], preferred_element_type=f32)
-            power = jnp.sum(raw * raw, axis=-1, keepdims=True) * (1.0 / L)
-            whitened = raw * lax.rsqrt(power + 1e-06)
-            head = whitened[:, :CHUNK] if tail is None else tail + whitened[:, :CHUNK]
-            spec[:, w * tiles * CHUNK : (w * tiles + 1) * CHUNK] = head.astype(bf16)
-            spec[:, (w * tiles + 1) * CHUNK : (w + 1) * tiles * CHUNK] = whitened[:, CHUNK : tiles * CHUNK].astype(bf16)
-            tail = whitened[:, tiles * CHUNK :]
-        spec[:, W * tiles * CHUNK :] = tail.astype(bf16)
-
-    give_ref[...] = jnp.where(even, spec[CB : 3 * CB, :].astype(f32), spec[: 2 * CB, :].astype(f32)).astype(bf16)
+            filt[j, r : r + 1, :] = value[j : j + 1].astype(bf16)
+    whiten(filt, dft_ref, ahead_spec)
     row = lax.broadcasted_iota(jnp.int32, (count, count), 0)
     column = lax.broadcasted_iota(jnp.int32, (count, count), 1)
     ahead = row - index_ref[0]
     ahead = jnp.where(ahead < 0, ahead + count, ahead)
     order = jnp.where(ahead == column, 1.0, 0.0).astype(bf16)
-    spec[NEAR * CB :, :] = jnp.dot(order, spec[NEAR * CB :, :], preferred_element_type=f32).astype(bf16)
-
-
-def turn_kernel(seg_ref, pseg_ref, spec, lag_ref, out_ref, src_ref, turned, totals, swapped):
-    count = spec.shape[0] - NEAR * CB
+    src_ref[...] = jnp.dot(order, ahead_spec[...], preferred_element_type=f32).astype(bf16)
+
     own = spec[:CB, :].astype(f32)
     pieces = []
     for w in range(W):
@@ -262,12 +270,7 @@
         )
 
     def write(step, slot):
-        start = step * GROUP
         write_pairs(totals.at[slot], step, own_seg, pseg_ref, out_ref, range(0, BAND + 1, 2))
-        sources = jnp.concatenate(
-            [totals[slot, g * CB : (g + 1) * CB, NEAR * CB :] for g in range(GROUP)], axis=1
-        )
-        src_ref[:, start * count : (start + GROUP) * count] = sources.astype(bf16)
 
     for step in range(LAGS // GROUP):
         multiply(step, step % 2)
@@ -287,7 +290,12 @@
             out_ref[i, :, lanes] = jnp.where(keep, both, 0.0).astype(bf16)
 
 
-def rest_kernel(seg_ref, pseg_ref, turned, take, even_ref, out_hbm, odd_ref, totals, even_sems, odd_sems):
+def rest_kernel(
+    seg_ref, pseg_ref, turned, take, sources, even_ref, out_hbm, src_ref, odd_ref, totals, others, even_sems, odd_sems
+):
+    count = sources.shape[0]
+    others[: 2 * CB, :] = take[...]
+    others[2 * CB :, :] = sources[...]
     early = start_loads(
         tuple((even_ref.at[i], out_hbm.at[k]) for i, k in enumerate(range(0, BAND + 1, 2))), even_sems
     )
@@ -303,11 +311,15 @@
     def multiply(step, slot):
         first = step * GROUP * CB
         totals[slot] = lax.dot_general(
-            turned[first : first + GROUP * CB, :], take[...], (((1,), (1,)), ((), ())), preferred_element_type=f32
+            turned[first : first + GROUP * CB, :], others[...], (((1,), (1,)), ((), ())), preferred_element_type=f32
         )
 
     def write(step, slot):
         write_pairs(totals.at[slot], step, own_seg, pseg_ref, odd_ref, range(1, BAND + 1, 2))
+        products = jnp.concatenate(
+            [totals[slot, g * CB : (g + 1) * CB, 2 * CB :] for g in range(GROUP)], axis=1
+        )
+        src_ref[:, step * GROUP * count : (step + 1) * GROUP * count] = products.astype(bf16)
         for i in range(BAND // 2):
             store(step, i).start()
 
@@ -404,49 +416,56 @@
     sfour, stwo = swap(four), swap(two)
 
     limit = pltpu.CompilerParams(vmem_limit_bytes=MAIN_LIMIT if few else None)
-    spec, give = call(
-        functools.partial(spectra_kernel, len(parts), count),
+    spec, give, near = call(
+        spectra_kernel,
         (
-            jax.ShapeDtypeStruct((NEAR * CB + count, KP), bf16),
+            jax.ShapeDtypeStruct((NEAR * CB, KP), bf16),
             jax.ShapeDtypeStruct((2 * CB, KP), bf16),
+            jax.ShapeDtypeStruct((NCHUNK, SLOT, CHUNK), bf16),
         ),
         [
             pltpu.VMEM((NCHUNK, ROWS + 2 * HALO, CHUNK), f32),
             pltpu.VMEM((2, NCHUNK * CB, SPAN * CHUNK), bf16),
-            pltpu.VMEM((NCHUNK, NEAR * CB + count, CHUNK), bf16),
+            pltpu.VMEM((NCHUNK, NEAR * CB, CHUNK), bf16),
             pltpu.VMEM((NEAR * SLOT, SPAN * CHUNK), f32),
         ],
-        [SMEM] + [VMEM] * (10 + len(parts)),
+        [SMEM] + [VMEM] * 10,
         compiler_params=limit,
-    )(index, own, two, four, sown, stwo, sfour, halo, *parts, segs, band, dft)
+    )(index, own, two, four, sown, stwo, sfour, halo, segs, band, dft)
     take = swap(give)
-    even_blocks, source_out, turned = call(
-        turn_kernel,
+    even_blocks, sources, turned = call(
+        functools.partial(turn_kernel, count),
         (
             jax.ShapeDtypeStruct((NEAR, CB, LAGS * CB), bf16),
-            jax.ShapeDtypeStruct((CB, LAGS * count), bf16),
+            jax.ShapeDtypeStruct((count, KP), bf16),
             jax.ShapeDtypeStruct((LAGS * CB, KP), bf16),
         ),
         [
-            pltpu.VMEM((2, GROUP * CB, NEAR * CB + count), f32),
+            pltpu.VMEM((2, GROUP * CB, NEAR * CB), f32),
             pltpu.VMEM((CB, KP), f32),
+            pltpu.VMEM((NCHUNK, count, CHUNK), bf16),
+            pltpu.VMEM((count, KP), bf16),
         ],
-        [VMEM] * 4,
+        [SMEM] + [VMEM] * (6 + len(parts)),
         compiler_params=limit,
-    )(segs, pseg, spec, lags)
-    stacked = pl.pallas_call(
+    )(index, segs, pseg, spec, lags, dft, near, *parts)
+    stacked, source_out = pl.pallas_call(
         rest_kernel,
-        out_shape=jax.ShapeDtypeStruct((BAND + 1, CB, LAGS * CB), bf16),
-        in_specs=[VMEM] * 5,
-        out_specs=HBM,
+        out_shape=(
+            jax.ShapeDtypeStruct((BAND + 1, CB, LAGS * CB), bf16),
+            jax.ShapeDtypeStruct((CB, LAGS * count), bf16),
+        ),
+        in_specs=[VMEM] * 6,
+        out_specs=(HBM, VMEM),
         scratch_shapes=[
             pltpu.VMEM((BAND // 2, CB, LAGS * CB), bf16),
-            pltpu.VMEM((2, GROUP * CB, 2 * CB), f32),
+            pltpu.VMEM((2, GROUP * CB, 2 * CB + count), f32),
+            pltpu.VMEM((2 * CB + count, KP), bf16),
             pltpu.SemaphoreType.DMA((NEAR,)),
             pltpu.SemaphoreType.DMA((LAGS // GROUP, BAND // 2)),
         ],
         compiler_params=limit,
-    )(segs, pseg, turned, take, even_blocks)
+    )(segs, pseg, turned, take, sources, even_blocks)
     return (jnp.swapaxes(stacked, 0, 1), source_out)
 
 

time: 42.3 us -> 48.6 us (1.15)
  the two profiles are of different devices: /device:TPU:5 before, /device:TPU:0 now
where the time goes in v8:
time: 48.6 us; the launch traced here: 48.4 us
  waiting for transfers between devices  17.8 us (37%)
  starting transfers between devices  16.8 us (35%)
  Pallas kernels  13.1 us (27%)
  between operations  0.71 us (1%)
    ppermute x7, starting transfers between devices, ahead(): lax.ppermute(value, 'fibre', [(i, (i - distance) % count) for i in range(...  13.8 us
    ppermute x7, waiting for transfers between devices, ahead(): lax.ppermute(value, 'fibre', [(i, (i - distance) % count) for i in range(...  11.5 us
    ppermute x1, waiting for transfers between devices, per_device(): halo = lax.ppermute(edge, 'fibre', route)  5.01 us
    pallas_call x1, Pallas kernels, per_device(): pl.pallas_call(rest_kernel, out_shape=(jax.ShapeDtypeStruct((BAND + 1, CB...  3.71 us
    pallas_call x1, Pallas kernels, per_device(): call(spectra_kernel, (jax.ShapeDtypeStruct((NEAR * CB, KP), bf16), jax.Sh...  3.4 us
    pallas_call x1, Pallas kernels, per_device(): call(functools.partial(turn_kernel, count), (jax.ShapeDtypeStruct((NEAR,...  3.26 us
    ppermute x1, starting transfers between devices, per_device(): halo = lax.ppermute(edge, 'fibre', route)  2.43 us
    pallas_call x1, Pallas kernels, per_device(): call(prep_kernel, (jax.ShapeDtypeStruct((SLOT, CHUNK), bf16), jax.ShapeDt...  1.82 us
  transfers between devices with their start and end apart: 13, of which 6 were waited for; matrix products, arithmetic and copies ran while one was open for 0% of the time, Pallas kernels for 12%

profile of v8, /device:TPU:0, one launch (start us, length us, event | category | flops | bytes accessed | tf_op | source)
XLA Modules:
  0.0 48.4 jit_solution(505333589528598610)
XLA Ops:
  0.6 5.1 %collective-permute-start.3 = (bf16[64,1600]{1,0:T(8,128)(2,1)}, bf16[64,1600]{1,0:T(8,128)(2,1)S(1)}, u32[]{:S(2)}, u32[]{:S(2)}) collective-permute-start(bf16[64,1600]{1,0:T(8,128)(2,1)} %own_hbm.3), channel_id=1, source_target_pairs={{0,12},{1,13},{2,14},{3,15},{4,0},{5,1},{6,2},{7,3},{8,4},{9,5},{1... | collective-permute-start | bytes 614408 | tf_op jit(solution)/shard_map/ppermute | solution.py:354
  5.8 1.4 %collective-permute-start.2 = (bf16[64,1600]{1,0:T(8,128)(2,1)}, bf16[64,1600]{1,0:T(8,128)(2,1)S(1)}, u32[]{:S(2)}, u32[]{:S(2)}) collective-permute-start(bf16[64,1600]{1,0:T(8,128)(2,1)} %own_hbm.3), channel_id=1, source_target_pairs={{0,14},{1,15},{2,0},{3,1},{4,2},{5,3},{6,4},{7,5},{8,6},{9,7},{10,... | collective-permute-start | bytes 614408 | tf_op jit(solution)/shard_map/ppermute | solution.py:354
  7.2 0.0 collective-permute-start.1
  7.2 4.5 %collective-permute-done.3.refs_3_ = bf16[64,1600]{1,0:T(8,128)(2,1)S(1)} collective-permute-done((bf16[64,1600]{1,0:T(8,128)(2,1)}, bf16[64,1600]{1,0:T(8,128)(2,1)S(1)}, u32[]{:S(2)}, u32[]{:S(2)}) %collective-permute-start.3) | collective-permute-done | bytes 204832 | tf_op jit(solution)/shard_map/ppermute | solution.py:354
  11.7 0.0 collective-permute-start.5
  11.7 3.4 %collective-permute-done.2.refs_2_ = bf16[64,1600]{1,0:T(8,128)(2,1)S(1)} collective-permute-done((bf16[64,1600]{1,0:T(8,128)(2,1)}, bf16[64,1600]{1,0:T(8,128)(2,1)S(1)}, u32[]{:S(2)}, u32[]{:S(2)}) %collective-permute-start.2) | collective-permute-done | bytes 204832 | tf_op jit(solution)/shard_map/ppermute | solution.py:354
  15.2 0.8 %shard_map.68.edge_ref = bf16[16,1600]{1,0:T(8,128)(2,1)S(1)} custom-call(bf16[64,1600]{1,0:T(8,128)(2,1)} %own_hbm.3), custom_call_target="tpu_custom_call" | custom-call | tf_op jit(solution)/shard_map/pallas_call | solution.py:363
  15.9 2.4 %collective-permute-start = (bf16[16,1600]{1,0:T(8,128)(2,1)S(1)}, bf16[16,1600]{1,0:T(8,128)(2,1)S(1)}, u32[]{:S(2)}, u32[]{:S(2)}) collective-permute-start(bf16[16,1600]{1,0:T(8,128)(2,1)S(1)} %shard_map.68.edge_ref), channel_id=1, source_target_pairs={{0,11},{1,2},{2,13},{3,4},{4,15},{5,6},{6,1},{7,8},{8,3},{9,10},{1... | collective-permute-start | bytes 153608 | tf_op jit(solution)/shard_map/ppermute | solution.py:371
  18.4 5.0 %collective-permute-done.halo_ref.refs_7_ = bf16[16,1600]{1,0:T(8,128)(2,1)S(1)} collective-permute-done((bf16[16,1600]{1,0:T(8,128)(2,1)S(1)}, bf16[16,1600]{1,0:T(8,128)(2,1)S(1)}, u32[]{:S(2)}, u32[]{:S(2)}) %collective-permute-start) | collective-permute-done | bytes 51232 | tf_op jit(solution)/shard_map/ppermute | solution.py:371
  23.4 1.8 %shard_map.69 = (bf16[16,128]{1,0:T(8,128)(2,1)S(1)}, bf16[1152,256]{1,0:T(8,128)(2,1)S(1)}, f32[336,128]{1,0:T(8,128)S(1)}, bf16[64,1600]{1,0:T(8,128)(2,1)S(1)...) custom-call(s32[1]{0:T(128)} %bitcast.index_ref.refs_0_, bf16[16,1600]{1,0:T(8,128)(2,1)S(1)} %shard_map.68.edge_ref, ...), custom_call_target="tpu_custom_call" | custom-call | tf_op jit(solution)/shard_map/pallas_call | solution.py:377
  25.2 3.4 %shard_map.71 = (bf16[192,1664]{1,0:T(8,128)(2,1)S(1)}, bf16[128,1664]{1,0:T(8,128)(2,1)S(1)}, bf16[13,16,128]{2,1,0:T(8,128)(2,1)S(1)}) custom-call(s32[1]{0:T(128)} %bitcast.index_ref.refs_0_, bf16[64,1600]{1,0:T(8,128)(2,1)S(1)} %get-tuple-element.17.refs_1_, bf16[64,1600]{1,0:T(8,128)(2,1)S(1)} %collective-permute-done.2.refs_2_, ...), custom_call_target="tpu_custom_call" | custom-call | tf_op jit(solution)/shard_map/pallas_call | solution.py:419
  28.6 0.1 collective-permute-start.12
  28.7 0.5 %collective-permute-start.6 = (bf16[16,128]{1,0:T(8,128)(2,1)S(1)}, bf16[16,128]{1,0:T(8,128)(2,1)S(1)}, u32[]{:S(2)}, u32[]{:S(2)}) collective-permute-start(bf16[16,128]{1,0:T(8,128)(2,1)S(1)} %get-tuple-element.23), channel_id=1, source_target_pairs={{0,1},{1,0},{2,3},{3,2},{4,5},{5,4},{6,7},{7,6},{8,9},{9,8},{10,11... | collective-permute-start | bytes 12296 | tf_op jit(solution)/shard_map/ppermute | solution.py:357
  29.2 1.3 %collective-permute-done.6 = bf16[16,128]{1,0:T(8,128)(2,1)S(1)} collective-permute-done((bf16[16,128]{1,0:T(8,128)(2,1)S(1)}, bf16[16,128]{1,0:T(8,128)(2,1)S(1)}, u32[]{:S(2)}, u32[]{:S(2)}) %collective-permute-start.6) | collective-permute-done | bytes 4128 | tf_op jit(solution)/shard_map/ppermute | solution.py:357
  30.5 0.1 collective-permute-start.10
  30.6 1.6 %collective-permute-start.9 = (bf16[32,128]{1,0:T(8,128)(2,1)S(1)}, bf16[32,128]{1,0:T(8,128)(2,1)S(1)}, u32[]{:S(2)}, u32[]{:S(2)}) collective-permute-start(bf16[32,128]{1,0:T(8,128)(2,1)S(1)} %constant_dynamic-update-slice_fusion.refs_7_), channel_id=1, source_target_pairs={{0,6},{1,7},{2,8},{3,9},{4,10},{5,11},{6,12},{7,13},{8,14},{9,15},... | collective-permute-start | bytes 24584 | tf_op jit(solution)/shard_map/ppermute | solution.py:354
  32.3 3.7 %collective-permute-start.8 = (bf16[32,128]{1,0:T(8,128)(2,1)S(1)}, bf16[32,128]{1,0:T(8,128)(2,1)S(1)}, u32[]{:S(2)}, u32[]{:S(2)}) collective-permute-start(bf16[32,128]{1,0:T(8,128)(2,1)S(1)} %constant_dynamic-update-slice_fusion.refs_7_), channel_id=1, source_target_pairs={{0,8},{1,9},{2,10},{3,11},{4,12},{5,13},{6,14},{7,15},{8,0},{9,1},... | collective-permute-start | bytes 24584 | tf_op jit(solution)/shard_map/ppermute | solution.py:354
  35.9 0.9 %collective-permute-done.11.refs_12_ = bf16[32,128]{1,0:T(8,128)(2,1)S(1)} collective-permute-done((bf16[32,128]{1,0:T(8,128)(2,1)S(1)}, bf16[32,128]{1,0:T(8,128)(2,1)S(1)}, u32[]{:S(2)}, u32[]{:S(2)}) %collective-permute-start.11) | collective-permute-done | bytes 8224 | tf_op jit(solution)/shard_map/ppermute | solution.py:354
  36.8 1.8 %collective-permute-start.7 = (bf16[32,128]{1,0:T(8,128)(2,1)S(1)}, bf16[32,128]{1,0:T(8,128)(2,1)S(1)}, u32[]{:S(2)}, u32[]{:S(2)}) collective-permute-start(bf16[32,128]{1,0:T(8,128)(2,1)S(1)} %constant_dynamic-update-slice_fusion.refs_7_), channel_id=1, source_target_pairs={{0,10},{1,11},{2,12},{3,13},{4,14},{5,15},{6,0},{7,1},{8,2},{9,3},... | collective-permute-start | bytes 24584 | tf_op jit(solution)/shard_map/ppermute | solution.py:354
  38.6 0.1 shard_map.70.refs_2_.pseg_ref
  38.7 0.0 collective-permute-done.8.refs_9_
  38.8 2.6 %collective-permute-done.7.refs_8_ = bf16[32,128]{1,0:T(8,128)(2,1)S(1)} collective-permute-done((bf16[32,128]{1,0:T(8,128)(2,1)S(1)}, bf16[32,128]{1,0:T(8,128)(2,1)S(1)}, u32[]{:S(2)}, u32[]{:S(2)}) %collective-permute-start.7) | collective-permute-done | bytes 8224 | tf_op jit(solution)/shard_map/ppermute | solution.py:354
  41.4 3.3 %shard_map.72 = (bf16[3,64,2048]{2,1,0:T(8,128)(2,1)S(1)}, bf16[16,1664]{1,0:T(8,128)(2,1)S(1)}, bf16[2048,1664]{1,0:T(8,128)(2,1)S(1)}) custom-call(s32[1]{0:T(128)} %bitcast.index_ref.refs_0_, f32[336,128]{1,0:T(8,128)S(1)} %get-tuple-element.16.seg_ref.refs_8_.refs_1_, f32[8,128]{1,0:T(8,128)S(1)} %shard_map.70.refs_2_.pseg_ref, ...), custom_call_target="tpu_custom_call" | custom-call | tf_op jit(solution)/shard_map/pallas_call | solution.py:436
  44.7 3.7 %shard_map.73 = (bf16[5,64,2048]{2,1,0:T(8,128)(2,1)}, bf16[64,512]{1,0:T(8,128)(2,1)}) custom-call(f32[336,128]{1,0:T(8,128)S(1)} %get-tuple-element.16.seg_ref.refs_8_.refs_1_, f32[8,128]{1,0:T(8,128)S(1)} %shard_map.70.refs_2_.pseg_ref, bf16[2048,1664]{1,0:T(8,128)(2,1)S(1)} %get-tuple-element.24.turned, ...), custom_call_target="tpu_custom_call" | custom-call | tf_op jit(solution)/shard_map/pallas_call | solution.py:452
  (10 shorter events, 0.0 us)
Async XLA Ops:
  0.6 11.1 %collective-permute-start.3 = (bf16[64,1600]{1,0:T(8,128)(2,1)}, bf16[64,1600]{1,0:T(8,128)(2,1)S(1)}, u32[]{:S(2)}, u32[]{:S(2)}) collective-permute-start(bf16[64,1600]{1,0:T(8,128)(2,1)} %own_hbm.3), channel_id=1, source_target_pairs={{0,12},{1,13},{2,14},{3,15},{4,0},{5,1},{6,2},{7,3},{8,4},{9,5},{1... | collective-permute-start | bytes 614408 | tf_op jit(solution)/shard_map/ppermute | solution.py:354
  5.8 9.4 %collective-permute-start.2 = (bf16[64,1600]{1,0:T(8,128)(2,1)}, bf16[64,1600]{1,0:T(8,128)(2,1)S(1)}, u32[]{:S(2)}, u32[]{:S(2)}) collective-permute-start(bf16[64,1600]{1,0:T(8,128)(2,1)} %own_hbm.3), channel_id=1, source_target_pairs={{0,14},{1,15},{2,0},{3,1},{4,2},{5,3},{6,4},{7,5},{8,6},{9,7},{10,... | collective-permute-start | bytes 614408 | tf_op jit(solution)/shard_map/ppermute | solution.py:354
  7.2 16.2 %collective-permute-start.1 = (bf16[64,1600]{1,0:T(8,128)(2,1)}, bf16[64,1600]{1,0:T(8,128)(2,1)S(1)}, u32[]{:S(2)}, u32[]{:S(2)}) collective-permute-start(bf16[64,1600]{1,0:T(8,128)(2,1)} %own_hbm.3), channel_id=1, source_target_pairs={{0,1},{1,0},{2,3},{3,2},{4,5},{5,4},{6,7},{7,6},{8,9},{9,8},{10,11... | collective-permute-start | bytes 614408 | tf_op jit(solution)/shard_map/ppermute | solution.py:357
  11.7 13.5 %collective-permute-start.5 = (bf16[64,1600]{1,0:T(8,128)(2,1)S(1)}, bf16[64,1600]{1,0:T(8,128)(2,1)S(1)}, u32[]{:S(2)}, u32[]{:S(2)}) collective-permute-start(bf16[64,1600]{1,0:T(8,128)(2,1)S(1)} %collective-permute-done.3.refs_3_), channel_id=1, source_target_pairs={{0,1},{1,0},{2,3},{3,2},{4,5},{5,4},{6,7},{7,6},{8,9},{9,8},{10,11... | collective-permute-start | bytes 614408 | tf_op jit(solution)/shard_map/ppermute | solution.py:357
  15.2 10.1 %collective-permute-start.4 = (bf16[64,1600]{1,0:T(8,128)(2,1)S(1)}, bf16[64,1600]{1,0:T(8,128)(2,1)S(1)}, u32[]{:S(2)}, u32[]{:S(2)}) collective-permute-start(bf16[64,1600]{1,0:T(8,128)(2,1)S(1)} %collective-permute-done.2.refs_2_), channel_id=1, source_target_pairs={{0,1},{1,0},{2,3},{3,2},{4,5},{5,4},{6,7},{7,6},{8,9},{9,8},{10,11... | collective-permute-start | bytes 614408 | tf_op jit(solution)/shard_map/ppermute | solution.py:357
  15.9 7.4 %collective-permute-start = (bf16[16,1600]{1,0:T(8,128)(2,1)S(1)}, bf16[16,1600]{1,0:T(8,128)(2,1)S(1)}, u32[]{:S(2)}, u32[]{:S(2)}) collective-permute-start(bf16[16,1600]{1,0:T(8,128)(2,1)S(1)} %shard_map.68.edge_ref), channel_id=1, source_target_pairs={{0,11},{1,2},{2,13},{3,4},{4,15},{5,6},{6,1},{7,8},{8,3},{9,10},{1... | collective-permute-start | bytes 153608 | tf_op jit(solution)/shard_map/ppermute | solution.py:371
  28.6 16.0 %collective-permute-start.12 = (bf16[128,1664]{1,0:T(8,128)(2,1)S(1)}, bf16[128,1664]{1,0:T(8,128)(2,1)S(1)}, u32[]{:S(2)}, u32[]{:S(2)}) collective-permute-start(bf16[128,1664]{1,0:T(8,128)(2,1)S(1)} %get-tuple-element.25), channel_id=1, source_target_pairs={{0,1},{1,0},{2,3},{3,2},{4,5},{5,4},{6,7},{7,6},{8,9},{9,8},{10,11... | collective-permute-start | bytes 1277960 | tf_op jit(solution)/shard_map/ppermute | solution.py:357
  28.7 1.8 %collective-permute-start.6 = (bf16[16,128]{1,0:T(8,128)(2,1)S(1)}, bf16[16,128]{1,0:T(8,128)(2,1)S(1)}, u32[]{:S(2)}, u32[]{:S(2)}) collective-permute-start(bf16[16,128]{1,0:T(8,128)(2,1)S(1)} %get-tuple-element.23), channel_id=1, source_target_pairs={{0,1},{1,0},{2,3},{3,2},{4,5},{5,4},{6,7},{7,6},{8,9},{9,8},{10,11... | collective-permute-start | bytes 12296 | tf_op jit(solution)/shard_map/ppermute | solution.py:357
  30.5 6.3 %collective-permute-start.11 = (bf16[32,128]{1,0:T(8,128)(2,1)S(1)}, bf16[32,128]{1,0:T(8,128)(2,1)S(1)}, u32[]{:S(2)}, u32[]{:S(2)}) collective-permute-start(bf16[32,128]{1,0:T(8,128)(2,1)S(1)} %constant_dynamic-update-slice_fusion.refs_7_), channel_id=1, source_target_pairs={{0,2},{1,3},{2,4},{3,5},{4,6},{5,7},{6,8},{7,9},{8,10},{9,11},{10,... | collective-permute-start | bytes 24584 | tf_op jit(solution)/shard_map/ppermute | solution.py:354
  30.5 8.2 %collective-permute-start.10 = (bf16[32,128]{1,0:T(8,128)(2,1)S(1)}, bf16[32,128]{1,0:T(8,128)(2,1)S(1)}, u32[]{:S(2)}, u32[]{:S(2)}) collective-permute-start(bf16[32,128]{1,0:T(8,128)(2,1)S(1)} %constant_dynamic-update-slice_fusion.refs_7_), channel_id=1, source_target_pairs={{0,4},{1,5},{2,6},{3,7},{4,8},{5,9},{6,10},{7,11},{8,12},{9,13},{1... | collective-permute-start | bytes 24584 | tf_op jit(solution)/shard_map/ppermute | solution.py:354
  30.6 8.1 %collective-permute-start.9 = (bf16[32,128]{1,0:T(8,128)(2,1)S(1)}, bf16[32,128]{1,0:T(8,128)(2,1)S(1)}, u32[]{:S(2)}, u32[]{:S(2)}) collective-permute-start(bf16[32,128]{1,0:T(8,128)(2,1)S(1)} %constant_dynamic-update-slice_fusion.refs_7_), channel_id=1, source_target_pairs={{0,6},{1,7},{2,8},{3,9},{4,10},{5,11},{6,12},{7,13},{8,14},{9,15},... | collective-permute-start | bytes 24584 | tf_op jit(solution)/shard_map/ppermute | solution.py:354
  32.3 6.5 %collective-permute-start.8 = (bf16[32,128]{1,0:T(8,128)(2,1)S(1)}, bf16[32,128]{1,0:T(8,128)(2,1)S(1)}, u32[]{:S(2)}, u32[]{:S(2)}) collective-permute-start(bf16[32,128]{1,0:T(8,128)(2,1)S(1)} %constant_dynamic-update-slice_fusion.refs_7_), channel_id=1, source_target_pairs={{0,8},{1,9},{2,10},{3,11},{4,12},{5,13},{6,14},{7,15},{8,0},{9,1},... | collective-permute-start | bytes 24584 | tf_op jit(solution)/shard_map/ppermute | solution.py:354
  36.8 4.5 %collective-permute-start.7 = (bf16[32,128]{1,0:T(8,128)(2,1)S(1)}, bf16[32,128]{1,0:T(8,128)(2,1)S(1)}, u32[]{:S(2)}, u32[]{:S(2)}) collective-permute-start(bf16[32,128]{1,0:T(8,128)(2,1)S(1)} %constant_dynamic-update-slice_fusion.refs_7_), channel_id=1, source_target_pairs={{0,10},{1,11},{2,12},{3,13},{4,14},{5,15},{6,0},{7,1},{8,2},{9,3},... | collective-permute-start | bytes 24584 | tf_op jit(solution)/shard_map/ppermute | solution.py:354

commit v9 on v8

--- a/solution.py
+++ b/solution.py
@@ -162,7 +162,7 @@
 
 def spectra_kernel(*refs):
     index_ref, own_ref, two_ref, four_ref, sown_ref, stwo_ref, sfour_ref, halo_ref = refs[:8]
-    seg_ref, band_ref, dft_ref, spec, give_ref, near_ref, rec, masked, filt, line = refs[8:]
+    seg_ref, band_ref, dft_ref, spec, give_ref, rec, masked, filt = refs[8:]
     even = index_ref[0] % 2 == 0
 
     def put(start, rows):
@@ -199,21 +199,6 @@
                 result = result + share[(j - 1) * CB : j * CB, CHUNK:]
             filt[j, i * CB : (i + 1) * CB, :] = result.astype(bf16)
 
-    between = [HALO + r * CB for r in range(1, BAND + 2, 2)]
-
-    def row_at(i, e, j):
-        at = between[i] - HALF + e
-        return rec[j, at : at + 1, :]
-
-    local = filter_rows(row_at, seg_ref, between, line, band_ref)
-    near_ref[...] = jnp.zeros_like(near_ref)
-    for r in range(BAND + 2):
-        for j in range(NCHUNK):
-            if r % 2 == 0:
-                near_ref[j, r : r + 1, :] = filt[j, r // 2 * CB : r // 2 * CB + 1, :]
-            else:
-                near_ref[j, r : r + 1, :] = local[r // 2][j : j + 1].astype(bf16)
-
     @pl.when(index_ref[0] >= 0)
     def _():
         whiten(filt, dft_ref, spec)
@@ -221,32 +206,23 @@
     give_ref[...] = jnp.where(even, spec[CB:, :].astype(f32), spec[: 2 * CB, :].astype(f32)).astype(bf16)
 
 
-def turn_kernel(count, *refs):
-    index_ref, seg_ref, pseg_ref, spec, lag_ref, dft_ref, near_ref = refs[:7]
-    part_refs, refs = refs[7:-7], refs[-7:]
-    out_ref, src_ref, turned, totals, swapped, filt, ahead_spec = refs
-    even = index_ref[0] % 2 == 0
-
-    rows = []
-    for ref in part_refs:
-        value = ref[...].astype(f32)
-        rows += [value[at : at + SLOT] for at in range(0, value.shape[0], SLOT)]
-    mine, theirs = rows[::2], rows[1::2]
-    lists = count // 2
-    skip = lists - len(mine)
-    mine, theirs = ([part[0]] + [None] * skip + part[1:] for part in (mine, theirs))
-    filt[:, :SLOT, :] = near_ref[...]
-    for r in range(BAND + 2, count):
-        value = mine[r // 2] if r % 2 == 0 else jnp.where(even, theirs[r // 2], theirs[(r // 2 + 1) % lists])
+def turn_kernel(
+    doubled, index_ref, seg_ref, pseg_ref, spec, lag_ref, dft_ref, low_ref, high_ref,
+    out_ref, src_ref, turned, totals, swapped, filt, found,
+):
+    count = filt.shape[1]
+    for q in range(count):
+        ref, at = (low_ref, q * SLOT) if 2 * q < count else (high_ref, q * SLOT - low_ref.shape[0])
+        rows = ref[at : at + SLOT, :].astype(f32)
         for j in range(NCHUNK):
-            filt[j, r : r + 1, :] = value[j : j + 1].astype(bf16)
-    whiten(filt, dft_ref, ahead_spec)
+            filt[j, q : q + 1, :] = rows[j : j + 1].astype(bf16)
+    whiten(filt, dft_ref, found)
     row = lax.broadcasted_iota(jnp.int32, (count, count), 0)
     column = lax.broadcasted_iota(jnp.int32, (count, count), 1)
-    ahead = row - index_ref[0]
-    ahead = jnp.where(ahead < 0, ahead + count, ahead)
-    order = jnp.where(ahead == column, 1.0, 0.0).astype(bf16)
-    src_ref[...] = jnp.dot(order, ahead_spec[...], preferred_element_type=f32).astype(bf16)
+    if doubled:
+        row = jnp.bitwise_xor(row, index_ref[0])
+    order = jnp.where(row == column, 1.0, 0.0).astype(bf16)
+    src_ref[...] = jnp.dot(order, found[...], preferred_element_type=f32).astype(bf16)
 
     own = spec[:CB, :].astype(f32)
     pieces = []
@@ -291,7 +267,8 @@
 
 
 def rest_kernel(
-    seg_ref, pseg_ref, turned, take, sources, even_ref, out_hbm, src_ref, odd_ref, totals, others, even_sems, odd_sems
+    seg_ref, pseg_ref, turned, take, sources, even_ref, out_hbm, src_hbm,
+    odd_ref, src_ref, totals, others, even_sems, odd_sems, src_sems,
 ):
     count = sources.shape[0]
     others[: 2 * CB, :] = take[...]
@@ -307,6 +284,10 @@
         return pltpu.make_async_copy(
             odd_ref.at[i, :, lanes], out_hbm.at[2 * i + 1, :, lanes], odd_sems.at[step, i]
         )
+
+    def store_sources(step):
+        lanes = pl.ds(step * GROUP * count, GROUP * count)
+        return pltpu.make_async_copy(src_ref.at[:, lanes], src_hbm.at[:, lanes], src_sems.at[step])
 
     def multiply(step, slot):
         first = step * GROUP * CB
@@ -322,6 +303,7 @@
         src_ref[:, step * GROUP * count : (step + 1) * GROUP * count] = products.astype(bf16)
         for i in range(BAND // 2):
             store(step, i).start()
+        store_sources(step).start()
 
     for step in range(steps):
         multiply(step, step % 2)
@@ -331,6 +313,7 @@
     for step in range(steps):
         for i in range(BAND // 2):
             store(step, i).wait()
+        store_sources(step).wait()
     for load in early:
         load.wait()
 
@@ -397,18 +380,17 @@
         stay(lags),
     )
 
-    lists = count // 2
-    pair = jnp.concatenate([source, swap(source)], axis=0)
-    first = BAND // 2 + 1 if lists <= 8 else 1
-    parts = [pair] + [ahead(pair, 2 * s) for s in range(first, min(8, lists))]
-    have = 8
-    while have < lists:
-        known = jnp.concatenate(parts, axis=0)
-        for s in range(1, 8):
-            left = lists - s * have
-            if left > 0:
-                parts.append(ahead(known[: 2 * SLOT * left], 2 * s * have))
-        have = min(8 * have, lists)
+    doubled = count & (count - 1) == 0
+    if doubled:
+        rows, bit = source, 1
+        while bit < count:
+            other = lax.ppermute(rows, "fibre", [(i, i ^ bit) for i in range(count)])
+            halves = (rows, other)
+            if 2 * bit < count:
+                rows = jnp.concatenate(halves, axis=0)
+            bit *= 2
+    else:
+        halves = jnp.split(lax.all_gather(source, "fibre", axis=0, tiled=True), 2, axis=0)
     pseg = call(
         functools.partial(partner_kernel, count), jax.ShapeDtypeStruct((8, CHUNK), f32), (), [SMEM, VMEM],
         compiler_params=pltpu.CompilerParams(vmem_limit_bytes=TABLE_LIMIT),
@@ -416,25 +398,23 @@
     sfour, stwo = swap(four), swap(two)
 
     limit = pltpu.CompilerParams(vmem_limit_bytes=MAIN_LIMIT if few else None)
-    spec, give, near = call(
+    spec, give = call(
         spectra_kernel,
         (
             jax.ShapeDtypeStruct((NEAR * CB, KP), bf16),
             jax.ShapeDtypeStruct((2 * CB, KP), bf16),
-            jax.ShapeDtypeStruct((NCHUNK, SLOT, CHUNK), bf16),
         ),
         [
             pltpu.VMEM((NCHUNK, ROWS + 2 * HALO, CHUNK), f32),
             pltpu.VMEM((2, NCHUNK * CB, SPAN * CHUNK), bf16),
             pltpu.VMEM((NCHUNK, NEAR * CB, CHUNK), bf16),
-            pltpu.VMEM((NEAR * SLOT, SPAN * CHUNK), f32),
         ],
         [SMEM] + [VMEM] * 10,
         compiler_params=limit,
     )(index, own, two, four, sown, stwo, sfour, halo, segs, band, dft)
     take = swap(give)
     even_blocks, sources, turned = call(
-        functools.partial(turn_kernel, count),
+        functools.partial(turn_kernel, doubled),
         (
             jax.ShapeDtypeStruct((NEAR, CB, LAGS * CB), bf16),
             jax.ShapeDtypeStruct((count, KP), bf16),
@@ -446,9 +426,9 @@
             pltpu.VMEM((NCHUNK, count, CHUNK), bf16),
             pltpu.VMEM((count, KP), bf16),
         ],
-        [SMEM] + [VMEM] * (6 + len(parts)),
+        [SMEM] + [VMEM] * 7,
         compiler_params=limit,
-    )(index, segs, pseg, spec, lags, dft, near, *parts)
+    )(index, segs, pseg, spec, lags, dft, *halves)
     stacked, source_out = pl.pallas_call(
         rest_kernel,
         out_shape=(
@@ -456,13 +436,15 @@
             jax.ShapeDtypeStruct((CB, LAGS * count), bf16),
         ),
         in_specs=[VMEM] * 6,
-        out_specs=(HBM, VMEM),
+        out_specs=(HBM, HBM),
         scratch_shapes=[
             pltpu.VMEM((BAND // 2, CB, LAGS * CB), bf16),
+            pltpu.VMEM((CB, LAGS * count), bf16),
             pltpu.VMEM((2, GROUP * CB, 2 * CB + count), f32),
             pltpu.VMEM((2 * CB + count, KP), bf16),
             pltpu.SemaphoreType.DMA((NEAR,)),
             pltpu.SemaphoreType.DMA((LAGS // GROUP, BAND // 2)),
+            pltpu.SemaphoreType.DMA((LAGS // GROUP,)),
         ],
         compiler_params=limit,
     )(segs, pseg, turned, take, sources, even_blocks)

time: 48.6 us -> 39.9 us (0.82)
  waiting for transfers between devices: 17.8 us -> 12.6 us
  starting transfers between devices: 16.8 us -> 13.9 us
  Pallas kernels: 13.1 us -> 12.4 us
    ppermute x7 -> x2, waiting for transfers between devices: 11.5 us -> 0.01 us  [ahead(): lax.ppermute(value, 'fibre', [(i, (i - distance) % count) for i in range(...]
    ppermute x7 -> x2, starting transfers between devices: 13.8 us -> 6.06 us  [ahead(): lax.ppermute(value, 'fibre', [(i, (i - distance) % count) for i in range(...]
    ppermute x0 -> x4, starting transfers between devices: none -> 6.28 us  [per_device(): other = lax.ppermute(rows, 'fibre', [(i, i ^ bit) for i in range(count)])]
    ppermute x0 -> x4, waiting for transfers between devices: none -> 4.38 us  [per_device(): other = lax.ppermute(rows, 'fibre', [(i, i ^ bit) for i in range(count)])]
    ppermute x1, waiting for transfers between devices: 5.01 us -> 8.23 us  [per_device(): halo = lax.ppermute(edge, 'fibre', route)]
    ppermute x1, starting transfers between devices: 2.43 us -> 0.06 us  [per_device(): halo = lax.ppermute(edge, 'fibre', route)]
    ppermute x5 -> x4, waiting for transfers between devices: 1.27 us -> 0.03 us  [swap(): return lax.ppermute(value, 'fibre', [(i, i ^ 1) for i in range(count)])]
    ppermute x5 -> x4, starting transfers between devices: 0.58 us -> 1.5 us  [swap(): return lax.ppermute(value, 'fibre', [(i, i ^ 1) for i in range(count)])]
  transfers between devices with their start and end apart: 13 -> 11, of which waited for: 6 -> 4; matrix products, arithmetic and copies ran while one was open for 0% -> 0% of each run, Pallas kernels for 12% -> 23%
where the time goes in v9:
time: 39.9 us; the launch traced here: 39.7 us
  starting transfers between devices  13.9 us (35%)
  waiting for transfers between devices  12.6 us (32%)
  Pallas kernels  12.4 us (31%)
  between operations  0.71 us (2%)
    ppermute x1, waiting for transfers between devices, per_device(): halo = lax.ppermute(edge, 'fibre', route)  8.23 us
    ppermute x4, starting transfers between devices, per_device(): other = lax.ppermute(rows, 'fibre', [(i, i ^ bit) for i in range(count)])  6.28 us
    ppermute x2, starting transfers between devices, ahead(): lax.ppermute(value, 'fibre', [(i, (i - distance) % count) for i in range(...  6.06 us
    ppermute x4, waiting for transfers between devices, per_device(): other = lax.ppermute(rows, 'fibre', [(i, i ^ bit) for i in range(count)])  4.38 us
    pallas_call x1, Pallas kernels, per_device(): call(functools.partial(turn_kernel, doubled), (jax.ShapeDtypeStruct((NEAR...  3.32 us
    pallas_call x1, Pallas kernels, per_device(): call(spectra_kernel, (jax.ShapeDtypeStruct((NEAR * CB, KP), bf16), jax.Sh...  3.28 us
    pallas_call x1, Pallas kernels, per_device(): pl.pallas_call(rest_kernel, out_shape=(jax.ShapeDtypeStruct((BAND + 1, CB...  3.12 us
    pallas_call x1, Pallas kernels, per_device(): call(prep_kernel, (jax.ShapeDtypeStruct((SLOT, CHUNK), bf16), jax.ShapeDt...  1.82 us
  transfers between devices with their start and end apart: 11, of which 4 were waited for; matrix products, arithmetic and copies ran while one was open for 0% of the time, Pallas kernels for 23%

profile of v9, /device:TPU:0, one launch (start us, length us, event | category | flops | bytes accessed | tf_op | source)
XLA Modules:
  0.0 39.7 jit_solution(7136551878800621175)
XLA Ops:
  0.6 0.6 %collective-permute-start.1 = (bf16[64,1600]{1,0:T(8,128)(2,1)}, bf16[64,1600]{1,0:T(8,128)(2,1)S(1)}, u32[]{:S(2)}, u32[]{:S(2)}) collective-permute-start(bf16[64,1600]{1,0:T(8,128)(2,1)} %own_hbm.3), channel_id=1, source_target_pairs={{0,1},{1,0},{2,3},{3,2},{4,5},{5,4},{6,7},{7,6},{8,9},{9,8},{10,11... | collective-permute-start | bytes 614408 | tf_op jit(solution)/shard_map/ppermute | solution.py:340
  1.2 4.7 %collective-permute-start.3 = (bf16[64,1600]{1,0:T(8,128)(2,1)}, bf16[64,1600]{1,0:T(8,128)(2,1)S(1)}, u32[]{:S(2)}, u32[]{:S(2)}) collective-permute-start(bf16[64,1600]{1,0:T(8,128)(2,1)} %own_hbm.3), channel_id=1, source_target_pairs={{0,12},{1,13},{2,14},{3,15},{4,0},{5,1},{6,2},{7,3},{8,4},{9,5},{1... | collective-permute-start | bytes 614408 | tf_op jit(solution)/shard_map/ppermute | solution.py:337
  5.8 1.4 %collective-permute-start.2 = (bf16[64,1600]{1,0:T(8,128)(2,1)}, bf16[64,1600]{1,0:T(8,128)(2,1)S(1)}, u32[]{:S(2)}, u32[]{:S(2)}) collective-permute-start(bf16[64,1600]{1,0:T(8,128)(2,1)} %own_hbm.3), channel_id=1, source_target_pairs={{0,14},{1,15},{2,0},{3,1},{4,2},{5,3},{6,4},{7,5},{8,6},{9,7},{10,... | collective-permute-start | bytes 614408 | tf_op jit(solution)/shard_map/ppermute | solution.py:337
  7.2 0.8 %shard_map.68.edge_ref = bf16[16,1600]{1,0:T(8,128)(2,1)S(1)} custom-call(bf16[64,1600]{1,0:T(8,128)(2,1)} %own_hbm.3), custom_call_target="tpu_custom_call" | custom-call | tf_op jit(solution)/shard_map/pallas_call | solution.py:346
  8.0 0.1 collective-permute-start
  8.1 8.2 %collective-permute-done.halo_ref.refs_7_ = bf16[16,1600]{1,0:T(8,128)(2,1)S(1)} collective-permute-done((bf16[16,1600]{1,0:T(8,128)(2,1)S(1)}, bf16[16,1600]{1,0:T(8,128)(2,1)S(1)}, u32[]{:S(2)}, u32[]{:S(2)}) %collective-permute-start) | collective-permute-done | bytes 51232 | tf_op jit(solution)/shard_map/ppermute | solution.py:354
  16.4 1.8 %shard_map.69 = (bf16[16,128]{1,0:T(8,128)(2,1)S(1)}, bf16[1152,256]{1,0:T(8,128)(2,1)S(1)}, f32[336,128]{1,0:T(8,128)S(1)}, bf16[64,1600]{1,0:T(8,128)(2,1)S(1)...) custom-call(s32[1]{0:T(128)} %bitcast.index_ref.refs_0_, bf16[16,1600]{1,0:T(8,128)(2,1)S(1)} %shard_map.68.edge_ref, ...), custom_call_target="tpu_custom_call" | custom-call | tf_op jit(solution)/shard_map/pallas_call | solution.py:360
  18.2 0.1 collective-permute-start.6
  18.3 0.5 %collective-permute-start.5 = (bf16[64,1600]{1,0:T(8,128)(2,1)S(1)}, bf16[64,1600]{1,0:T(8,128)(2,1)S(1)}, u32[]{:S(2)}, u32[]{:S(2)}) collective-permute-start(bf16[64,1600]{1,0:T(8,128)(2,1)S(1)} %collective-permute-done.3.refs_3_), channel_id=1, source_target_pairs={{0,1},{1,0},{2,3},{3,2},{4,5},{5,4},{6,7},{7,6},{8,9},{9,8},{10,11... | collective-permute-start | bytes 614408 | tf_op jit(solution)/shard_map/ppermute | solution.py:340
  18.8 0.0 collective-permute-done.2.refs_2_
  18.8 0.1 collective-permute-start.4
  18.9 0.6 %collective-permute-done.6 = bf16[16,128]{1,0:T(8,128)(2,1)S(1)} collective-permute-done((bf16[16,128]{1,0:T(8,128)(2,1)S(1)}, bf16[16,128]{1,0:T(8,128)(2,1)S(1)}, u32[]{:S(2)}, u32[]{:S(2)}) %collective-permute-start.6) | collective-permute-done | bytes 4128 | tf_op jit(solution)/shard_map/ppermute | solution.py:387
  19.4 0.8 %collective-permute-start.7 = (bf16[32,128]{1,0:T(8,128)(2,1)S(1)}, bf16[32,128]{1,0:T(8,128)(2,1)S(1)}, u32[]{:S(2)}, u32[]{:S(2)}) collective-permute-start(bf16[32,128]{1,0:T(8,128)(2,1)S(1)} %pad_maximum_fusion.1), channel_id=1, source_target_pairs={{0,2},{1,3},{2,0},{3,1},{4,6},{5,7},{6,4},{7,5},{8,10},{9,11},{10,... | collective-permute-start | bytes 24584 | tf_op jit(solution)/shard_map/ppermute | solution.py:387
  20.2 0.0 collective-permute-done.5.refs_6_
  20.2 0.0 collective-permute-done.4.refs_5_
  20.2 3.3 %shard_map.71 = (bf16[192,1664]{1,0:T(8,128)(2,1)S(1)}, bf16[128,1664]{1,0:T(8,128)(2,1)S(1)}) custom-call(s32[1]{0:T(128)} %bitcast.index_ref.refs_0_, bf16[64,1600]{1,0:T(8,128)(2,1)S(1)} %get-tuple-element.16.refs_1_, bf16[64,1600]{1,0:T(8,128)(2,1)S(1)} %collective-permute-done.2.refs_2_, bf16[64,1600]{1,0:T(8,128)(2,1)S(1)} %collective-permute-done.3.refs_3_, ...), custom_call_target="tpu_custom_call" | custom-call | tf_op jit(solution)/shard_map/pallas_call | solution.py:401
  23.5 0.4 collective-permute-start.10
  23.9 2.1 %collective-permute-start.8 = (bf16[64,128]{1,0:T(8,128)(2,1)S(1)}, bf16[64,128]{1,0:T(8,128)(2,1)S(1)}, u32[]{:S(2)}, u32[]{:S(2)}) collective-permute-start(bf16[64,128]{1,0:T(8,128)(2,1)S(1)} %pad_maximum_fusion), channel_id=1, source_target_pairs={{0,4},{1,5},{2,6},{3,7},{4,0},{5,1},{6,2},{7,3},{8,12},{9,13},{10,... | collective-permute-start | bytes 49160 | tf_op jit(solution)/shard_map/ppermute | solution.py:387
  26.0 1.7 %collective-permute-done.8 = bf16[64,128]{1,0:T(8,128)(2,1)S(1)} collective-permute-done((bf16[64,128]{1,0:T(8,128)(2,1)S(1)}, bf16[64,128]{1,0:T(8,128)(2,1)S(1)}, u32[]{:S(2)}, u32[]{:S(2)}) %collective-permute-start.8) | collective-permute-done | bytes 16416 | tf_op jit(solution)/shard_map/ppermute | solution.py:387
  27.7 3.3 %collective-permute-start.9 = (bf16[128,128]{1,0:T(8,128)(2,1)S(1)}, bf16[128,128]{1,0:T(8,128)(2,1)S(1)}, u32[]{:S(2)}, u32[]{:S(2)}) collective-permute-start(bf16[128,128]{1,0:T(8,128)(2,1)S(1)} %constant_dynamic-update-slice_fusion.low_ref), channel_id=1, source_target_pairs={{0,8},{1,9},{2,10},{3,11},{4,12},{5,13},{6,14},{7,15},{8,0},{9,1},... | collective-permute-start | bytes 98312 | tf_op jit(solution)/shard_map/ppermute | solution.py:387
  31.0 0.1 shard_map.70.pseg_ref
  31.2 2.1 %collective-permute-done.9.high_ref = bf16[128,128]{1,0:T(8,128)(2,1)S(1)} collective-permute-done((bf16[128,128]{1,0:T(8,128)(2,1)S(1)}, bf16[128,128]{1,0:T(8,128)(2,1)S(1)}, u32[]{:S(2)}, u32[]{:S(2)}) %collective-permute-start.9) | collective-permute-done | bytes 32800 | tf_op jit(solution)/shard_map/ppermute | solution.py:387
  33.3 3.3 %shard_map.72 = (bf16[3,64,2048]{2,1,0:T(8,128)(2,1)S(1)}, bf16[16,1664]{1,0:T(8,128)(2,1)S(1)}, bf16[2048,1664]{1,0:T(8,128)(2,1)S(1)}) custom-call(s32[1]{0:T(128)} %bitcast.index_ref.refs_0_, f32[336,128]{1,0:T(8,128)S(1)} %get-tuple-element.15.seg_ref.refs_8_, f32[8,128]{1,0:T(8,128)S(1)} %shard_map.70.pseg_ref, ...), custom_call_target="tpu_custom_call" | custom-call | tf_op jit(solution)/shard_map/pallas_call | solution.py:416
  36.6 3.1 %shard_map.73 = (bf16[5,64,2048]{2,1,0:T(8,128)(2,1)}, bf16[64,512]{1,0:T(8,128)(2,1)}) custom-call(f32[336,128]{1,0:T(8,128)S(1)} %get-tuple-element.15.seg_ref.refs_8_, f32[8,128]{1,0:T(8,128)S(1)} %shard_map.70.pseg_ref, bf16[2048,1664]{1,0:T(8,128)(2,1)S(1)} %get-tuple-element.22.turned, bf16[128,1664]{1,0:T(8,128)(2,1)S(1)} %collective-permute-done.10.take, ...), custom_call_target="tpu_custom_call" | custom-call | tf_op jit(solution)/shard_map/pallas_call | solution.py:432
  (10 shorter events, 0.0 us)
Async XLA Ops:
  0.6 15.7 %collective-permute-start.1 = (bf16[64,1600]{1,0:T(8,128)(2,1)}, bf16[64,1600]{1,0:T(8,128)(2,1)S(1)}, u32[]{:S(2)}, u32[]{:S(2)}) collective-permute-start(bf16[64,1600]{1,0:T(8,128)(2,1)} %own_hbm.3), channel_id=1, source_target_pairs={{0,1},{1,0},{2,3},{3,2},{4,5},{5,4},{6,7},{7,6},{8,9},{9,8},{10,11... | collective-permute-start | bytes 614408 | tf_op jit(solution)/shard_map/ppermute | solution.py:340
  1.2 17.1 %collective-permute-start.3 = (bf16[64,1600]{1,0:T(8,128)(2,1)}, bf16[64,1600]{1,0:T(8,128)(2,1)S(1)}, u32[]{:S(2)}, u32[]{:S(2)}) collective-permute-start(bf16[64,1600]{1,0:T(8,128)(2,1)} %own_hbm.3), channel_id=1, source_target_pairs={{0,12},{1,13},{2,14},{3,15},{4,0},{5,1},{6,2},{7,3},{8,4},{9,5},{1... | collective-permute-start | bytes 614408 | tf_op jit(solution)/shard_map/ppermute | solution.py:337
  5.8 12.9 %collective-permute-start.2 = (bf16[64,1600]{1,0:T(8,128)(2,1)}, bf16[64,1600]{1,0:T(8,128)(2,1)S(1)}, u32[]{:S(2)}, u32[]{:S(2)}) collective-permute-start(bf16[64,1600]{1,0:T(8,128)(2,1)} %own_hbm.3), channel_id=1, source_target_pairs={{0,14},{1,15},{2,0},{3,1},{4,2},{5,3},{6,4},{7,5},{8,6},{9,7},{10,... | collective-permute-start | bytes 614408 | tf_op jit(solution)/shard_map/ppermute | solution.py:337
  8.0 8.3 %collective-permute-start = (bf16[16,1600]{1,0:T(8,128)(2,1)S(1)}, bf16[16,1600]{1,0:T(8,128)(2,1)S(1)}, u32[]{:S(2)}, u32[]{:S(2)}) collective-permute-start(bf16[16,1600]{1,0:T(8,128)(2,1)S(1)} %shard_map.68.edge_ref), channel_id=1, source_target_pairs={{0,11},{1,2},{2,13},{3,4},{4,15},{5,6},{6,1},{7,8},{8,3},{9,10},{1... | collective-permute-start | bytes 153608 | tf_op jit(solution)/shard_map/ppermute | solution.py:354
  18.2 1.2 %collective-permute-start.6 = (bf16[16,128]{1,0:T(8,128)(2,1)S(1)}, bf16[16,128]{1,0:T(8,128)(2,1)S(1)}, u32[]{:S(2)}, u32[]{:S(2)}) collective-permute-start(bf16[16,128]{1,0:T(8,128)(2,1)S(1)} %get-tuple-element.21), channel_id=1, source_target_pairs={{0,1},{1,0},{2,3},{3,2},{4,5},{5,4},{6,7},{7,6},{8,9},{9,8},{10,11... | collective-permute-start | bytes 12296 | tf_op jit(solution)/shard_map/ppermute | solution.py:387
  18.3 1.9 %collective-permute-start.5 = (bf16[64,1600]{1,0:T(8,128)(2,1)S(1)}, bf16[64,1600]{1,0:T(8,128)(2,1)S(1)}, u32[]{:S(2)}, u32[]{:S(2)}) collective-permute-start(bf16[64,1600]{1,0:T(8,128)(2,1)S(1)} %collective-permute-done.3.refs_3_), channel_id=1, source_target_pairs={{0,1},{1,0},{2,3},{3,2},{4,5},{5,4},{6,7},{7,6},{8,9},{9,8},{10,11... | collective-permute-start | bytes 614408 | tf_op jit(solution)/shard_map/ppermute | solution.py:340
  18.8 1.5 %collective-permute-start.4 = (bf16[64,1600]{1,0:T(8,128)(2,1)S(1)}, bf16[64,1600]{1,0:T(8,128)(2,1)S(1)}, u32[]{:S(2)}, u32[]{:S(2)}) collective-permute-start(bf16[64,1600]{1,0:T(8,128)(2,1)S(1)} %collective-permute-done.2.refs_2_), channel_id=1, source_target_pairs={{0,1},{1,0},{2,3},{3,2},{4,5},{5,4},{6,7},{7,6},{8,9},{9,8},{10,11... | collective-permute-start | bytes 614408 | tf_op jit(solution)/shard_map/ppermute | solution.py:340
  19.4 4.5 %collective-permute-start.7 = (bf16[32,128]{1,0:T(8,128)(2,1)S(1)}, bf16[32,128]{1,0:T(8,128)(2,1)S(1)}, u32[]{:S(2)}, u32[]{:S(2)}) collective-permute-start(bf16[32,128]{1,0:T(8,128)(2,1)S(1)} %pad_maximum_fusion.1), channel_id=1, source_target_pairs={{0,2},{1,3},{2,0},{3,1},{4,6},{5,7},{6,4},{7,5},{8,10},{9,11},{10,... | collective-permute-start | bytes 24584 | tf_op jit(solution)/shard_map/ppermute | solution.py:387
  23.5 13.1 %collective-permute-start.10 = (bf16[128,1664]{1,0:T(8,128)(2,1)S(1)}, bf16[128,1664]{1,0:T(8,128)(2,1)S(1)}, u32[]{:S(2)}, u32[]{:S(2)}) collective-permute-start(bf16[128,1664]{1,0:T(8,128)(2,1)S(1)} %get-tuple-element.23), channel_id=1, source_target_pairs={{0,1},{1,0},{2,3},{3,2},{4,5},{5,4},{6,7},{7,6},{8,9},{9,8},{10,11... | collective-permute-start | bytes 1277960 | tf_op jit(solution)/shard_map/ppermute | solution.py:340
  23.9 3.8 %collective-permute-start.8 = (bf16[64,128]{1,0:T(8,128)(2,1)S(1)}, bf16[64,128]{1,0:T(8,128)(2,1)S(1)}, u32[]{:S(2)}, u32[]{:S(2)}) collective-permute-start(bf16[64,128]{1,0:T(8,128)(2,1)S(1)} %pad_maximum_fusion), channel_id=1, source_target_pairs={{0,4},{1,5},{2,6},{3,7},{4,0},{5,1},{6,2},{7,3},{8,12},{9,13},{10,... | collective-permute-start | bytes 49160 | tf_op jit(solution)/shard_map/ppermute | solution.py:387
  27.7 5.5 %collective-permute-start.9 = (bf16[128,128]{1,0:T(8,128)(2,1)S(1)}, bf16[128,128]{1,0:T(8,128)(2,1)S(1)}, u32[]{:S(2)}, u32[]{:S(2)}) collective-permute-start(bf16[128,128]{1,0:T(8,128)(2,1)S(1)} %constant_dynamic-update-slice_fusion.low_ref), channel_id=1, source_target_pairs={{0,8},{1,9},{2,10},{3,11},{4,12},{5,13},{6,14},{7,15},{8,0},{9,1},... | collective-permute-start | bytes 98312 | tf_op jit(solution)/shard_map/ppermute | solution.py:387

commit v10 on v9

--- a/solution.py
+++ b/solution.py
@@ -206,24 +206,7 @@
     give_ref[...] = jnp.where(even, spec[CB:, :].astype(f32), spec[: 2 * CB, :].astype(f32)).astype(bf16)
 
 
-def turn_kernel(
-    doubled, index_ref, seg_ref, pseg_ref, spec, lag_ref, dft_ref, low_ref, high_ref,
-    out_ref, src_ref, turned, totals, swapped, filt, found,
-):
-    count = filt.shape[1]
-    for q in range(count):
-        ref, at = (low_ref, q * SLOT) if 2 * q < count else (high_ref, q * SLOT - low_ref.shape[0])
-        rows = ref[at : at + SLOT, :].astype(f32)
-        for j in range(NCHUNK):
-            filt[j, q : q + 1, :] = rows[j : j + 1].astype(bf16)
-    whiten(filt, dft_ref, found)
-    row = lax.broadcasted_iota(jnp.int32, (count, count), 0)
-    column = lax.broadcasted_iota(jnp.int32, (count, count), 1)
-    if doubled:
-        row = jnp.bitwise_xor(row, index_ref[0])
-    order = jnp.where(row == column, 1.0, 0.0).astype(bf16)
-    src_ref[...] = jnp.dot(order, found[...], preferred_element_type=f32).astype(bf16)
-
+def turn_kernel(seg_ref, pseg_ref, spec, lag_ref, out_ref, turned, totals, swapped):
     own = spec[:CB, :].astype(f32)
     pieces = []
     for w in range(W):
@@ -267,15 +250,26 @@
 
 
 def rest_kernel(
-    seg_ref, pseg_ref, turned, take, sources, even_ref, out_hbm, src_hbm,
-    odd_ref, src_ref, totals, others, even_sems, odd_sems, src_sems,
+    doubled, index_ref, seg_ref, pseg_ref, turned, take, dft_ref, low_ref, high_ref, even_ref, out_hbm, src_hbm,
+    odd_ref, src_ref, totals, others, filt, found, even_sems, odd_sems, src_sems,
 ):
-    count = sources.shape[0]
-    others[: 2 * CB, :] = take[...]
-    others[2 * CB :, :] = sources[...]
     early = start_loads(
         tuple((even_ref.at[i], out_hbm.at[k]) for i, k in enumerate(range(0, BAND + 1, 2))), even_sems
     )
+    count = filt.shape[1]
+    for q in range(count):
+        ref, at = (low_ref, q * SLOT) if 2 * q < count else (high_ref, q * SLOT - low_ref.shape[0])
+        rows = ref[at : at + SLOT, :].astype(f32)
+        for j in range(NCHUNK):
+            filt[j, q : q + 1, :] = rows[j : j + 1].astype(bf16)
+    whiten(filt, dft_ref, found)
+    row = lax.broadcasted_iota(jnp.int32, (count, count), 0)
+    column = lax.broadcasted_iota(jnp.int32, (count, count), 1)
+    if doubled:
+        row = jnp.bitwise_xor(row, index_ref[0])
+    order = jnp.where(row == column, 1.0, 0.0).astype(bf16)
+    others[2 * CB :, :] = jnp.dot(order, found[...], preferred_element_type=f32).astype(bf16)
+    others[: 2 * CB, :] = take[...]
     own_seg = seg_ref[HALO : HALO + CB, :]
     steps = LAGS // GROUP
 
@@ -413,41 +407,40 @@
         compiler_params=limit,
     )(index, own, two, four, sown, stwo, sfour, halo, segs, band, dft)
     take = swap(give)
-    even_blocks, sources, turned = call(
-        functools.partial(turn_kernel, doubled),
+    even_blocks, turned = call(
+        turn_kernel,
         (
             jax.ShapeDtypeStruct((NEAR, CB, LAGS * CB), bf16),
-            jax.ShapeDtypeStruct((count, KP), bf16),
             jax.ShapeDtypeStruct((LAGS * CB, KP), bf16),
         ),
         [
             pltpu.VMEM((2, GROUP * CB, NEAR * CB), f32),
             pltpu.VMEM((CB, KP), f32),
-            pltpu.VMEM((NCHUNK, count, CHUNK), bf16),
-            pltpu.VMEM((count, KP), bf16),
         ],
-        [SMEM] + [VMEM] * 7,
+        [VMEM] * 4,
         compiler_params=limit,
-    )(index, segs, pseg, spec, lags, dft, *halves)
+    )(segs, pseg, spec, lags)
     stacked, source_out = pl.pallas_call(
-        rest_kernel,
+        functools.partial(rest_kernel, doubled),
         out_shape=(
             jax.ShapeDtypeStruct((BAND + 1, CB, LAGS * CB), bf16),
             jax.ShapeDtypeStruct((CB, LAGS * count), bf16),
         ),
-        in_specs=[VMEM] * 6,
+        in_specs=[SMEM] + [VMEM] * 8,
         out_specs=(HBM, HBM),
         scratch_shapes=[
             pltpu.VMEM((BAND // 2, CB, LAGS * CB), bf16),
             pltpu.VMEM((CB, LAGS * count), bf16),
             pltpu.VMEM((2, GROUP * CB, 2 * CB + count), f32),
             pltpu.VMEM((2 * CB + count, KP), bf16),
+            pltpu.VMEM((NCHUNK, count, CHUNK), bf16),
+            pltpu.VMEM((count, KP), bf16),
             pltpu.SemaphoreType.DMA((NEAR,)),
             pltpu.SemaphoreType.DMA((LAGS // GROUP, BAND // 2)),
             pltpu.SemaphoreType.DMA((LAGS // GROUP,)),
         ],
         compiler_params=limit,
-    )(segs, pseg, turned, take, sources, even_blocks)
+    )(index, segs, pseg, turned, take, dft, *halves, even_blocks)
     return (jnp.swapaxes(stacked, 0, 1), source_out)
 
 

time: 39.9 us -> 38 us (0.952)
  waiting for transfers between devices: 12.6 us -> 10.5 us
    ppermute x4, waiting for transfers between devices: 4.38 us -> 2.28 us  [per_device(): other = lax.ppermute(rows, 'fibre', [(i, i ^ bit) for i in range(count)])]
  transfers between devices with their start and end apart: 11 -> 11, of which waited for: 4 -> 3; matrix products, arithmetic and copies ran while one was open for 0% -> 0% of each run, Pallas kernels for 23% -> 24%
where the time goes in v10:
time: 38 us; the launch traced here: 37.8 us
  starting transfers between devices  13.9 us (37%)
  Pallas kernels  12.6 us (33%)
  waiting for transfers between devices  10.5 us (28%)
  between operations  0.71 us (2%)
    ppermute x1, waiting for transfers between devices, per_device(): halo = lax.ppermute(edge, 'fibre', route)  8.23 us
    ppermute x4, starting transfers between devices, per_device(): other = lax.ppermute(rows, 'fibre', [(i, i ^ bit) for i in range(count)])  6.27 us
    ppermute x2, starting transfers between devices, ahead(): lax.ppermute(value, 'fibre', [(i, (i - distance) % count) for i in range(...  6.06 us
    pallas_call x1, Pallas kernels, per_device(): pl.pallas_call(functools.partial(rest_kernel, doubled), out_shape=(jax.Sh...  3.62 us
    pallas_call x1, Pallas kernels, per_device(): call(spectra_kernel, (jax.ShapeDtypeStruct((NEAR * CB, KP), bf16), jax.Sh...  3.32 us
    pallas_call x1, Pallas kernels, per_device(): call(turn_kernel, (jax.ShapeDtypeStruct((NEAR, CB, LAGS * CB), bf16), jax...  2.96 us
    ppermute x4, waiting for transfers between devices, per_device(): other = lax.ppermute(rows, 'fibre', [(i, i ^ bit) for i in range(count)])  2.28 us
    pallas_call x1, Pallas kernels, per_device(): call(prep_kernel, (jax.ShapeDtypeStruct((SLOT, CHUNK), bf16), jax.ShapeDt...  1.82 us
  transfers between devices with their start and end apart: 11, of which 3 were waited for; matrix products, arithmetic and copies ran while one was open for 0% of the time, Pallas kernels for 24%

profile of v10, /device:TPU:0, one launch (start us, length us, event | category | flops | bytes accessed | tf_op | source)
XLA Modules:
  0.0 37.8 jit_solution(5672968979354692611)
XLA Ops:
  0.6 0.6 %collective-permute-start.1 = (bf16[64,1600]{1,0:T(8,128)(2,1)}, bf16[64,1600]{1,0:T(8,128)(2,1)S(1)}, u32[]{:S(2)}, u32[]{:S(2)}) collective-permute-start(bf16[64,1600]{1,0:T(8,128)(2,1)} %own_hbm.3), channel_id=1, source_target_pairs={{0,1},{1,0},{2,3},{3,2},{4,5},{5,4},{6,7},{7,6},{8,9},{9,8},{10,11... | collective-permute-start | bytes 614408 | tf_op jit(solution)/shard_map/ppermute | solution.py:334
  1.2 4.7 %collective-permute-start.3 = (bf16[64,1600]{1,0:T(8,128)(2,1)}, bf16[64,1600]{1,0:T(8,128)(2,1)S(1)}, u32[]{:S(2)}, u32[]{:S(2)}) collective-permute-start(bf16[64,1600]{1,0:T(8,128)(2,1)} %own_hbm.3), channel_id=1, source_target_pairs={{0,12},{1,13},{2,14},{3,15},{4,0},{5,1},{6,2},{7,3},{8,4},{9,5},{1... | collective-permute-start | bytes 614408 | tf_op jit(solution)/shard_map/ppermute | solution.py:331
  5.8 1.4 %collective-permute-start.2 = (bf16[64,1600]{1,0:T(8,128)(2,1)}, bf16[64,1600]{1,0:T(8,128)(2,1)S(1)}, u32[]{:S(2)}, u32[]{:S(2)}) collective-permute-start(bf16[64,1600]{1,0:T(8,128)(2,1)} %own_hbm.3), channel_id=1, source_target_pairs={{0,14},{1,15},{2,0},{3,1},{4,2},{5,3},{6,4},{7,5},{8,6},{9,7},{10,... | collective-permute-start | bytes 614408 | tf_op jit(solution)/shard_map/ppermute | solution.py:331
  7.2 0.8 %shard_map.68.edge_ref = bf16[16,1600]{1,0:T(8,128)(2,1)S(1)} custom-call(bf16[64,1600]{1,0:T(8,128)(2,1)} %own_hbm.3), custom_call_target="tpu_custom_call" | custom-call | tf_op jit(solution)/shard_map/pallas_call | solution.py:340
  8.0 0.1 collective-permute-start
  8.1 8.2 %collective-permute-done.halo_ref.refs_7_ = bf16[16,1600]{1,0:T(8,128)(2,1)S(1)} collective-permute-done((bf16[16,1600]{1,0:T(8,128)(2,1)S(1)}, bf16[16,1600]{1,0:T(8,128)(2,1)S(1)}, u32[]{:S(2)}, u32[]{:S(2)}) %collective-permute-start) | collective-permute-done | bytes 51232 | tf_op jit(solution)/shard_map/ppermute | solution.py:348
  16.4 1.8 %shard_map.69 = (bf16[16,128]{1,0:T(8,128)(2,1)S(1)}, bf16[1152,256]{1,0:T(8,128)(2,1)S(1)}, f32[336,128]{1,0:T(8,128)S(1)}, bf16[64,1600]{1,0:T(8,128)(2,1)S(1)...) custom-call(s32[1]{0:T(128)} %bitcast.index_ref.refs_0_, bf16[16,1600]{1,0:T(8,128)(2,1)S(1)} %shard_map.68.edge_ref, ...), custom_call_target="tpu_custom_call" | custom-call | tf_op jit(solution)/shard_map/pallas_call | solution.py:354
  18.2 0.1 collective-permute-start.7
  18.3 0.5 %collective-permute-start.5 = (bf16[64,1600]{1,0:T(8,128)(2,1)S(1)}, bf16[64,1600]{1,0:T(8,128)(2,1)S(1)}, u32[]{:S(2)}, u32[]{:S(2)}) collective-permute-start(bf16[64,1600]{1,0:T(8,128)(2,1)S(1)} %collective-permute-done.3.refs_3_), channel_id=1, source_target_pairs={{0,1},{1,0},{2,3},{3,2},{4,5},{5,4},{6,7},{7,6},{8,9},{9,8},{10,11... | collective-permute-start | bytes 614408 | tf_op jit(solution)/shard_map/ppermute | solution.py:334
  18.8 0.0 collective-permute-done.2.refs_2_
  18.8 0.1 collective-permute-start.4
  18.9 0.6 %collective-permute-done.7 = bf16[16,128]{1,0:T(8,128)(2,1)S(1)} collective-permute-done((bf16[16,128]{1,0:T(8,128)(2,1)S(1)}, bf16[16,128]{1,0:T(8,128)(2,1)S(1)}, u32[]{:S(2)}, u32[]{:S(2)}) %collective-permute-start.7) | collective-permute-done | bytes 4128 | tf_op jit(solution)/shard_map/ppermute | solution.py:381
  19.4 0.8 %collective-permute-start.8 = (bf16[32,128]{1,0:T(8,128)(2,1)S(1)}, bf16[32,128]{1,0:T(8,128)(2,1)S(1)}, u32[]{:S(2)}, u32[]{:S(2)}) collective-permute-start(bf16[32,128]{1,0:T(8,128)(2,1)S(1)} %pad_maximum_fusion.1), channel_id=1, source_target_pairs={{0,2},{1,3},{2,0},{3,1},{4,6},{5,7},{6,4},{7,5},{8,10},{9,11},{10,... | collective-permute-start | bytes 24584 | tf_op jit(solution)/shard_map/ppermute | solution.py:381
  20.2 0.0 collective-permute-done.5.refs_6_
  20.2 0.0 collective-permute-done.4.refs_5_
  20.2 3.3 %shard_map.71 = (bf16[192,1664]{1,0:T(8,128)(2,1)S(1)}, bf16[128,1664]{1,0:T(8,128)(2,1)S(1)}) custom-call(s32[1]{0:T(128)} %bitcast.index_ref.refs_0_, bf16[64,1600]{1,0:T(8,128)(2,1)S(1)} %get-tuple-element.15.refs_1_, bf16[64,1600]{1,0:T(8,128)(2,1)S(1)} %collective-permute-done.2.refs_2_, bf16[64,1600]{1,0:T(8,128)(2,1)S(1)} %collective-permute-done.3.refs_3_, ...), custom_call_target="tpu_custom_call" | custom-call | tf_op jit(solution)/shard_map/pallas_call | solution.py:395
  23.6 0.4 collective-permute-start.6
  23.9 0.0 collective-permute-done.8
  23.9 2.1 %collective-permute-start.9 = (bf16[64,128]{1,0:T(8,128)(2,1)S(1)}, bf16[64,128]{1,0:T(8,128)(2,1)S(1)}, u32[]{:S(2)}, u32[]{:S(2)}) collective-permute-start(bf16[64,128]{1,0:T(8,128)(2,1)S(1)} %pad_maximum_fusion), channel_id=1, source_target_pairs={{0,4},{1,5},{2,6},{3,7},{4,0},{5,1},{6,2},{7,3},{8,12},{9,13},{10,... | collective-permute-start | bytes 49160 | tf_op jit(solution)/shard_map/ppermute | solution.py:381
  26.0 1.7 %collective-permute-done.9 = bf16[64,128]{1,0:T(8,128)(2,1)S(1)} collective-permute-done((bf16[64,128]{1,0:T(8,128)(2,1)S(1)}, bf16[64,128]{1,0:T(8,128)(2,1)S(1)}, u32[]{:S(2)}, u32[]{:S(2)}) %collective-permute-start.9) | collective-permute-done | bytes 16416 | tf_op jit(solution)/shard_map/ppermute | solution.py:381
  27.8 3.3 %collective-permute-start.10 = (bf16[128,128]{1,0:T(8,128)(2,1)S(1)}, bf16[128,128]{1,0:T(8,128)(2,1)S(1)}, u32[]{:S(2)}, u32[]{:S(2)}) collective-permute-start(bf16[128,128]{1,0:T(8,128)(2,1)S(1)} %constant_dynamic-update-slice_fusion.low_ref), channel_id=1, source_target_pairs={{0,8},{1,9},{2,10},{3,11},{4,12},{5,13},{6,14},{7,15},{8,0},{9,1},... | collective-permute-start | bytes 98312 | tf_op jit(solution)/shard_map/ppermute | solution.py:381
  31.1 0.1 shard_map.70.pseg_ref
  31.2 3.0 %shard_map.72 = (bf16[3,64,2048]{2,1,0:T(8,128)(2,1)S(1)}, bf16[2048,1664]{1,0:T(8,128)(2,1)S(1)}) custom-call(f32[336,128]{1,0:T(8,128)S(1)} %get-tuple-element.14.seg_ref.refs_8_, f32[8,128]{1,0:T(8,128)S(1)} %shard_map.70.pseg_ref, bf16[192,1664]{1,0:T(8,128)(2,1)S(1)} %get-tuple-element.18.spec, f32[2,32,1664]{2,1,0:T(8,128)S(1)} %get-tuple-element.19.lag_ref), custom_call_target="tpu_custom_call" | custom-call | tf_op jit(solution)/shard_map/pallas_call | solution.py:410
  34.2 3.6 %shard_map.73 = (bf16[5,64,2048]{2,1,0:T(8,128)(2,1)}, bf16[64,512]{1,0:T(8,128)(2,1)}) custom-call(s32[1]{0:T(128)} %bitcast.index_ref.refs_0_, f32[336,128]{1,0:T(8,128)S(1)} %get-tuple-element.14.seg_ref.refs_8_, f32[8,128]{1,0:T(8,128)S(1)} %shard_map.70.pseg_ref, bf16[2048,1664]{1,0:T(8,128)(2,1)S(1)} %get-tuple-element.20.turned, ...), custom_call_target="tpu_custom_call" | custom-call | tf_op jit(solution)/shard_map/pallas_call | solution.py:423
  (10 shorter events, 0.0 us)
Async XLA Ops:
  0.6 15.7 %collective-permute-start.1 = (bf16[64,1600]{1,0:T(8,128)(2,1)}, bf16[64,1600]{1,0:T(8,128)(2,1)S(1)}, u32[]{:S(2)}, u32[]{:S(2)}) collective-permute-start(bf16[64,1600]{1,0:T(8,128)(2,1)} %own_hbm.3), channel_id=1, source_target_pairs={{0,1},{1,0},{2,3},{3,2},{4,5},{5,4},{6,7},{7,6},{8,9},{9,8},{10,11... | collective-permute-start | bytes 614408 | tf_op jit(solution)/shard_map/ppermute | solution.py:334
  1.2 17.1 %collective-permute-start.3 = (bf16[64,1600]{1,0:T(8,128)(2,1)}, bf16[64,1600]{1,0:T(8,128)(2,1)S(1)}, u32[]{:S(2)}, u32[]{:S(2)}) collective-permute-start(bf16[64,1600]{1,0:T(8,128)(2,1)} %own_hbm.3), channel_id=1, source_target_pairs={{0,12},{1,13},{2,14},{3,15},{4,0},{5,1},{6,2},{7,3},{8,4},{9,5},{1... | collective-permute-start | bytes 614408 | tf_op jit(solution)/shard_map/ppermute | solution.py:331
  5.8 12.9 %collective-permute-start.2 = (bf16[64,1600]{1,0:T(8,128)(2,1)}, bf16[64,1600]{1,0:T(8,128)(2,1)S(1)}, u32[]{:S(2)}, u32[]{:S(2)}) collective-permute-start(bf16[64,1600]{1,0:T(8,128)(2,1)} %own_hbm.3), channel_id=1, source_target_pairs={{0,14},{1,15},{2,0},{3,1},{4,2},{5,3},{6,4},{7,5},{8,6},{9,7},{10,... | collective-permute-start | bytes 614408 | tf_op jit(solution)/shard_map/ppermute | solution.py:331
  8.0 8.3 %collective-permute-start = (bf16[16,1600]{1,0:T(8,128)(2,1)S(1)}, bf16[16,1600]{1,0:T(8,128)(2,1)S(1)}, u32[]{:S(2)}, u32[]{:S(2)}) collective-permute-start(bf16[16,1600]{1,0:T(8,128)(2,1)S(1)} %shard_map.68.edge_ref), channel_id=1, source_target_pairs={{0,11},{1,2},{2,13},{3,4},{4,15},{5,6},{6,1},{7,8},{8,3},{9,10},{1... | collective-permute-start | bytes 153608 | tf_op jit(solution)/shard_map/ppermute | solution.py:348
  18.2 1.2 %collective-permute-start.7 = (bf16[16,128]{1,0:T(8,128)(2,1)S(1)}, bf16[16,128]{1,0:T(8,128)(2,1)S(1)}, u32[]{:S(2)}, u32[]{:S(2)}) collective-permute-start(bf16[16,128]{1,0:T(8,128)(2,1)S(1)} %get-tuple-element.22), channel_id=1, source_target_pairs={{0,1},{1,0},{2,3},{3,2},{4,5},{5,4},{6,7},{7,6},{8,9},{9,8},{10,11... | collective-permute-start | bytes 12296 | tf_op jit(solution)/shard_map/ppermute | solution.py:381
  18.3 1.9 %collective-permute-start.5 = (bf16[64,1600]{1,0:T(8,128)(2,1)S(1)}, bf16[64,1600]{1,0:T(8,128)(2,1)S(1)}, u32[]{:S(2)}, u32[]{:S(2)}) collective-permute-start(bf16[64,1600]{1,0:T(8,128)(2,1)S(1)} %collective-permute-done.3.refs_3_), channel_id=1, source_target_pairs={{0,1},{1,0},{2,3},{3,2},{4,5},{5,4},{6,7},{7,6},{8,9},{9,8},{10,11... | collective-permute-start | bytes 614408 | tf_op jit(solution)/shard_map/ppermute | solution.py:334
  18.8 1.5 %collective-permute-start.4 = (bf16[64,1600]{1,0:T(8,128)(2,1)S(1)}, bf16[64,1600]{1,0:T(8,128)(2,1)S(1)}, u32[]{:S(2)}, u32[]{:S(2)}) collective-permute-start(bf16[64,1600]{1,0:T(8,128)(2,1)S(1)} %collective-permute-done.2.refs_2_), channel_id=1, source_target_pairs={{0,1},{1,0},{2,3},{3,2},{4,5},{5,4},{6,7},{7,6},{8,9},{9,8},{10,11... | collective-permute-start | bytes 614408 | tf_op jit(solution)/shard_map/ppermute | solution.py:334
  19.4 4.5 %collective-permute-start.8 = (bf16[32,128]{1,0:T(8,128)(2,1)S(1)}, bf16[32,128]{1,0:T(8,128)(2,1)S(1)}, u32[]{:S(2)}, u32[]{:S(2)}) collective-permute-start(bf16[32,128]{1,0:T(8,128)(2,1)S(1)} %pad_maximum_fusion.1), channel_id=1, source_target_pairs={{0,2},{1,3},{2,0},{3,1},{4,6},{5,7},{6,4},{7,5},{8,10},{9,11},{10,... | collective-permute-start | bytes 24584 | tf_op jit(solution)/shard_map/ppermute | solution.py:381
  23.6 10.6 %collective-permute-start.6 = (bf16[128,1664]{1,0:T(8,128)(2,1)S(1)}, bf16[128,1664]{1,0:T(8,128)(2,1)S(1)}, u32[]{:S(2)}, u32[]{:S(2)}) collective-permute-start(bf16[128,1664]{1,0:T(8,128)(2,1)S(1)} %get-tuple-element.21), channel_id=1, source_target_pairs={{0,1},{1,0},{2,3},{3,2},{4,5},{5,4},{6,7},{7,6},{8,9},{9,8},{10,11... | collective-permute-start | bytes 1277960 | tf_op jit(solution)/shard_map/ppermute | solution.py:334
  23.9 3.8 %collective-permute-start.9 = (bf16[64,128]{1,0:T(8,128)(2,1)S(1)}, bf16[64,128]{1,0:T(8,128)(2,1)S(1)}, u32[]{:S(2)}, u32[]{:S(2)}) collective-permute-start(bf16[64,128]{1,0:T(8,128)(2,1)S(1)} %pad_maximum_fusion), channel_id=1, source_target_pairs={{0,4},{1,5},{2,6},{3,7},{4,0},{5,1},{6,2},{7,3},{8,12},{9,13},{10,... | collective-permute-start | bytes 49160 | tf_op jit(solution)/shard_map/ppermute | solution.py:381
  27.8 6.4 %collective-permute-start.10 = (bf16[128,128]{1,0:T(8,128)(2,1)S(1)}, bf16[128,128]{1,0:T(8,128)(2,1)S(1)}, u32[]{:S(2)}, u32[]{:S(2)}) collective-permute-start(bf16[128,128]{1,0:T(8,128)(2,1)S(1)} %constant_dynamic-update-slice_fusion.low_ref), channel_id=1, source_target_pairs={{0,8},{1,9},{2,10},{3,11},{4,12},{5,13},{6,14},{7,15},{8,0},{9,1},... | collective-permute-start | bytes 98312 | tf_op jit(solution)/shard_map/ppermute | solution.py:381

commit v11 on v10

--- a/solution.py
+++ b/solution.py
@@ -100,12 +100,10 @@
 
 
 def prep_kernel(
-    index_ref, edge_ref, halo_ref, sown_ref, taps_hbm, ids_hbm, own_hbm, dft_hbm, lag_hbm,
-    source_ref, band_ref, seg_ref, own_ref, dft_ref, lag_ref, taps_ref, ids_ref, line, sems,
+    index_ref, edge_ref, halo_ref, sown_ref, taps_hbm, ids_hbm, own_hbm,
+    source_ref, band_ref, seg_ref, own_ref, taps_ref, ids_ref, line, sems,
 ):
-    loads = start_loads(
-        ((taps_hbm, taps_ref), (ids_hbm, ids_ref), (own_hbm, own_ref), (dft_hbm, dft_ref), (lag_hbm, lag_ref)), sems
-    )
+    loads = start_loads(((taps_hbm, taps_ref), (ids_hbm, ids_ref), (own_hbm, own_ref)), sems)
     device = index_ref[0]
     total = ids_ref.shape[1]
     loads[0].wait()
@@ -162,7 +160,8 @@
 
 def spectra_kernel(*refs):
     index_ref, own_ref, two_ref, four_ref, sown_ref, stwo_ref, sfour_ref, halo_ref = refs[:8]
-    seg_ref, band_ref, dft_ref, spec, give_ref, rec, masked, filt = refs[8:]
+    seg_ref, band_ref, dft_hbm, lag_hbm, spec, give_ref, dft_ref, lag_ref, rec, masked, filt, sems = refs[8:]
+    loads = start_loads(((dft_hbm, dft_ref), (lag_hbm, lag_ref)), sems)
     even = index_ref[0] % 2 == 0
 
     def put(start, rows):
@@ -198,6 +197,9 @@
             if j:
                 result = result + share[(j - 1) * CB : j * CB, CHUNK:]
             filt[j, i * CB : (i + 1) * CB, :] = result.astype(bf16)
+
+    for load in loads:
+        load.wait()
 
     @pl.when(index_ref[0] >= 0)
     def _():
@@ -351,27 +353,24 @@
     two = ahead(records, 2)
 
     dft, lags = dft_tables(), lag_tables()
-    source, band, segs, own, dft, lags = call(
+    source, band, segs, own = call(
         prep_kernel,
         (
             jax.ShapeDtypeStruct((SLOT, CHUNK), bf16),
             jax.ShapeDtypeStruct((SPAN * CHUNK, 2 * CHUNK), bf16),
             jax.ShapeDtypeStruct((ROWS + 2 * HALO, CHUNK), f32),
             jax.ShapeDtypeStruct(records.shape, bf16),
-            jax.ShapeDtypeStruct(dft.shape, bf16),
-            jax.ShapeDtypeStruct(lags.shape, f32),
         ),
         [
             pltpu.VMEM(filter_taps.shape, bf16),
             pltpu.VMEM((1,) + segment_ids.shape, jnp.int32),
             pltpu.VMEM((SLOT, SPAN * CHUNK), f32),
-            pltpu.SemaphoreType.DMA((5,)),
+            pltpu.SemaphoreType.DMA((3,)),
         ],
-        [SMEM] + [VMEM] * 3 + [HBM] * 5,
+        [SMEM] + [VMEM] * 3 + [HBM] * 3,
         compiler_params=pltpu.CompilerParams(vmem_limit_bytes=PREP_LIMIT if few else None),
     )(
-        index, edge, halo, sown, stay(filter_taps), stay(segment_ids.reshape(1, -1)), stay(records), stay(dft),
-        stay(lags),
+        index, edge, halo, sown, stay(filter_taps), stay(segment_ids.reshape(1, -1)), stay(records),
     )
 
     doubled = count & (count - 1) == 0
@@ -392,20 +391,23 @@
     sfour, stwo = swap(four), swap(two)
 
     limit = pltpu.CompilerParams(vmem_limit_bytes=MAIN_LIMIT if few else None)
-    spec, give = call(
+    spec, give, dft, lags = call(
         spectra_kernel,
         (
             jax.ShapeDtypeStruct((NEAR * CB, KP), bf16),
             jax.ShapeDtypeStruct((2 * CB, KP), bf16),
+            jax.ShapeDtypeStruct(dft.shape, dft.dtype),
+            jax.ShapeDtypeStruct(lags.shape, lags.dtype),
         ),
         [
             pltpu.VMEM((NCHUNK, ROWS + 2 * HALO, CHUNK), f32),
             pltpu.VMEM((2, NCHUNK * CB, SPAN * CHUNK), bf16),
             pltpu.VMEM((NCHUNK, NEAR * CB, CHUNK), bf16),
+            pltpu.SemaphoreType.DMA((2,)),
         ],
-        [SMEM] + [VMEM] * 10,
+        [SMEM] + [VMEM] * 9 + [HBM] * 2,
         compiler_params=limit,
-    )(index, own, two, four, sown, stwo, sfour, halo, segs, band, dft)
+    )(index, own, two, four, sown, stwo, sfour, halo, segs, band, stay(dft), stay(lags))
     take = swap(give)
     even_blocks, turned = call(
         turn_kernel,

time: 38 us -> 37.7 us (level)
  transfers between devices with their start and end apart: 11 -> 11, of which waited for: 3 -> 3; matrix products, arithmetic and copies ran while one was open for 0% -> 0% of each run, Pallas kernels for 24% -> 23%
where the time goes in v11:
time: 37.7 us; the launch traced here: 37.5 us
  starting transfers between devices  13.9 us (37%)
  Pallas kernels  12.3 us (33%)
  waiting for transfers between devices  10.5 us (28%)
  between operations  0.71 us (2%)
    ppermute x1, waiting for transfers between devices, per_device(): halo = lax.ppermute(edge, 'fibre', route)  8.23 us
    ppermute x4, starting transfers between devices, per_device(): other = lax.ppermute(rows, 'fibre', [(i, i ^ bit) for i in range(count)])  6.28 us
    ppermute x2, starting transfers between devices, ahead(): lax.ppermute(value, 'fibre', [(i, (i - distance) % count) for i in range(...  6.06 us
    pallas_call x1, Pallas kernels, per_device(): pl.pallas_call(functools.partial(rest_kernel, doubled), out_shape=(jax.Sh...  3.61 us
    pallas_call x1, Pallas kernels, per_device(): call(spectra_kernel, (jax.ShapeDtypeStruct((NEAR * CB, KP), bf16), jax.Sh...  3.36 us
    pallas_call x1, Pallas kernels, per_device(): call(turn_kernel, (jax.ShapeDtypeStruct((NEAR, CB, LAGS * CB), bf16), jax...  2.9 us
    ppermute x4, waiting for transfers between devices, per_device(): other = lax.ppermute(rows, 'fibre', [(i, i ^ bit) for i in range(count)])  2.28 us
    pallas_call x1, Pallas kernels, per_device(): call(prep_kernel, (jax.ShapeDtypeStruct((SLOT, CHUNK), bf16), jax.ShapeDt...  1.55 us
  transfers between devices with their start and end apart: 11, of which 3 were waited for; matrix products, arithmetic and copies ran while one was open for 0% of the time, Pallas kernels for 23%

profile of v11, /device:TPU:0, one launch (start us, length us, event | category | flops | bytes accessed | tf_op | source)
XLA Modules:
  0.0 37.5 jit_solution(1288912302657443697)
XLA Ops:
  0.6 0.6 %collective-permute-start.1 = (bf16[64,1600]{1,0:T(8,128)(2,1)}, bf16[64,1600]{1,0:T(8,128)(2,1)S(1)}, u32[]{:S(2)}, u32[]{:S(2)}) collective-permute-start(bf16[64,1600]{1,0:T(8,128)(2,1)} %own_hbm.3), channel_id=1, source_target_pairs={{0,1},{1,0},{2,3},{3,2},{4,5},{5,4},{6,7},{7,6},{8,9},{9,8},{10,11... | collective-permute-start | bytes 614408 | tf_op jit(solution)/shard_map/ppermute | solution.py:336
  1.2 4.7 %collective-permute-start.3 = (bf16[64,1600]{1,0:T(8,128)(2,1)}, bf16[64,1600]{1,0:T(8,128)(2,1)S(1)}, u32[]{:S(2)}, u32[]{:S(2)}) collective-permute-start(bf16[64,1600]{1,0:T(8,128)(2,1)} %own_hbm.3), channel_id=1, source_target_pairs={{0,12},{1,13},{2,14},{3,15},{4,0},{5,1},{6,2},{7,3},{8,4},{9,5},{1... | collective-permute-start | bytes 614408 | tf_op jit(solution)/shard_map/ppermute | solution.py:333
  5.8 1.4 %collective-permute-start.2 = (bf16[64,1600]{1,0:T(8,128)(2,1)}, bf16[64,1600]{1,0:T(8,128)(2,1)S(1)}, u32[]{:S(2)}, u32[]{:S(2)}) collective-permute-start(bf16[64,1600]{1,0:T(8,128)(2,1)} %own_hbm.3), channel_id=1, source_target_pairs={{0,14},{1,15},{2,0},{3,1},{4,2},{5,3},{6,4},{7,5},{8,6},{9,7},{10,... | collective-permute-start | bytes 614408 | tf_op jit(solution)/shard_map/ppermute | solution.py:333
  7.2 0.8 %shard_map.68.edge_ref = bf16[16,1600]{1,0:T(8,128)(2,1)S(1)} custom-call(bf16[64,1600]{1,0:T(8,128)(2,1)} %own_hbm.3), custom_call_target="tpu_custom_call" | custom-call | tf_op jit(solution)/shard_map/pallas_call | solution.py:342
  8.0 0.1 collective-permute-start
  8.1 8.2 %collective-permute-done.halo_ref.refs_7_ = bf16[16,1600]{1,0:T(8,128)(2,1)S(1)} collective-permute-done((bf16[16,1600]{1,0:T(8,128)(2,1)S(1)}, bf16[16,1600]{1,0:T(8,128)(2,1)S(1)}, u32[]{:S(2)}, u32[]{:S(2)}) %collective-permute-start) | collective-permute-done | bytes 51232 | tf_op jit(solution)/shard_map/ppermute | solution.py:350
  16.3 0.0 collective-permute-done.1.sown_ref.refs_4_
  16.4 1.6 %shard_map.69 = (bf16[16,128]{1,0:T(8,128)(2,1)S(1)}, bf16[1152,256]{1,0:T(8,128)(2,1)S(1)}, f32[336,128]{1,0:T(8,128)S(1)}, bf16[64,1600]{1,0:T(8,128)(2,1)S(1)}) custom-call(s32[1]{0:T(128)} %bitcast.index_ref.refs_0_, bf16[16,1600]{1,0:T(8,128)(2,1)S(1)} %shard_map.68.edge_ref, bf16[16,1600]{1,0:T(8,128)(2,1)S(1)} %collective-permute-done.halo_ref.refs_7_, ...), custom_call_target="tpu_custom_call" | custom-call | tf_op jit(solution)/shard_map/pallas_call | solution.py:356
  17.9 0.1 collective-permute-start.7
  18.0 0.5 %collective-permute-start.5 = (bf16[64,1600]{1,0:T(8,128)(2,1)S(1)}, bf16[64,1600]{1,0:T(8,128)(2,1)S(1)}, u32[]{:S(2)}, u32[]{:S(2)}) collective-permute-start(bf16[64,1600]{1,0:T(8,128)(2,1)S(1)} %collective-permute-done.3.refs_3_), channel_id=1, source_target_pairs={{0,1},{1,0},{2,3},{3,2},{4,5},{5,4},{6,7},{7,6},{8,9},{9,8},{10,11... | collective-permute-start | bytes 614408 | tf_op jit(solution)/shard_map/ppermute | solution.py:336
  18.5 0.0 collective-permute-done.2.refs_2_
  18.5 0.1 collective-permute-start.4
  18.6 0.6 %collective-permute-done.7 = bf16[16,128]{1,0:T(8,128)(2,1)S(1)} collective-permute-done((bf16[16,128]{1,0:T(8,128)(2,1)S(1)}, bf16[16,128]{1,0:T(8,128)(2,1)S(1)}, u32[]{:S(2)}, u32[]{:S(2)}) %collective-permute-start.7) | collective-permute-done | bytes 4128 | tf_op jit(solution)/shard_map/ppermute | solution.py:380
  19.1 0.8 %collective-permute-start.8 = (bf16[32,128]{1,0:T(8,128)(2,1)S(1)}, bf16[32,128]{1,0:T(8,128)(2,1)S(1)}, u32[]{:S(2)}, u32[]{:S(2)}) collective-permute-start(bf16[32,128]{1,0:T(8,128)(2,1)S(1)} %pad_maximum_fusion.1), channel_id=1, source_target_pairs={{0,2},{1,3},{2,0},{3,1},{4,6},{5,7},{6,4},{7,5},{8,10},{9,11},{10,... | collective-permute-start | bytes 24584 | tf_op jit(solution)/shard_map/ppermute | solution.py:380
  19.9 0.0 collective-permute-done.4.refs_5_
  20.0 3.4 %shard_map.71 = (bf16[192,1664]{1,0:T(8,128)(2,1)S(1)}, bf16[128,1664]{1,0:T(8,128)(2,1)S(1)}, bf16[4,512,512]{2,1,0:T(8,128)(2,1)S(1)}, f32[2,32,1664]{2,1,0:T(8,128)S(1)}) custom-call(s32[1]{0:T(128)} %bitcast.index_ref.refs_0_, bf16[64,1600]{1,0:T(8,128)(2,1)S(1)} %get-tuple-element.15.refs_1_, bf16[64,1600]{1,0:T(8,128)(2,1)S(1)} %collective-permute-done.2.refs_2_, ...), custom_call_target="tpu_custom_call" | custom-call | tf_op jit(solution)/shard_map/pallas_call | solution.py:394
  23.3 0.4 collective-permute-start.6
  23.7 2.1 %collective-permute-start.9 = (bf16[64,128]{1,0:T(8,128)(2,1)S(1)}, bf16[64,128]{1,0:T(8,128)(2,1)S(1)}, u32[]{:S(2)}, u32[]{:S(2)}) collective-permute-start(bf16[64,128]{1,0:T(8,128)(2,1)S(1)} %pad_maximum_fusion), channel_id=1, source_target_pairs={{0,4},{1,5},{2,6},{3,7},{4,0},{5,1},{6,2},{7,3},{8,12},{9,13},{10,... | collective-permute-start | bytes 49160 | tf_op jit(solution)/shard_map/ppermute | solution.py:380
  25.8 1.7 %collective-permute-done.9 = bf16[64,128]{1,0:T(8,128)(2,1)S(1)} collective-permute-done((bf16[64,128]{1,0:T(8,128)(2,1)S(1)}, bf16[64,128]{1,0:T(8,128)(2,1)S(1)}, u32[]{:S(2)}, u32[]{:S(2)}) %collective-permute-start.9) | collective-permute-done | bytes 16416 | tf_op jit(solution)/shard_map/ppermute | solution.py:380
  27.5 3.3 %collective-permute-start.10 = (bf16[128,128]{1,0:T(8,128)(2,1)S(1)}, bf16[128,128]{1,0:T(8,128)(2,1)S(1)}, u32[]{:S(2)}, u32[]{:S(2)}) collective-permute-start(bf16[128,128]{1,0:T(8,128)(2,1)S(1)} %constant_dynamic-update-slice_fusion.low_ref), channel_id=1, source_target_pairs={{0,8},{1,9},{2,10},{3,11},{4,12},{5,13},{6,14},{7,15},{8,0},{9,1},... | collective-permute-start | bytes 98312 | tf_op jit(solution)/shard_map/ppermute | solution.py:380
  30.9 0.1 shard_map.70.pseg_ref
  31.0 2.9 %shard_map.72 = (bf16[3,64,2048]{2,1,0:T(8,128)(2,1)S(1)}, bf16[2048,1664]{1,0:T(8,128)(2,1)S(1)}) custom-call(f32[336,128]{1,0:T(8,128)S(1)} %get-tuple-element.14.seg_ref.refs_8_, f32[8,128]{1,0:T(8,128)S(1)} %shard_map.70.pseg_ref, bf16[192,1664]{1,0:T(8,128)(2,1)S(1)} %get-tuple-element.17.spec, f32[2,32,1664]{2,1,0:T(8,128)S(1)} %get-tuple-element.18.lag_ref), custom_call_target="tpu_custom_call" | custom-call | tf_op jit(solution)/shard_map/pallas_call | solution.py:412
  33.9 0.0 collective-permute-done.10.high_ref
  33.9 3.6 %shard_map.73 = (bf16[5,64,2048]{2,1,0:T(8,128)(2,1)}, bf16[64,512]{1,0:T(8,128)(2,1)}) custom-call(s32[1]{0:T(128)} %bitcast.index_ref.refs_0_, f32[336,128]{1,0:T(8,128)S(1)} %get-tuple-element.14.seg_ref.refs_8_, f32[8,128]{1,0:T(8,128)S(1)} %shard_map.70.pseg_ref, bf16[2048,1664]{1,0:T(8,128)(2,1)S(1)} %get-tuple-element.19.turned, ...), custom_call_target="tpu_custom_call" | custom-call | tf_op jit(solution)/shard_map/pallas_call | solution.py:425
  (10 shorter events, 0.0 us)
Async XLA Ops:
  0.6 15.7 %collective-permute-start.1 = (bf16[64,1600]{1,0:T(8,128)(2,1)}, bf16[64,1600]{1,0:T(8,128)(2,1)S(1)}, u32[]{:S(2)}, u32[]{:S(2)}) collective-permute-start(bf16[64,1600]{1,0:T(8,128)(2,1)} %own_hbm.3), channel_id=1, source_target_pairs={{0,1},{1,0},{2,3},{3,2},{4,5},{5,4},{6,7},{7,6},{8,9},{9,8},{10,11... | collective-permute-start | bytes 614408 | tf_op jit(solution)/shard_map/ppermute | solution.py:336
  1.2 16.8 %collective-permute-start.3 = (bf16[64,1600]{1,0:T(8,128)(2,1)}, bf16[64,1600]{1,0:T(8,128)(2,1)S(1)}, u32[]{:S(2)}, u32[]{:S(2)}) collective-permute-start(bf16[64,1600]{1,0:T(8,128)(2,1)} %own_hbm.3), channel_id=1, source_target_pairs={{0,12},{1,13},{2,14},{3,15},{4,0},{5,1},{6,2},{7,3},{8,4},{9,5},{1... | collective-permute-start | bytes 614408 | tf_op jit(solution)/shard_map/ppermute | solution.py:333
  5.8 12.7 %collective-permute-start.2 = (bf16[64,1600]{1,0:T(8,128)(2,1)}, bf16[64,1600]{1,0:T(8,128)(2,1)S(1)}, u32[]{:S(2)}, u32[]{:S(2)}) collective-permute-start(bf16[64,1600]{1,0:T(8,128)(2,1)} %own_hbm.3), channel_id=1, source_target_pairs={{0,14},{1,15},{2,0},{3,1},{4,2},{5,3},{6,4},{7,5},{8,6},{9,7},{10,... | collective-permute-start | bytes 614408 | tf_op jit(solution)/shard_map/ppermute | solution.py:333
  8.0 8.3 %collective-permute-start = (bf16[16,1600]{1,0:T(8,128)(2,1)S(1)}, bf16[16,1600]{1,0:T(8,128)(2,1)S(1)}, u32[]{:S(2)}, u32[]{:S(2)}) collective-permute-start(bf16[16,1600]{1,0:T(8,128)(2,1)S(1)} %shard_map.68.edge_ref), channel_id=1, source_target_pairs={{0,11},{1,2},{2,13},{3,4},{4,15},{5,6},{6,1},{7,8},{8,3},{9,10},{1... | collective-permute-start | bytes 153608 | tf_op jit(solution)/shard_map/ppermute | solution.py:350
  17.9 1.2 %collective-permute-start.7 = (bf16[16,128]{1,0:T(8,128)(2,1)S(1)}, bf16[16,128]{1,0:T(8,128)(2,1)S(1)}, u32[]{:S(2)}, u32[]{:S(2)}) collective-permute-start(bf16[16,128]{1,0:T(8,128)(2,1)S(1)} %get-tuple-element.22), channel_id=1, source_target_pairs={{0,1},{1,0},{2,3},{3,2},{4,5},{5,4},{6,7},{7,6},{8,9},{9,8},{10,11... | collective-permute-start | bytes 12296 | tf_op jit(solution)/shard_map/ppermute | solution.py:380
  18.0 1.9 %collective-permute-start.5 = (bf16[64,1600]{1,0:T(8,128)(2,1)S(1)}, bf16[64,1600]{1,0:T(8,128)(2,1)S(1)}, u32[]{:S(2)}, u32[]{:S(2)}) collective-permute-start(bf16[64,1600]{1,0:T(8,128)(2,1)S(1)} %collective-permute-done.3.refs_3_), channel_id=1, source_target_pairs={{0,1},{1,0},{2,3},{3,2},{4,5},{5,4},{6,7},{7,6},{8,9},{9,8},{10,11... | collective-permute-start | bytes 614408 | tf_op jit(solution)/shard_map/ppermute | solution.py:336
  18.5 1.5 %collective-permute-start.4 = (bf16[64,1600]{1,0:T(8,128)(2,1)S(1)}, bf16[64,1600]{1,0:T(8,128)(2,1)S(1)}, u32[]{:S(2)}, u32[]{:S(2)}) collective-permute-start(bf16[64,1600]{1,0:T(8,128)(2,1)S(1)} %collective-permute-done.2.refs_2_), channel_id=1, source_target_pairs={{0,1},{1,0},{2,3},{3,2},{4,5},{5,4},{6,7},{7,6},{8,9},{9,8},{10,11... | collective-permute-start | bytes 614408 | tf_op jit(solution)/shard_map/ppermute | solution.py:336
  19.1 4.6 %collective-permute-start.8 = (bf16[32,128]{1,0:T(8,128)(2,1)S(1)}, bf16[32,128]{1,0:T(8,128)(2,1)S(1)}, u32[]{:S(2)}, u32[]{:S(2)}) collective-permute-start(bf16[32,128]{1,0:T(8,128)(2,1)S(1)} %pad_maximum_fusion.1), channel_id=1, source_target_pairs={{0,2},{1,3},{2,0},{3,1},{4,6},{5,7},{6,4},{7,5},{8,10},{9,11},{10,... | collective-permute-start | bytes 24584 | tf_op jit(solution)/shard_map/ppermute | solution.py:380
  23.3 10.5 %collective-permute-start.6 = (bf16[128,1664]{1,0:T(8,128)(2,1)S(1)}, bf16[128,1664]{1,0:T(8,128)(2,1)S(1)}, u32[]{:S(2)}, u32[]{:S(2)}) collective-permute-start(bf16[128,1664]{1,0:T(8,128)(2,1)S(1)} %get-tuple-element.20), channel_id=1, source_target_pairs={{0,1},{1,0},{2,3},{3,2},{4,5},{5,4},{6,7},{7,6},{8,9},{9,8},{10,11... | collective-permute-start | bytes 1277960 | tf_op jit(solution)/shard_map/ppermute | solution.py:336
  23.7 3.8 %collective-permute-start.9 = (bf16[64,128]{1,0:T(8,128)(2,1)S(1)}, bf16[64,128]{1,0:T(8,128)(2,1)S(1)}, u32[]{:S(2)}, u32[]{:S(2)}) collective-permute-start(bf16[64,128]{1,0:T(8,128)(2,1)S(1)} %pad_maximum_fusion), channel_id=1, source_target_pairs={{0,4},{1,5},{2,6},{3,7},{4,0},{5,1},{6,2},{7,3},{8,12},{9,13},{10,... | collective-permute-start | bytes 49160 | tf_op jit(solution)/shard_map/ppermute | solution.py:380
  27.5 6.3 %collective-permute-start.10 = (bf16[128,128]{1,0:T(8,128)(2,1)S(1)}, bf16[128,128]{1,0:T(8,128)(2,1)S(1)}, u32[]{:S(2)}, u32[]{:S(2)}) collective-permute-start(bf16[128,128]{1,0:T(8,128)(2,1)S(1)} %constant_dynamic-update-slice_fusion.low_ref), channel_id=1, source_target_pairs={{0,8},{1,9},{2,10},{3,11},{4,12},{5,13},{6,14},{7,15},{8,0},{9,1},... | collective-permute-start | bytes 98312 | tf_op jit(solution)/shard_map/ppermute | solution.py:380
